TPU v7x, 32 devices: a whole 2x2x4 slice. The times are simulated.
32 devices in a mesh: shard: 4 (over y, x), ctx: 2 (over core), tp: 4 (over z).
Axes of the slice: x: 2, y: 2, z: 4, core: 2. Of those that a mesh axis runs over, the one named last changes fastest.
Arguments:
- inputs: bfloat16 [8192, 768], P(('shard', 'ctx', 'tp')), may hold values from -6 to 6
- encoder: bfloat16 [8192, 768], P(('shard', 'ctx', 'tp')), may hold values from -6 to 6
- prefix: int32 [4], P('shard'), may hold values from 204 to 1024
- targets: int32 [8192], P(('shard', 'ctx')), may hold values from 0 to 32127
- cotangent: bfloat16 [8192, 768], P(('shard', 'ctx', 'tp')), may hold values from -6 to 6
- gain_self: bfloat16 [768], P('shard'), may hold values from 0.5 to 1.5
- query_self: bfloat16 [768, 768], P('shard', 'tp'), may hold values from -0.3125 to 0.3125
- key_self: bfloat16 [768, 768], P('shard', 'tp'), may hold values from -0.3125 to 0.3125
- value_self: bfloat16 [768, 768], P('shard', 'tp'), may hold values from -0.21875 to 0.21875
- output_self: bfloat16 [768, 768], P('tp', 'shard'), may hold values from -0.875 to 0.875
- gain_cross: bfloat16 [768], P('shard'), may hold values from 0.5 to 1.5
- query_cross: bfloat16 [768, 768], P('shard', 'tp'), may hold values from -0.3125 to 0.3125
- key_cross: bfloat16 [768, 768], P('shard', 'tp'), may hold values from -0.3125 to 0.3125
- value_cross: bfloat16 [768, 768], P('shard', 'tp'), may hold values from -0.21875 to 0.21875
- output_cross: bfloat16 [768, 768], P('tp', 'shard'), may hold values from -1.25 to 1.25
- gain_hidden: bfloat16 [768], P('shard'), may hold values from 0.5 to 1.5
- gate_weight: bfloat16 [768, 2048], P('shard', 'tp'), may hold values from -0.21875 to 0.21875
- up_weight: bfloat16 [768, 2048], P('shard', 'tp'), may hold values from -0.21875 to 0.21875
- down_weight: bfloat16 [2048, 768], P('tp', 'shard'), may hold values from -0.25 to 0.25
- gain_exit: bfloat16 [768], P('shard'), may hold values from 0.5 to 1.5
- embedding: bfloat16 [32128, 768], P('tp', 'shard'), may hold values from -9 to 9
Outputs:
- layer_output: bfloat16 [8192, 768], P(('shard', 'ctx', 'tp'))
- exit_loss: float32 [8192], P(('shard', 'ctx'))
- inputs_grad: float32 [8192, 768], P(('shard', 'ctx', 'tp'))
- encoder_grad: float32 [8192, 768], P(('shard', 'ctx', 'tp'))
- gain_self_grad: float32 [768], P('shard')
- query_self_grad: float32 [768, 768], P('shard', 'tp')
- key_self_grad: float32 [768, 768], P('shard', 'tp')
- value_self_grad: float32 [768, 768], P('shard', 'tp')
- output_self_grad: float32 [768, 768], P('tp', 'shard')
- gain_cross_grad: float32 [768], P('shard')
- query_cross_grad: float32 [768, 768], P('shard', 'tp')
- key_cross_grad: float32 [768, 768], P('shard', 'tp')
- value_cross_grad: float32 [768, 768], P('shard', 'tp')
- output_cross_grad: float32 [768, 768], P('tp', 'shard')
- gain_hidden_grad: float32 [768], P('shard')
- gate_weight_grad: float32 [768, 2048], P('shard', 'tp')
- up_weight_grad: float32 [768, 2048], P('shard', 'tp')
- down_weight_grad: float32 [2048, 768], P('tp', 'shard')
- gain_exit_grad: float32 [768], P('shard')
- embedding_grad: float32 [32128, 768], P('tp', 'shard')
All inputs are finite; a program needn't handle non-finite values.
Results may differ from a plain program's by a relative error of at most 0.028.
Values may be sent and summed in bfloat16 or wider, within the bound.
A program may use at most 256 MiB of HBM per device.

v0:
```python
from functools import partial

import jax
import jax.numpy as jnp
from jax import lax
from jax.sharding import PartitionSpec as P

D = 768
HEAD_DIM = 64


EPS = 1e-06
MASKED = -1e30


def combined_all(shard, axis, combine):
    everything = jax.tree.map(lambda part: lax.all_gather(part, axis), shard)
    first = jax.tree.map(lambda part: part[0], everything)

    def lap(k, so_far):
        return combine(so_far, jax.tree.map(lambda part: part[k], everything))

    return lax.fori_loop(1, lax.axis_size(axis), lap, first)


def normalize(hidden, gain):
    inverse = lax.rsqrt(jnp.mean(hidden * hidden, axis=-1, keepdims=True) + EPS)
    return (hidden * inverse * gain, inverse)


def norm_back(hidden, inverse, gain, upstream):
    scaled = upstream * gain
    inner = jnp.mean(scaled * hidden, axis=-1, keepdims=True)
    back = inverse * scaled - hidden * (inverse * inverse * inverse) * inner
    return (back, jnp.sum(upstream * hidden * inverse, axis=0))


def spread(rows):
    return lax.all_gather(rows, "tp", axis=0, tiled=True)


def settle(partial_sum):
    return lax.psum_scatter(partial_sum, "tp", scatter_dimension=0, tiled=True)


def split_heads(matrix):
    return matrix.reshape(matrix.shape[0], matrix.shape[1] // HEAD_DIM, HEAD_DIM)


def combine(first, second):
    top = jnp.maximum(first[0], second[0])
    total = first[1] * jnp.exp(first[0] - top) + second[1] * jnp.exp(second[0] - top)
    return (top, total, first[2] + second[2])


def attend(query, keys, values, visible):
    rows = query.shape[0]
    block = min(512, rows)
    scale = HEAD_DIM ** (-0.5)
    query_h = split_heads(query)
    keys_h = split_heads(keys)
    values_h = split_heads(values)
    outputs = []
    logsums = []
    for first in range(0, rows, block):
        scores = (
            jnp.einsum(
                "qhd,khd->hqk",
                query_h[first : first + block],
                keys_h,
                preferred_element_type=jnp.float32,
            )
            * scale
        )
        scores = jnp.where(visible(first, block)[None], scores, MASKED)
        top = jnp.max(scores, axis=-1, keepdims=True)
        expo = jnp.exp(scores - top)
        total = jnp.sum(expo, axis=-1, keepdims=True)
        probs = (expo / total).astype(jnp.bfloat16)
        outputs.append(
            jnp.einsum("hqk,khd->qhd", probs, values_h, preferred_element_type=jnp.float32).astype(
                jnp.bfloat16
            )
        )
        logsums.append(top + jnp.log(total))
    attended = jnp.concatenate(outputs, axis=0).reshape(rows, query.shape[1])
    return (attended, jnp.concatenate(logsums, axis=1))


def attend_back(query, keys, values, visible, logsum, grad_out):
    rows = query.shape[0]
    block = min(512, rows)
    scale = HEAD_DIM ** (-0.5)
    query_h = split_heads(query)
    keys_h = split_heads(keys)
    values_h = split_heads(values)
    grad_h = split_heads(grad_out)
    key_acc = jnp.zeros(keys_h.shape, jnp.float32)
    value_acc = jnp.zeros(values_h.shape, jnp.float32)
    query_grads = []
    for first in range(0, rows, block):
        part = query_h[first : first + block]
        grad_part = grad_h[first : first + block]
        scores = (
            jnp.einsum("qhd,khd->hqk", part, keys_h, preferred_element_type=jnp.float32) * scale
        )
        scores = jnp.where(visible(first, block)[None], scores, MASKED)
        probs = jnp.exp(scores - logsum[:, first : first + block])
        grad_probs = jnp.einsum(
            "qhd,khd->hqk", grad_part, values_h, preferred_element_type=jnp.float32
        )
        inner = jnp.sum(grad_probs * probs, axis=-1, keepdims=True)
        grad_scores = (probs * (grad_probs - inner)).astype(jnp.bfloat16)
        query_grads.append(
            (
                jnp.einsum("hqk,khd->qhd", grad_scores, keys_h, preferred_element_type=jnp.float32)
                * scale
            ).astype(jnp.bfloat16)
        )
        key_acc = (
            key_acc
            + jnp.einsum("hqk,qhd->khd", grad_scores, part, preferred_element_type=jnp.float32)
            * scale
        )
        value_acc = value_acc + jnp.einsum(
            "hqk,qhd->khd",
            probs.astype(jnp.bfloat16),
            grad_part,
            preferred_element_type=jnp.float32,
        )
    grad_query = jnp.concatenate(query_grads, axis=0).reshape(rows, query.shape[1])
    return (
        grad_query,
        key_acc.reshape(keys.shape[0], keys.shape[1]),
        value_acc.reshape(values.shape[0], values.shape[1]),
    )


def matmul(left, right):
    return jnp.dot(left, right, preferred_element_type=jnp.float32)


def left_t(left, right):
    return jnp.einsum("ra,rb->ab", left, right, preferred_element_type=jnp.float32)


def right_t(left, right):
    return jnp.einsum("ra,ba->rb", left, right, preferred_element_type=jnp.float32)


def per_device(
    inputs,
    encoder,
    prefix,
    targets,
    cotangent,
    gain_self,
    query_self,
    key_self,
    value_self,
    output_self,
    gain_cross,
    query_cross,
    key_cross,
    value_cross,
    output_cross,
    gain_hidden,
    gate_weight,
    up_weight,
    down_weight,
    gain_exit,
    embedding,
):
    full = (
        lax.all_gather(gain_self, "shard", axis=0, tiled=True),
        lax.all_gather(query_self, "shard", axis=0, tiled=True),
        lax.all_gather(key_self, "shard", axis=0, tiled=True),
        lax.all_gather(value_self, "shard", axis=0, tiled=True),
        lax.all_gather(output_self, "shard", axis=1, tiled=True),
        lax.all_gather(gain_cross, "shard", axis=0, tiled=True),
        lax.all_gather(query_cross, "shard", axis=0, tiled=True),
        lax.all_gather(key_cross, "shard", axis=0, tiled=True),
        lax.all_gather(value_cross, "shard", axis=0, tiled=True),
        lax.all_gather(output_cross, "shard", axis=1, tiled=True),
        lax.all_gather(gain_hidden, "shard", axis=0, tiled=True),
        lax.all_gather(gate_weight, "shard", axis=0, tiled=True),
        lax.all_gather(up_weight, "shard", axis=0, tiled=True),
        lax.all_gather(down_weight, "shard", axis=1, tiled=True),
        lax.all_gather(gain_exit, "shard", axis=0, tiled=True),
        lax.all_gather(embedding, "shard", axis=1, tiled=True),
    )
    (
        gain_self,
        query_self,
        key_self,
        value_self,
        output_self,
        gain_cross,
        query_cross,
        key_cross,
        value_cross,
        output_cross,
        gain_hidden,
        gate_weight,
        up_weight,
        down_weight,
        gain_exit,
        embedding,
    ) = full
    gain_one = gain_self.astype(jnp.float32)
    gain_two = gain_cross.astype(jnp.float32)
    gain_three = gain_hidden.astype(jnp.float32)
    gain_four = gain_exit.astype(jnp.float32)
    group_rows = inputs.shape[0] * lax.axis_size("tp")
    offset = lax.axis_index("ctx") * group_rows
    limit = prefix[0]
    inputs_f = inputs.astype(jnp.float32)
    normed1, inverse1 = normalize(inputs_f, gain_one)
    group1 = spread(normed1.astype(jnp.bfloat16))
    query1 = matmul(group1, query_self).astype(jnp.bfloat16)
    key_local = matmul(group1, key_self).astype(jnp.bfloat16)
    value_local = matmul(group1, value_self).astype(jnp.bfloat16)
    encoder_rows = spread(encoder)
    key_enc_local = matmul(encoder_rows, key_cross).astype(jnp.bfloat16)
    value_enc_local = matmul(encoder_rows, value_cross).astype(jnp.bfloat16)
    keys_all, values_all, keys_enc, values_enc = (
        lax.all_gather(key_local, "ctx", axis=0, tiled=True),
        lax.all_gather(value_local, "ctx", axis=0, tiled=True),
        lax.all_gather(key_enc_local, "ctx", axis=0, tiled=True),
        lax.all_gather(value_enc_local, "ctx", axis=0, tiled=True),
    )
    positions = jnp.arange(keys_all.shape[0], dtype=jnp.int32)

    def causal(first, count):
        rows = offset + first + jnp.arange(count, dtype=jnp.int32)
        return (positions[None, :] <= rows[:, None]) | (positions[None, :] < limit)

    def open_all(first, count):
        return jnp.ones((count, keys_enc.shape[0]), dtype=jnp.bool_)

    attended1, logsum_self = attend(query1, keys_all, values_all, causal)
    hidden1 = inputs_f + settle(matmul(attended1, output_self))
    normed2, inverse2 = normalize(hidden1, gain_two)
    group2 = spread(normed2.astype(jnp.bfloat16))
    query2 = matmul(group2, query_cross).astype(jnp.bfloat16)
    attended2, logsum_cross = attend(query2, keys_enc, values_enc, open_all)
    hidden2 = hidden1 + settle(matmul(attended2, output_cross))
    normed3, inverse3 = normalize(hidden2, gain_three)
    group3 = spread(normed3.astype(jnp.bfloat16))
    gate = matmul(group3, gate_weight)
    upper = matmul(group3, up_weight)
    active = jax.nn.gelu(gate, approximate=True)
    product_b = (active * upper).astype(jnp.bfloat16)
    final = hidden2 + settle(matmul(product_b, down_weight))
    normed4, inverse4 = normalize(final, gain_four)
    group4 = spread(normed4.astype(jnp.bfloat16))
    vocab = embedding.shape[0]
    vocab_ids = lax.axis_index("tp") * vocab + jnp.arange(vocab, dtype=jnp.int32)
    scale_out = D ** (-0.5)
    block = min(512, group4.shape[0])
    tops = []
    totals = []
    picks = []
    for first in range(0, group4.shape[0], block):
        logits = (
            jnp.einsum(
                "rd,vd->rv",
                group4[first : first + block],
                embedding,
                preferred_element_type=jnp.float32,
            )
            * scale_out
        )
        top = jnp.max(logits, axis=-1)
        tops.append(top)
        totals.append(jnp.sum(jnp.exp(logits - top[:, None]), axis=-1))
        hits = vocab_ids[None, :] == targets[first : first + block, None]
        picks.append(jnp.sum(jnp.where(hits, logits, 0.0), axis=-1))
    top_all, total_all, picked = combined_all(
        (jnp.concatenate(tops), jnp.concatenate(totals), jnp.concatenate(picks)), "tp", combine
    )
    logsum_exit = top_all + jnp.log(total_all)
    exit_loss = logsum_exit - picked
    exit_terms = []
    embedding_grad = jnp.zeros(embedding.shape, jnp.float32)
    for first in range(0, group4.shape[0], block):
        part = group4[first : first + block]
        logits = (
            jnp.einsum("rd,vd->rv", part, embedding, preferred_element_type=jnp.float32) * scale_out
        )
        hits = vocab_ids[None, :] == targets[first : first + block, None]
        grad_logits = (
            jnp.exp(logits - logsum_exit[first : first + block, None]) - hits.astype(jnp.float32)
        ).astype(jnp.bfloat16)
        exit_terms.append(matmul(grad_logits, embedding) * scale_out)
        embedding_grad = embedding_grad + left_t(grad_logits, part) * scale_out
    grad_normed4 = settle(jnp.concatenate(exit_terms, axis=0))
    back4, gain_exit_grad = norm_back(final, inverse4, gain_four, grad_normed4)
    grad_final = cotangent.astype(jnp.float32) + back4
    grad_final_b = spread(grad_final.astype(jnp.bfloat16))
    down_grad = left_t(product_b, grad_final_b)
    grad_product = right_t(grad_final_b, down_weight)
    unused, gelu_pull = jax.vjp(partial(jax.nn.gelu, approximate=True), gate)
    grad_gate = gelu_pull(grad_product * upper)[0].astype(jnp.bfloat16)
    grad_upper = (grad_product * active).astype(jnp.bfloat16)
    gate_grad = left_t(group3, grad_gate)
    upper_grad = left_t(group3, grad_upper)
    grad_normed3 = settle(right_t(grad_gate, gate_weight) + right_t(grad_upper, up_weight))
    back3, gain_hidden_grad = norm_back(hidden2, inverse3, gain_three, grad_normed3)
    grad_hidden2 = grad_final + back3
    grad_hidden2_b = spread(grad_hidden2.astype(jnp.bfloat16))
    out_cross_grad = left_t(attended2, grad_hidden2_b)
    grad_attended2 = right_t(grad_hidden2_b, output_cross).astype(jnp.bfloat16)
    grad_query2, key_enc_acc, value_enc_acc = attend_back(
        query2, keys_enc, values_enc, open_all, logsum_cross, grad_attended2
    )
    query_cross_grad = left_t(group2, grad_query2)
    grad_normed2 = settle(right_t(grad_query2, query_cross))
    back2, gain_cross_grad = norm_back(hidden1, inverse2, gain_two, grad_normed2)
    grad_hidden1 = grad_hidden2 + back2
    grad_hidden1_b = spread(grad_hidden1.astype(jnp.bfloat16))
    out_self_grad = left_t(attended1, grad_hidden1_b)
    grad_attended1 = right_t(grad_hidden1_b, output_self).astype(jnp.bfloat16)
    grad_query1, key_acc, value_acc = attend_back(
        query1, keys_all, values_all, causal, logsum_self, grad_attended1
    )
    key_sum, value_sum, key_enc_sum, value_enc_sum = (
        lax.psum_scatter(key_acc, "ctx", scatter_dimension=0, tiled=True),
        lax.psum_scatter(value_acc, "ctx", scatter_dimension=0, tiled=True),
        lax.psum_scatter(key_enc_acc, "ctx", scatter_dimension=0, tiled=True),
        lax.psum_scatter(value_enc_acc, "ctx", scatter_dimension=0, tiled=True),
    )
    grad_key1 = key_sum.astype(jnp.bfloat16)
    grad_value1 = value_sum.astype(jnp.bfloat16)
    grad_key2 = key_enc_sum.astype(jnp.bfloat16)
    grad_value2 = value_enc_sum.astype(jnp.bfloat16)
    query_self_grad = left_t(group1, grad_query1)
    key_self_grad = left_t(group1, grad_key1)
    value_self_grad = left_t(group1, grad_value1)
    grad_normed1 = settle(
        right_t(grad_query1, query_self)
        + right_t(grad_key1, key_self)
        + right_t(grad_value1, value_self)
    )
    back1, gain_self_grad = norm_back(inputs_f, inverse1, gain_one, grad_normed1)
    inputs_grad = grad_hidden1 + back1
    key_cross_grad = left_t(encoder_rows, grad_key2)
    value_cross_grad = left_t(encoder_rows, grad_value2)
    encoder_grad = settle(right_t(grad_key2, key_cross) + right_t(grad_value2, value_cross))
    gain_self_grad, gain_cross_grad, gain_hidden_grad, gain_exit_grad = lax.psum(
        (gain_self_grad, gain_cross_grad, gain_hidden_grad, gain_exit_grad), "tp"
    )
    reduced = (
        lax.psum_scatter(gain_self_grad, "shard", scatter_dimension=0, tiled=True),
        lax.psum_scatter(query_self_grad, "shard", scatter_dimension=0, tiled=True),
        lax.psum_scatter(key_self_grad, "shard", scatter_dimension=0, tiled=True),
        lax.psum_scatter(value_self_grad, "shard", scatter_dimension=0, tiled=True),
        lax.psum_scatter(out_self_grad, "shard", scatter_dimension=1, tiled=True),
        lax.psum_scatter(gain_cross_grad, "shard", scatter_dimension=0, tiled=True),
        lax.psum_scatter(query_cross_grad, "shard", scatter_dimension=0, tiled=True),
        lax.psum_scatter(key_cross_grad, "shard", scatter_dimension=0, tiled=True),
        lax.psum_scatter(value_cross_grad, "shard", scatter_dimension=0, tiled=True),
        lax.psum_scatter(out_cross_grad, "shard", scatter_dimension=1, tiled=True),
        lax.psum_scatter(gain_hidden_grad, "shard", scatter_dimension=0, tiled=True),
        lax.psum_scatter(gate_grad, "shard", scatter_dimension=0, tiled=True),
        lax.psum_scatter(upper_grad, "shard", scatter_dimension=0, tiled=True),
        lax.psum_scatter(down_grad, "shard", scatter_dimension=1, tiled=True),
        lax.psum_scatter(gain_exit_grad, "shard", scatter_dimension=0, tiled=True),
        lax.psum_scatter(embedding_grad, "shard", scatter_dimension=1, tiled=True),
    )
    shards = lax.psum(
        (
            reduced[0],
            reduced[1],
            reduced[2],
            reduced[3],
            reduced[4],
            reduced[5],
            reduced[6],
            reduced[7],
            reduced[8],
            reduced[9],
            reduced[10],
            reduced[11],
            reduced[12],
            reduced[13],
            reduced[14],
            reduced[15],
        ),
        "ctx",
    )
    return (
        final.astype(jnp.bfloat16),
        exit_loss,
        inputs_grad,
        encoder_grad,
        shards[0],
        shards[1],
        shards[2],
        shards[3],
        shards[4],
        shards[5],
        shards[6],
        shards[7],
        shards[8],
        shards[9],
        shards[10],
        shards[11],
        shards[12],
        shards[13],
        shards[14],
        shards[15],
    )


def solution(mesh):
    return jax.shard_map(
        per_device,
        mesh=mesh,
        in_specs=(
            P(("shard", "ctx", "tp"), None),
            P(("shard", "ctx", "tp"), None),
            P("shard"),
            P(("shard", "ctx")),
            P(("shard", "ctx", "tp"), None),
            P("shard"),
            P("shard", "tp"),
            P("shard", "tp"),
            P("shard", "tp"),
            P("tp", "shard"),
            P("shard"),
            P("shard", "tp"),
            P("shard", "tp"),
            P("shard", "tp"),
            P("tp", "shard"),
            P("shard"),
            P("shard", "tp"),
            P("shard", "tp"),
            P("tp", "shard"),
            P("shard"),
            P("tp", "shard"),
        ),
        out_specs=(
            P(("shard", "ctx", "tp"), None),
            P(("shard", "ctx")),
            P(("shard", "ctx", "tp"), None),
            P(("shard", "ctx", "tp"), None),
            P("shard"),
            P("shard", "tp"),
            P("shard", "tp"),
            P("shard", "tp"),
            P("tp", "shard"),
            P("shard"),
            P("shard", "tp"),
            P("shard", "tp"),
            P("shard", "tp"),
            P("tp", "shard"),
            P("shard"),
            P("shard", "tp"),
            P("shard", "tp"),
            P("tp", "shard"),
            P("shard"),
            P("tp", "shard"),
        ),
        check_vma=False,
    )
```

profile of v0, /device:TPU:0, one launch (start us, length us, event | category | flops | bytes accessed | tf_op | source)
XLA Modules:
  0.0 1849.3 jit_solution(1806466330006752084)
XLA Ops:
  104.2 59.9 %reduce-scatter.33.cloned.1.call-done = f32[256,768]{1,0:T(8,128)} async-done(((f32[1024,768]{1,0:T(8,128)}), f32[256,768]{1,0:T(8,128)}) %reduce-scatter.33.cloned.1.call-update) | async-done | bytes 786448 | tf_op jit(solution)/shard_map/reduce_scatter | solution.py:43
  214.5 26.4 %all-gather.17.cloned.1.call-done = bf16[1024,768]{1,0:T(8,128)(2,1)} async-done(((bf16[256,768]{1,0:T(8,128)(2,1)}), bf16[1024,768]{1,0:T(8,128)(2,1)}) %all-gather.17.cloned.1.call-update) | async-done | bytes 1572880 | tf_op jit(solution)/shard_map/all_gather | solution.py:39
  261.8 59.2 %reduce-scatter.35.cloned.1.call-done = f32[256,768]{1,0:T(8,128)} async-done(((f32[1024,768]{1,0:T(8,128)}), f32[256,768]{1,0:T(8,128)}) %reduce-scatter.35.cloned.1.call-update) | async-done | bytes 786448 | tf_op jit(solution)/shard_map/reduce_scatter | solution.py:43
  371.5 58.6 %reduce-scatter.37.cloned.1.call-done = f32[256,768]{1,0:T(8,128)} async-done(((f32[1024,768]{1,0:T(8,128)}), f32[256,768]{1,0:T(8,128)}) %reduce-scatter.37.cloned.1.call-update) | async-done | bytes 786448 | tf_op jit(solution)/shard_map/reduce_scatter | solution.py:43
  433.6 59.2 %all-gather.23.cloned.1.call-done = bf16[8032,768]{0,1:T(8,128)(2,1)} async-done(((bf16[8032,192]{0,1:T(8,128)(2,1)}), bf16[8032,768]{0,1:T(8,128)(2,1)}) %all-gather.23.cloned.1.call-update) | async-done | bytes 12337168 | tf_op jit(solution)/shard_map/all_gather | solution.py:190
  492.7 39.0 %all-gather.21.cloned.1.call-done = bf16[1024,768]{1,0:T(8,128)(2,1)} async-done(((bf16[256,768]{1,0:T(8,128)(2,1)}), bf16[1024,768]{1,0:T(8,128)(2,1)}) %all-gather.21.cloned.1.call-update) | async-done | bytes 1572880 | tf_op jit(solution)/shard_map/all_gather | solution.py:39
  531.7 18.9 %multiply_reduce_fusion = (f32[512]{0:T(512)}, f32[512,8032]{0,1:T(8,128)}) fusion(bf16[8032,768]{0,1:T(8,128)(2,1)} %all-gather.23.cloned.1.call-done, bf16[1024,768]{1,0:T(8,128)(2,1)} %all-gather.21.cloned.1.call-done), kind=kOutput, calls=%fused_computation.17 | convolution fusion | flops 6324846080 | bytes 29624320 | tf_op jit(solution)/shard_map/rd,vd->rv/dot_general | solution.py:266
  550.6 18.8 %multiply_reduce_fusion.1 = (f32[512]{0:T(512)}, f32[512,8032]{0,1:T(8,128)}) fusion(bf16[8032,768]{0,1:T(8,128)(2,1)} %all-gather.23.cloned.1.call-done, bf16[1024,768]{1,0:T(8,128)(2,1)} %all-gather.21.cloned.1.call-done), kind=kOutput, calls=%fused_computation.18 | convolution fusion | flops 6324846080 | bytes 29624320 | tf_op jit(solution)/shard_map/rd,vd->rv/dot_general | solution.py:266
  570.1 15.3 fusion
  585.4 13.1 all-gather.1
  636.5 14.2 convolution_multiply_fusion.1
  650.7 14.2 convolution_multiply_fusion
  666.9 59.2 %reduce-scatter.39.cloned.1.call-done = f32[256,768]{1,0:T(8,128)} async-done(((f32[1024,768]{1,0:T(8,128)}), f32[256,768]{1,0:T(8,128)}) %reduce-scatter.39.cloned.1.call-update) | async-done | bytes 786448 | tf_op jit(solution)/shard_map/reduce_scatter | solution.py:43
  730.7 36.9 %all-gather.25.cloned.1.call-done = bf16[1024,768]{1,0:T(8,128)(2,1)} async-done(((bf16[256,768]{1,0:T(8,128)(2,1)}), bf16[1024,768]{1,0:T(8,128)(2,1)}) %all-gather.25.cloned.1.call-update) | async-done | bytes 1572880 | tf_op jit(solution)/shard_map/all_gather | solution.py:39
  777.5 58.8 %reduce-scatter.41.cloned.1.call-done = f32[256,768]{1,0:T(8,128)} async-done(((f32[1024,768]{1,0:T(8,128)}), f32[256,768]{1,0:T(8,128)}) %reduce-scatter.41.cloned.1.call-update) | async-done | bytes 786448 | tf_op jit(solution)/shard_map/reduce_scatter | solution.py:43
  842.1 35.6 %all-gather.27.cloned.1.call-done = bf16[1024,768]{1,0:T(8,128)(2,1)} async-done(((bf16[256,768]{1,0:T(8,128)(2,1)}), bf16[1024,768]{1,0:T(8,128)(2,1)}) %all-gather.27.cloned.1.call-update) | async-done | bytes 1572880 | tf_op jit(solution)/shard_map/all_gather | solution.py:39
  924.0 59.2 %reduce-scatter.43.cloned.1.call-done = f32[256,768]{1,0:T(8,128)} async-done(((f32[1024,768]{1,0:T(8,128)}), f32[256,768]{1,0:T(8,128)}) %reduce-scatter.43.cloned.1.call-update) | async-done | bytes 786448 | tf_op jit(solution)/shard_map/reduce_scatter | solution.py:43
  1120.7 18.8 %fusion.77 = f32[8032,768]{0,1:T(8,128)} fusion(bf16[1024,768]{1,0:T(8,128)(2,1)} %all-gather.21.cloned.1.call-done, f32[512,8032]{0,1:T(8,128)} %get-tuple-element.355, f32[512]{0:T(512)S(1)} %copy-done.114, s32[512]{0:T(512)S(1)} %copy-done.108, s32[8032]{0:T(1024)S(1)} %copy-done.62), kind=kOutput, calls=%fused_computation.158 | convolution fusion | flops 6341296128 | bytes 41946496 | tf_op jit(solution)/shard_map/ra,rb->ab/dot_general | solution.py:144
  1142.3 26.3 %add_multiply_fusion = f32[8032,768]{0,1:T(8,128)} fusion(f32[8032,768]{0,1:T(8,128)} %fusion.77, bf16[1024,768]{1,0:T(8,128)(2,1)} %all-gather.21.cloned.1.call-done, f32[512,8032]{0,1:T(8,128)} %get-tuple-element.353, f32[512]{0:T(512)S(1)} %copy-done.96, s32[512]{0:T(512)S(1)} %copy-done.84, s32[8032]{0:T(1024)S(1)} %copy-done.62), kind=kOutput, calls=%fused_computation.4 | convolution fusion | flops 6353633280 | bytes 66719104 | tf_op jit(solution)/shard_map/ra,rb->ab/dot_general | solution.py:144
  1178.5 26.0 %reduce-scatter.73.cloned.1.call-done = f32[192,192]{1,0:T(8,128)} async-done(((f32[768,192]{1,0:T(8,128)}), f32[192,192]{1,0:T(8,128)}) %reduce-scatter.73.cloned.1.call-update) | async-done | bytes 147472
  1206.3 32.1 %reduce-scatter.69.cloned.1.call-done = f32[512,192]{0,1:T(8,128)} async-done(((f32[512,768]{0,1:T(8,128)}), f32[512,192]{0,1:T(8,128)}) %reduce-scatter.69.cloned.1.call-update) | async-done | bytes 393232 | tf_op jit(solution)/shard_map/reduce_scatter | solution.py:367
  1238.3 34.0 %reduce-scatter.65.cloned.1.call-done = f32[192,512]{1,0:T(8,128)} async-done(((f32[768,512]{1,0:T(8,128)}), f32[192,512]{1,0:T(8,128)}) %reduce-scatter.65.cloned.1.call-update) | async-done | bytes 393232 | tf_op jit(solution)/shard_map/reduce_scatter | solution.py:365
  1272.3 33.8 %reduce-scatter.67.cloned.1.call-done = f32[192,512]{1,0:T(8,128)} async-done(((f32[768,512]{1,0:T(8,128)}), f32[192,512]{1,0:T(8,128)}) %reduce-scatter.67.cloned.1.call-update) | async-done | bytes 393232 | tf_op jit(solution)/shard_map/reduce_scatter | solution.py:366
  1306.1 29.1 %reduce-scatter.63.cloned.1.call-done = f32[192,192]{1,0:T(8,128)} async-done(((f32[768,192]{1,0:T(8,128)}), f32[192,192]{1,0:T(8,128)}) %reduce-scatter.63.cloned.1.call-update) | async-done | bytes 147472 | tf_op jit(solution)/shard_map/reduce_scatter | solution.py:360
  1335.2 29.6 %reduce-scatter.57.cloned.1.call-done = f32[192,192]{1,0:T(8,128)} async-done(((f32[768,192]{1,0:T(8,128)}), f32[192,192]{1,0:T(8,128)}) %reduce-scatter.57.cloned.1.call-update) | async-done | bytes 147472 | tf_op jit(solution)/shard_map/reduce_scatter | solution.py:355
  1364.8 29.0 %reduce-scatter.61.cloned.1.call-done = f32[192,192]{1,0:T(8,128)} async-done(((f32[768,192]{1,0:T(8,128)}), f32[192,192]{1,0:T(8,128)}) %reduce-scatter.61.cloned.1.call-update) | async-done | bytes 147472 | tf_op jit(solution)/shard_map/reduce_scatter | solution.py:357
  1393.8 28.9 %reduce-scatter.59.cloned.1.call-done = f32[192,192]{1,0:T(8,128)} async-done(((f32[768,192]{1,0:T(8,128)}), f32[192,192]{1,0:T(8,128)}) %reduce-scatter.59.cloned.1.call-update) | async-done | bytes 147472 | tf_op jit(solution)/shard_map/reduce_scatter | solution.py:356
  1422.7 221.9 %reduce-scatter.71.cloned.1.call-done = f32[8032,192]{0,1:T(8,128)} async-done(((f32[8032,768]{0,1:T(8,128)}), f32[8032,192]{0,1:T(8,128)}) %reduce-scatter.71.cloned.1.call-update) | async-done | bytes 6168592 | tf_op jit(solution)/shard_map/reduce_scatter | solution.py:369
  1648.8 58.8 %reduce-scatter.49.cloned.1.call-done = f32[256,768]{1,0:T(8,128)} async-done(((f32[1024,768]{1,0:T(8,128)}), f32[256,768]{1,0:T(8,128)}) %reduce-scatter.49.cloned.1.call-update) | async-done | bytes 786448 | tf_op jit(solution)/shard_map/reduce_scatter | solution.py:43
  1709.1 16.0 all-reduce.9
  1741.3 15.1 all-reduce.15.cloned.1.call-done
  1759.8 61.0 %reduce-scatter.55.cloned.1.call-done = f32[256,768]{1,0:T(8,128)} async-done(((f32[1024,768]{1,0:T(8,128)}), f32[256,768]{1,0:T(8,128)}) %reduce-scatter.55.cloned.1.call-update) | async-done | bytes 786448 | tf_op jit(solution)/shard_map/reduce_scatter | solution.py:43
  (531 shorter events, 527.5 us)
Async XLA Ops:
  29.2 134.9 %reduce-scatter.33.cloned.1.call-start = ((), (), s32[]{:S(2)}) async-start(), calls=%async_computation.25 | async-start | bytes 3932160 | tf_op jit(solution)/shard_map/reduce_scatter | solution.py:43
  103.4 101.9 %all-gather.15.cloned.1.call-start = ((), (), s32[]{:S(2)}) async-start(), calls=%async_computation.26 | async-start | bytes 1966080 | tf_op jit(solution)/shard_map/all_gather | solution.py:39
  104.2 136.7 %all-gather.17.cloned.1.call-start = ((), (), s32[]{:S(2)}) async-start(), calls=%async_computation.27 | async-start | bytes 1966080 | tf_op jit(solution)/shard_map/all_gather | solution.py:39
  166.9 154.1 %reduce-scatter.35.cloned.1.call-start = ((), (), s32[]{:S(2)}) async-start(), calls=%async_computation.28 | async-start | bytes 3932160 | tf_op jit(solution)/shard_map/reduce_scatter | solution.py:43
  261.7 99.9 %all-gather.19.cloned.1.call-start = ((), (), s32[]{:S(2)}) async-start(), calls=%async_computation.29 | async-start | bytes 1966080 | tf_op jit(solution)/shard_map/all_gather | solution.py:39
  324.4 105.7 %reduce-scatter.37.cloned.1.call-start = ((), (), s32[]{:S(2)}) async-start(), calls=%async_computation.30 | async-start | bytes 3932160 | tf_op jit(solution)/shard_map/reduce_scatter | solution.py:43
  370.8 121.9 %all-gather.23.cloned.1.call-start = ((), (), s32[]{:S(2)}) async-start(), calls=%async_computation.32 | async-start | bytes 15482880 | tf_op jit(solution)/shard_map/all_gather | solution.py:190
  371.4 160.3 %all-gather.21.cloned.1.call-start = ((), (), s32[]{:S(2)}) async-start(), calls=%async_computation.31 | async-start | bytes 1966080 | tf_op jit(solution)/shard_map/all_gather | solution.py:39
  432.9 293.2 %reduce-scatter.39.cloned.1.call-start = ((), (), s32[]{:S(2)}) async-start(), calls=%async_computation.33 | async-start | bytes 3932160 | tf_op jit(solution)/shard_map/reduce_scatter | solution.py:43
  666.8 100.8 %all-gather.25.cloned.1.call-start = ((), (), s32[]{:S(2)}) async-start(), calls=%async_computation.34 | async-start | bytes 1966080 | tf_op jit(solution)/shard_map/all_gather | solution.py:39
  730.6 105.6 %reduce-scatter.41.cloned.1.call-start = ((), (), s32[]{:S(2)}) async-start(), calls=%async_computation.35 | async-start | bytes 3932160 | tf_op jit(solution)/shard_map/reduce_scatter | solution.py:43
  777.0 100.7 %all-gather.27.cloned.1.call-start = ((), (), s32[]{:S(2)}) async-start(), calls=%async_computation.36 | async-start | bytes 1966080 | tf_op jit(solution)/shard_map/all_gather | solution.py:39
  840.6 142.6 %reduce-scatter.43.cloned.1.call-start = ((), (), s32[]{:S(2)}) async-start(), calls=%async_computation.37 | async-start | bytes 3932160 | tf_op jit(solution)/shard_map/reduce_scatter | solution.py:43
  924.0 100.2 %all-gather.29.cloned.1.call-start = ((), (), s32[]{:S(2)}) async-start(), calls=%async_computation.38 | async-start | bytes 1966080 | tf_op jit(solution)/shard_map/all_gather | solution.py:39
  987.0 95.4 %reduce-scatter.53.cloned.1.call-start = ((), (), s32[]{:S(2)}) async-start(), calls=%async_computation.43 | async-start | bytes 2359296 | tf_op jit(solution)/shard_map/reduce_scatter | solution.py:331
  1012.0 106.0 %reduce-scatter.47.cloned.1.call-start = ((), (), s32[]{:S(2)}) async-start(), calls=%async_computation.40 | async-start | bytes 2359296 | tf_op jit(solution)/shard_map/reduce_scatter | solution.py:329
  1047.8 91.7 %reduce-scatter.45.cloned.1.call-start = ((), (), s32[]{:S(2)}) async-start(), calls=%async_computation.39 | async-start | bytes 2359296 | tf_op jit(solution)/shard_map/reduce_scatter | solution.py:328
  1079.6 93.6 %reduce-scatter.79.cloned.1.call-start = ((), (), s32[]{:S(2)}) async-start(), calls=%async_computation.56 | async-start | bytes 983040
  1082.4 92.7 %reduce-scatter.77.cloned.1.call-start = ((), (), s32[]{:S(2)}) async-start(), calls=%async_computation.55 | async-start | bytes 983040
  1087.3 89.5 %reduce-scatter.75.cloned.1.call-start = ((), (), s32[]{:S(2)}) async-start(), calls=%async_computation.54 | async-start | bytes 983040
  1092.2 112.4 %reduce-scatter.73.cloned.1.call-start = ((), (), s32[]{:S(2)}) async-start(), calls=%async_computation.53 | async-start | bytes 983040
  1093.9 144.5 %reduce-scatter.69.cloned.1.call-start = ((), (), s32[]{:S(2)}) async-start(), calls=%async_computation.51 | async-start | bytes 1966080 | tf_op jit(solution)/shard_map/reduce_scatter | solution.py:367
  1098.0 174.3 %reduce-scatter.65.cloned.1.call-start = ((), (), s32[]{:S(2)}) async-start(), calls=%async_computation.49 | async-start | bytes 1966080 | tf_op jit(solution)/shard_map/reduce_scatter | solution.py:365
  1100.3 205.8 %reduce-scatter.67.cloned.1.call-start = ((), (), s32[]{:S(2)}) async-start(), calls=%async_computation.50 | async-start | bytes 1966080 | tf_op jit(solution)/shard_map/reduce_scatter | solution.py:366
  1104.4 230.8 %reduce-scatter.63.cloned.1.call-start = ((), (), s32[]{:S(2)}) async-start(), calls=%async_computation.48 | async-start | bytes 983040 | tf_op jit(solution)/shard_map/reduce_scatter | solution.py:360
  1106.0 258.8 %reduce-scatter.57.cloned.1.call-start = ((), (), s32[]{:S(2)}) async-start(), calls=%async_computation.45 | async-start | bytes 983040 | tf_op jit(solution)/shard_map/reduce_scatter | solution.py:355
  1117.9 275.9 %reduce-scatter.61.cloned.1.call-start = ((), (), s32[]{:S(2)}) async-start(), calls=%async_computation.47 | async-start | bytes 983040 | tf_op jit(solution)/shard_map/reduce_scatter | solution.py:357
  1120.7 302.0 %reduce-scatter.59.cloned.1.call-start = ((), (), s32[]{:S(2)}) async-start(), calls=%async_computation.46 | async-start | bytes 983040 | tf_op jit(solution)/shard_map/reduce_scatter | solution.py:356
  1142.2 502.3 %reduce-scatter.71.cloned.1.call-start = ((), (), s32[]{:S(2)}) async-start(), calls=%async_computation.52 | async-start | bytes 30965760 | tf_op jit(solution)/shard_map/reduce_scatter | solution.py:369
  1168.6 539.1 %reduce-scatter.49.cloned.1.call-start = ((), (), s32[]{:S(2)}) async-start(), calls=%async_computation.41 | async-start | bytes 3932160 | tf_op jit(solution)/shard_map/reduce_scatter | solution.py:43
  1173.2 583.2 %all-reduce.15.cloned.1.call-start = ((), (), s32[]{:S(2)}) async-start(), calls=%async_computation.57 | async-start | bytes 17891328 | tf_op jit(solution)/shard_map/psum | solution.py:371
  1644.6 176.2 %reduce-scatter.55.cloned.1.call-start = ((), (), s32[]{:S(2)}) async-start(), calls=%async_computation.44 | async-start | bytes 3932160 | tf_op jit(solution)/shard_map/reduce_scatter | solution.py:43
  (132 other events, 4229.4 us)
Sparse Core Ops, SparseCore 0:
  29.3 36.4 all-gather.12
  103.6 60.5 reduce-scatter.32
  165.7 37.0 all-gather.14
  204.8 35.9 all-gather.16
  261.9 59.1 reduce-scatter.34
  324.5 37.0 all-gather.18
  370.9 59.0 reduce-scatter.36
  777.1 59.1 reduce-scatter.40
  987.1 36.9 all-gather.28
  1026.3 7.9 reduce-scatter.52
  1036.6 10.2 reduce-scatter.50
  1048.9 10.2 reduce-scatter.46
  1079.8 8.0 reduce-scatter.44
  1090.6 27.3 reduce-scatter.78
  1120.7 26.0 reduce-scatter.76
  1149.5 26.0 reduce-scatter.74
  1178.4 26.0 reduce-scatter.72
  1207.4 30.8 reduce-scatter.68
  1241.3 30.9 reduce-scatter.64
  1275.1 30.9 reduce-scatter.66
  1309.0 26.1 reduce-scatter.62
  1338.6 26.0 reduce-scatter.56
  1367.7 26.0 reduce-scatter.60
  1396.5 26.0 reduce-scatter.58
  1425.9 218.6 reduce-scatter.70
  1647.4 60.2 reduce-scatter.48
  1712.8 43.5 all-reduce.14
  1759.2 61.5 reduce-scatter.54
Sparse Core Ops, SparseCore 1:
  373.1 119.5 all-gather.22
  494.7 36.9 all-gather.20
  666.9 59.1 reduce-scatter.38
  730.7 36.8 all-gather.24
  840.7 36.9 all-gather.26
  924.1 59.1 reduce-scatter.42
where the time goes:
time: 1860 us; the launch traced here: 1850 us
  waiting for transfers between devices  1170 us (63%)
  matrix products  302 us (16%)
  blocking collectives  201 us (11%)
  other arithmetic  90 us (5%)
  local copies, waits for them, and re-layouts  68 us (4%)
  between operations  19.7 us (1%)
    reduce_scatter x8, waiting for transfers between devices, settle(): return lax.psum_scatter(partial_sum, 'tp', scatter_dimension=0, tiled=True)  475 us
    reduce_scatter x1, waiting for transfers between devices, per_device(): lax.psum_scatter(embedding_grad, 'shard', scatter_dimension=1, tiled=True)  222 us
    all_gather x8, waiting for transfers between devices, spread(): return lax.all_gather(rows, 'tp', axis=0, tiled=True)  151 us
    dot_general x11, matrix products, left_t(): jnp.einsum('ra,rb->ab', left, right, preferred_element_type=jnp.float32)  68.6 us
    unnamed x293, local copies, waits for them, and re-layouts  59.5 us
    all_gather x1, waiting for transfers between devices, per_device(): lax.all_gather(embedding, 'shard', axis=1, tiled=True)  59.2 us
    dot_general x13, matrix products, matmul(): return jnp.dot(left, right, preferred_element_type=jnp.float32)  52.7 us
    all_gather x3, blocking collectives, combined_all(): everything = jax.tree.map(lambda part: lax.all_gather(part, axis), shard)  39.3 us
  transfers between devices with their start and end apart: 34, of which 25 were waited for; matrix products, arithmetic and copies ran while one was open for 11% of the time, Pallas kernels for 0%

commit v1 on v0

v1 whole, which is shorter than its diff:
```python
from functools import partial

import jax
import jax.numpy as jnp
from jax import lax
from jax.experimental import pallas as pl
from jax.experimental.pallas import tpu as pltpu
from jax.sharding import PartitionSpec as P

HEAD_DIM = 64
EPS = 1e-06
MASKED = -1e30
BF = jnp.bfloat16
F32 = jnp.float32
VMEM_LIMIT = 58 * 2**20


def attend_kernel(limit_ref, seen_ref, qt_ref, k_ref, vt_ref, o_ref, ot_ref, lse_ref, *, masked, blocks, chunk):
    half = lax.broadcasted_iota(jnp.int32, (2 * HEAD_DIM, 1), 0) // HEAD_DIM
    for head in range(2):
        part = slice(head * HEAD_DIM, (head + 1) * HEAD_DIM)
        for index, (first, count) in enumerate(blocks):
            columns = slice(first, first + count)
            qt = jnp.where(half == head, qt_ref[:, columns], 0).astype(BF)

            def step(i, carry):
                top, total, acc = carry
                start = pl.multiple_of(i * chunk, chunk)
                scores = jnp.dot(k_ref[pl.ds(start, chunk), :], qt, preferred_element_type=F32)
                if masked:
                    key = lax.broadcasted_iota(jnp.int32, (chunk, 1), 0) + start
                    scores = jnp.where(key < seen_ref[:, columns], scores, MASKED)
                new_top = jnp.maximum(top, jnp.max(scores, axis=0, keepdims=True))
                expo = jnp.exp(scores - new_top)
                shrink = jnp.exp(top - new_top)
                total = total * shrink + jnp.sum(expo, axis=0, keepdims=True)
                acc = acc * shrink + jnp.dot(
                    vt_ref[part, pl.ds(start, chunk)], expo.astype(BF), preferred_element_type=F32
                )
                return (new_top, total, acc)

            init = (
                jnp.full((1, count), MASKED, F32),
                jnp.zeros((1, count), F32),
                jnp.zeros((HEAD_DIM, count), F32),
            )
            if masked:
                top, total, acc = lax.fori_loop(0, limit_ref[index], step, init)
            else:
                top, total, acc = lax.fori_loop(0, k_ref.shape[0] // chunk, step, init, unroll=True)
            ot_ref[part, columns] = acc / total
            lse_ref[0, head : head + 1, columns] = top + jnp.log(total)
    o_ref[...] = jnp.transpose(ot_ref[...]).astype(BF)


def attend(limit, seen, qt, keys, values_t, masked, blocks, chunk):
    width, rows = qt.shape
    count = keys.shape[0]
    pairs = width // (2 * HEAD_DIM)
    pair = 2 * HEAD_DIM
    return pl.pallas_call(
        partial(attend_kernel, masked=masked, blocks=blocks, chunk=chunk),
        grid_spec=pltpu.PrefetchScalarGridSpec(
            num_scalar_prefetch=1,
            grid=(pairs,),
            in_specs=[
                pl.BlockSpec((1, rows), lambda p, lim: (0, 0)),
                pl.BlockSpec((pair, rows), lambda p, lim: (p, 0)),
                pl.BlockSpec((count, pair), lambda p, lim: (0, p)),
                pl.BlockSpec((pair, count), lambda p, lim: (p, 0)),
            ],
            out_specs=[
                pl.BlockSpec((rows, pair), lambda p, lim: (0, p)),
                pl.BlockSpec((pair, rows), lambda p, lim: (p, 0)),
                pl.BlockSpec((1, 8, rows), lambda p, lim: (p, 0, 0)),
            ],
        ),
        out_shape=(
            jax.ShapeDtypeStruct((rows, width), BF),
            jax.ShapeDtypeStruct((width, rows), F32),
            jax.ShapeDtypeStruct((pairs, 8, rows), F32),
        ),
        compiler_params=pltpu.CompilerParams(vmem_limit_bytes=VMEM_LIMIT),
        cost_estimate=pl.CostEstimate(
            flops=4 * rows * count * width, transcendentals=rows * count * width // HEAD_DIM,
            bytes_accessed=2 * count * width * 2 + 8 * rows * width,
        ),
        name="attend",
    )(limit, seen, qt, keys, values_t)


def attend_back_kernel(
    limit_ref, seen_ref, qt_ref, q_ref, k_ref, kt_ref, v_ref, do_ref, dot_ref, ot_ref, lse_ref,
    dq_ref, dk_ref, dv_ref, dk_acc, dv_acc, dqt_acc, *, masked, blocks, chunk,
):
    half = lax.broadcasted_iota(jnp.int32, (2 * HEAD_DIM, 1), 0) // HEAD_DIM
    lane = lax.broadcasted_iota(jnp.int32, (1, 2 * HEAD_DIM), 1) // HEAD_DIM
    dk_acc[...] = jnp.zeros_like(dk_acc)
    dv_acc[...] = jnp.zeros_like(dv_acc)
    for head in range(2):
        part = slice(head * HEAD_DIM, (head + 1) * HEAD_DIM)
        for index, (first, count) in enumerate(blocks):
            columns = slice(first, first + count)
            qt = jnp.where(half == head, qt_ref[:, columns], 0).astype(BF)
            dot_t = jnp.where(half == head, dot_ref[:, columns], 0).astype(BF)
            q = jnp.where(lane == head, q_ref[columns, :], 0).astype(BF)
            do = jnp.where(lane == head, do_ref[columns, :], 0).astype(BF)
            inner = jnp.sum(
                dot_ref[part, columns].astype(F32) * ot_ref[part, columns], axis=0, keepdims=True
            )
            lse = lse_ref[0, head : head + 1, columns]

            def step(i, acc):
                start = pl.multiple_of(i * chunk, chunk)
                here = pl.ds(start, chunk)
                scores = jnp.dot(k_ref[here, :], qt, preferred_element_type=F32)
                probs = jnp.exp(scores - lse)
                if masked:
                    key = lax.broadcasted_iota(jnp.int32, (chunk, 1), 0) + start
                    probs = jnp.where(key < seen_ref[:, columns], probs, 0.0)
                grad_probs = jnp.dot(v_ref[here, :], dot_t, preferred_element_type=F32)
                grad_scores = (probs * (grad_probs - inner)).astype(BF)
                dv_acc[here, :] += jnp.dot(probs.astype(BF), do, preferred_element_type=F32)
                dk_acc[here, :] += jnp.dot(grad_scores, q, preferred_element_type=F32)
                return acc + jnp.dot(kt_ref[part, here], grad_scores, preferred_element_type=F32)

            init = jnp.zeros((HEAD_DIM, count), F32)
            if masked:
                acc = lax.fori_loop(0, limit_ref[index], step, init)
            else:
                acc = lax.fori_loop(0, k_ref.shape[0] // chunk, step, init, unroll=True)
            dqt_acc[part, columns] = acc * HEAD_DIM**-0.5
    dq_ref[...] = jnp.transpose(dqt_acc[...]).astype(BF)
    dk_ref[...] = dk_acc[...].astype(BF)
    dv_ref[...] = dv_acc[...].astype(BF)


def attend_back(limit, seen, qt, query, keys, keys_t, values, grad, grad_t, out_t, lse, masked, blocks, chunk):
    width, rows = qt.shape
    count = keys.shape[0]
    pairs = width // (2 * HEAD_DIM)
    pair = 2 * HEAD_DIM
    by_row = pl.BlockSpec((pair, rows), lambda p, lim: (p, 0))
    by_column = pl.BlockSpec((rows, pair), lambda p, lim: (0, p))
    key_spec = pl.BlockSpec((count, pair), lambda p, lim: (0, p))
    return pl.pallas_call(
        partial(attend_back_kernel, masked=masked, blocks=blocks, chunk=chunk),
        grid_spec=pltpu.PrefetchScalarGridSpec(
            num_scalar_prefetch=1,
            grid=(pairs,),
            in_specs=[
                pl.BlockSpec((1, rows), lambda p, lim: (0, 0)),
                by_row,
                by_column,
                key_spec,
                pl.BlockSpec((pair, count), lambda p, lim: (p, 0)),
                key_spec,
                by_column,
                by_row,
                by_row,
                pl.BlockSpec((1, 8, rows), lambda p, lim: (p, 0, 0)),
            ],
            out_specs=[by_column, key_spec, key_spec],
            scratch_shapes=[
                pltpu.VMEM((count, pair), F32),
                pltpu.VMEM((count, pair), F32),
                pltpu.VMEM((pair, rows), F32),
            ],
        ),
        out_shape=(
            jax.ShapeDtypeStruct((rows, width), BF),
            jax.ShapeDtypeStruct((count, width), BF),
            jax.ShapeDtypeStruct((count, width), BF),
        ),
        compiler_params=pltpu.CompilerParams(vmem_limit_bytes=VMEM_LIMIT),
        cost_estimate=pl.CostEstimate(
            flops=10 * rows * count * width, transcendentals=rows * count * width // HEAD_DIM,
            bytes_accessed=5 * count * width * 2 + 14 * rows * width,
        ),
        name="attend_back",
    )(limit, seen, qt, query, keys, keys_t, values, grad, grad_t, out_t, lse)


def head_stats_kernel(pieces_ref, nt_ref, target_ref, stats_ref, emb_ref, *, vocab, block, rows, scale):
    step = pl.program_id(0)
    ids = lax.broadcasted_iota(jnp.int32, (block, 1), 0) + step * block
    emb = jnp.concatenate([pieces_ref[g] for g in range(pieces_ref.shape[0])], axis=1)
    emb = jnp.where(ids < vocab, emb, 0).astype(BF)
    emb_ref[...] = emb

    @pl.when(step == 0)
    def _():
        stats_ref[0:1, :] = jnp.full((1, stats_ref.shape[1]), MASKED, F32)
        stats_ref[1:8, :] = jnp.zeros((7, stats_ref.shape[1]), F32)

    for first in range(0, nt_ref.shape[1], rows):
        columns = slice(first, first + rows)
        logits = jnp.dot(emb, nt_ref[:, columns], preferred_element_type=F32) * scale
        logits = jnp.where(ids < vocab, logits, MASKED)
        hit = (ids == target_ref[:, columns]) & (ids < vocab)
        top = stats_ref[0:1, columns]
        new_top = jnp.maximum(top, jnp.max(logits, axis=0, keepdims=True))
        stats_ref[0:1, columns] = new_top
        stats_ref[1:2, columns] = stats_ref[1:2, columns] * jnp.exp(top - new_top) + jnp.sum(
            jnp.exp(logits - new_top), axis=0, keepdims=True
        )
        stats_ref[2:3, columns] += jnp.sum(jnp.where(hit, logits, 0.0), axis=0, keepdims=True)


def head_stats(pieces, normed_t, target, block, rows):
    groups, vocab, width = pieces.shape
    depth, total = normed_t.shape
    steps = pl.cdiv(vocab, block)
    return pl.pallas_call(
        partial(head_stats_kernel, vocab=vocab, block=block, rows=rows, scale=depth**-0.5),
        grid=(steps,),
        in_specs=[
            pl.BlockSpec((groups, block, width), lambda i: (0, i, 0)),
            pl.BlockSpec((depth, total), lambda i: (0, 0)),
            pl.BlockSpec((1, total), lambda i: (0, 0)),
        ],
        out_specs=[
            pl.BlockSpec((8, total), lambda i: (0, 0)),
            pl.BlockSpec((block, depth), lambda i: (i, 0)),
        ],
        out_shape=(
            jax.ShapeDtypeStruct((8, total), F32),
            jax.ShapeDtypeStruct((steps * block, depth), BF),
        ),
        compiler_params=pltpu.CompilerParams(vmem_limit_bytes=VMEM_LIMIT),
        cost_estimate=pl.CostEstimate(
            flops=2 * vocab * depth * total, transcendentals=vocab * total,
            bytes_accessed=4 * vocab * depth + 2 * depth * total,
        ),
        name="head_stats",
    )(pieces, normed_t, target)


def head_back_kernel(emb_ref, nt_ref, n_ref, target_ref, lse_ref, de_ref, dn_ref, dnt_acc, *, vocab, block, rows, scale):
    step = pl.program_id(0)
    ids = lax.broadcasted_iota(jnp.int32, (block, 1), 0) + step * block
    emb = emb_ref[...]
    emb_t = jnp.transpose(emb)

    @pl.when(step == 0)
    def _():
        dnt_acc[...] = jnp.zeros_like(dnt_acc)

    de = None
    for first in range(0, nt_ref.shape[1], rows):
        columns = slice(first, first + rows)
        logits = jnp.dot(emb, nt_ref[:, columns], preferred_element_type=F32) * scale
        probs = jnp.exp(logits - lse_ref[:, columns])
        probs = jnp.where(ids == target_ref[:, columns], probs - 1.0, probs)
        grad = jnp.where(ids < vocab, probs, 0.0).astype(BF)
        term = jnp.dot(grad, n_ref[columns, :], preferred_element_type=F32)
        de = term if de is None else de + term
        dnt_acc[:, columns] += jnp.dot(emb_t, grad, preferred_element_type=F32)
    de = (de * scale).astype(BF)
    width = de_ref.shape[2]
    for g in range(de_ref.shape[0]):
        de_ref[g] = de[:, g * width : (g + 1) * width]

    @pl.when(step == pl.num_programs(0) - 1)
    def _():
        dn_ref[...] = (jnp.transpose(dnt_acc[...]) * scale).astype(BF)


def head_back(emb, normed_t, normed, target, lse, groups, vocab, block, rows):
    depth, total = normed_t.shape
    steps = pl.cdiv(vocab, block)
    width = depth // groups
    return pl.pallas_call(
        partial(head_back_kernel, vocab=vocab, block=block, rows=rows, scale=depth**-0.5),
        grid=(steps,),
        in_specs=[
            pl.BlockSpec((block, depth), lambda i: (i, 0)),
            pl.BlockSpec((depth, total), lambda i: (0, 0)),
            pl.BlockSpec((total, depth), lambda i: (0, 0)),
            pl.BlockSpec((1, total), lambda i: (0, 0)),
            pl.BlockSpec((1, total), lambda i: (0, 0)),
        ],
        out_specs=[
            pl.BlockSpec((groups, block, width), lambda i: (0, i, 0)),
            pl.BlockSpec((total, depth), lambda i: (0, 0)),
        ],
        out_shape=(
            jax.ShapeDtypeStruct((groups, vocab, width), BF),
            jax.ShapeDtypeStruct((total, depth), BF),
        ),
        scratch_shapes=[pltpu.VMEM((depth, total), F32)],
        compiler_params=pltpu.CompilerParams(vmem_limit_bytes=VMEM_LIMIT),
        cost_estimate=pl.CostEstimate(
            flops=6 * vocab * depth * total, transcendentals=vocab * total,
            bytes_accessed=4 * vocab * depth + 6 * depth * total,
        ),
        name="head_back",
    )(emb, normed_t, normed, target, lse)


def normalize(hidden, gain):
    inverse = lax.rsqrt(jnp.mean(hidden * hidden, axis=-1, keepdims=True) + EPS)
    return (hidden * inverse * gain, inverse)


def norm_back(hidden, inverse, gain, upstream):
    scaled = upstream * gain
    inner = jnp.mean(scaled * hidden, axis=-1, keepdims=True)
    return inverse * scaled - hidden * (inverse * inverse * inverse) * inner


def matmul(left, right):
    return jnp.dot(left, right, preferred_element_type=F32)


def left_t(left, right):
    return jnp.einsum("ra,rb->ab", left, right, preferred_element_type=F32)


def right_t(left, right):
    return jnp.einsum("ra,ba->rb", left, right, preferred_element_type=F32)


def swap(array):
    return lax.ppermute(array, "ctx", [(0, 1), (1, 0)])


def per_device(
    inputs, encoder, prefix, targets, cotangent, gain_self, query_self, key_self, value_self, output_self,
    gain_cross, query_cross, key_cross, value_cross, output_cross, gain_hidden, gate_weight, up_weight,
    down_weight, gain_exit, embedding,
):
    tp = lax.axis_size("tp")
    ctx = lax.axis_size("ctx")
    shards = lax.axis_size("shard")
    assert tp == 4 and ctx == 2
    core = lax.axis_index("ctx")
    place = lax.axis_index("tp")
    rows, depth = inputs.shape
    group = rows * tp
    total = group * ctx
    hb = query_self.shape[1]
    width = 2 * hb
    fb = gate_weight.shape[1]
    pair = rows * ctx

    route_a = []
    route_b = []
    for c in range(2):
        for z in range(4):
            dest = c * 4 + z
            route_a.append(((z % 2) * 4 + 2 * c + z // 2, dest))
            route_b.append(((z % 2) * 4 + 2 * c + 1 - z // 2, dest))
    both = ("ctx", "tp")

    def spread_weights(parts):
        block = jnp.concatenate(parts, axis=1)
        first = lax.ppermute(block, both, route_a)
        second = lax.ppermute(block, both, route_b)
        columns = []
        start = 0
        for piece in parts:
            stop = start + piece.shape[1]
            columns += [first[:, start:stop], second[:, start:stop]]
            start = stop
        return lax.all_gather(jnp.concatenate(columns, axis=1), "shard", axis=0, tiled=True)

    def collect_weights(grad, widths):
        mine = lax.psum_scatter(grad, "shard", scatter_dimension=0, tiled=True)
        first = []
        second = []
        start = 0
        for size in widths:
            first.append(mine[:, start : start + size])
            second.append(mine[:, start + size : start + 2 * size])
            start += 2 * size
        back = lambda route: [(dest, source) for source, dest in route]
        one = lax.ppermute(jnp.concatenate(first, axis=1), both, back(route_a))
        two = lax.ppermute(jnp.concatenate(second, axis=1), both, back(route_b))
        part = (one.astype(F32) + two.astype(F32)).astype(BF)
        whole = part.astype(F32) + swap(part).astype(F32)
        outs = []
        start = 0
        for size in widths:
            outs.append(whole[:, start : start + size])
            start += size
        return outs

    def couple(own, other):
        return jnp.where(
            core == 0, jnp.concatenate([own, other], axis=0), jnp.concatenate([other, own], axis=0)
        )

    gains = lax.all_gather(jnp.stack([gain_self, gain_cross, gain_hidden, gain_exit]), "shard", axis=1, tiled=True)
    gain_one, gain_two, gain_three, gain_four = [gains[i].astype(F32) for i in range(4)]

    own_f = inputs.astype(F32)
    normed1_own, inverse1_own = normalize(own_f, gain_one)
    normed1_own = normed1_own.astype(BF)
    normed1 = lax.all_gather(normed1_own, both, axis=0, tiled=True)
    weights_self = spread_weights([query_self, key_self, value_self, output_self.T])
    encoder_all = lax.all_gather(encoder, both, axis=0, tiled=True)
    weights_cross = spread_weights([query_cross, key_cross, value_cross, output_cross.T])
    weights_ff = spread_weights([gate_weight, up_weight, down_weight.T])
    vocab_half = embedding.shape[0] // ctx
    emb_mine = lax.dynamic_slice_in_dim(embedding, core * vocab_half, vocab_half, axis=0)
    emb_pieces = lax.all_gather(emb_mine, "shard", axis=0)
    if shards != 4:
        emb_pieces = jnp.transpose(emb_pieces, (1, 0, 2)).reshape(1, vocab_half, depth)

    hidden0 = couple(inputs, swap(inputs)).astype(F32)
    cotangent_pair = couple(cotangent, swap(cotangent)).astype(F32)
    targets_all = couple(targets, swap(targets))

    def take_pair(array):
        cut = array.reshape(ctx, group, depth)
        return lax.dynamic_slice_in_dim(cut, place * rows, rows, axis=1).reshape(pair, depth)

    normed1_pair = take_pair(normed1)
    query_w, key_w, value_w, out_w = [weights_self[:, i * width : (i + 1) * width] for i in range(4)]
    scale = HEAD_DIM**-0.5

    def project_q(normed, weight):
        query = matmul(normed, weight).astype(BF) * jnp.asarray(scale, BF)
        return query, query.T

    positions = jnp.concatenate(
        [c * group + place * rows + jnp.arange(rows, dtype=jnp.int32) for c in range(2)]
    )
    limit = prefix[0]
    seen = jnp.maximum(positions + 1, limit)[None, :]
    chunk = 512
    last0 = jnp.maximum((place + 1) * rows, limit)
    last1 = jnp.maximum(group + (place + 1) * rows, limit)
    limits = jnp.stack([(last0 + chunk - 1) // chunk, (last1 + chunk - 1) // chunk]).astype(jnp.int32)
    causal_blocks = ((0, rows), (rows, rows))
    open_blocks = ((0, pair),)

    query1, query1_t = project_q(normed1_pair, query_w)
    key1 = matmul(normed1, key_w).astype(BF)
    value1 = matmul(normed1, value_w).astype(BF)
    attended1, attended1_t, lse1 = attend(
        limits, seen, query1_t, key1, value1.T, True, causal_blocks, chunk
    )

    def add_halves(partial_sum):
        part = partial_sum.astype(BF)
        return partial_sum + swap(part).astype(F32)

    hidden1 = hidden0 + add_halves(right_t(attended1, out_w))
    query2_w, key2_w, value2_w, out2_w = [weights_cross[:, i * width : (i + 1) * width] for i in range(4)]
    key2 = matmul(encoder_all, key2_w).astype(BF)
    value2 = matmul(encoder_all, value2_w).astype(BF)
    normed2, inverse2 = normalize(hidden1, gain_two)
    normed2 = normed2.astype(BF)
    query2, query2_t = project_q(normed2, query2_w)
    attended2, attended2_t, lse2 = attend(
        limits, seen, query2_t, key2, value2.T, False, open_blocks, chunk
    )
    hidden2 = hidden1 + add_halves(right_t(attended2, out2_w))
    normed3, inverse3 = normalize(hidden2, gain_three)
    normed3 = normed3.astype(BF)
    gate_w, up_w, down_w = [weights_ff[:, i * 2 * fb : (i + 1) * 2 * fb] for i in range(3)]
    gate = matmul(normed3, gate_w)
    upper = matmul(normed3, up_w)
    active = jax.nn.gelu(gate, approximate=True)
    product = (active * upper).astype(BF)
    final = hidden2 + add_halves(right_t(product, down_w))
    normed4, inverse4 = normalize(final, gain_four)
    normed4 = normed4.astype(BF)

    def mine(array):
        return lax.dynamic_slice_in_dim(array, core * rows, rows, axis=0)

    final_own = mine(final)
    normed4_all = lax.all_gather(mine(normed4), both, axis=0, tiled=True)
    normed4_t = normed4_all.T
    local_target = (targets_all - (place * embedding.shape[0] + core * vocab_half))[None, :].astype(jnp.int32)
    vblock, rblock = 512, 512
    stats, emb = head_stats(emb_pieces, normed4_t, local_target, vblock, rblock)
    every = lax.all_gather(stats[:3], both, axis=0)
    top = jnp.max(every[:, 0], axis=0)
    summed = jnp.sum(every[:, 1] * jnp.exp(every[:, 0] - top[None]), axis=0)
    picked = jnp.sum(every[:, 2], axis=0)
    logsum = top + jnp.log(summed)
    exit_loss = lax.dynamic_slice_in_dim(logsum - picked, core * group, group, axis=0)
    groups = emb_pieces.shape[0]
    emb_grad, grad_normed4 = head_back(
        emb, normed4_t, normed4_all, local_target, logsum[None, :], groups, vocab_half, vblock, rblock
    )
    if shards != 4:
        emb_grad = jnp.transpose(emb_grad.reshape(vocab_half, shards, depth // shards), (1, 0, 2))
    emb_sum = lax.psum_scatter(
        emb_grad.reshape(shards * vocab_half, depth // shards), "shard", scatter_dimension=0, tiled=True
    )
    embedding_grad = couple(emb_sum, swap(emb_sum)).astype(F32)

    gn4_own = lax.psum_scatter(grad_normed4, both, scatter_dimension=0, tiled=True)
    gn4 = couple(gn4_own, swap(gn4_own)).astype(F32)
    gain4_rows = gn4 * final * inverse4
    grad_final = cotangent_pair + norm_back(final, inverse4, gain_four, gn4)
    grad_final_b = grad_final.astype(BF)
    down_grad = left_t(grad_final_b, product).astype(BF)
    grad_product = matmul(grad_final_b, down_w)
    unused, gelu_pull = jax.vjp(partial(jax.nn.gelu, approximate=True), gate)
    grad_gate = gelu_pull(grad_product * upper)[0].astype(BF)
    grad_upper = (grad_product * active).astype(BF)
    gate_grad = left_t(normed3, grad_gate).astype(BF)
    upper_grad = left_t(normed3, grad_upper).astype(BF)
    ff_grads = collect_weights(jnp.concatenate([gate_grad, upper_grad, down_grad], axis=1), [fb, fb, fb])
    gn3 = add_halves(right_t(grad_gate, gate_w) + right_t(grad_upper, up_w))
    gain3_rows = gn3 * hidden2 * inverse3
    grad_hidden2 = grad_final + norm_back(hidden2, inverse3, gain_three, gn3)
    grad_hidden2_b = grad_hidden2.astype(BF)
    out2_grad = left_t(grad_hidden2_b, attended2).astype(BF)
    grad_attended2 = matmul(grad_hidden2_b, out2_w).astype(BF)
    grad_query2, grad_key2, grad_value2 = attend_back(
        limits, seen, query2_t, query2, key2, key2.T, value2, grad_attended2, grad_attended2.T,
        attended2_t, lse2, False, open_blocks, chunk,
    )
    query2_grad = left_t(normed2, grad_query2).astype(BF)
    key2_grad = left_t(encoder_all, grad_key2).astype(BF)
    value2_grad = left_t(encoder_all, grad_value2).astype(BF)
    cross_grads = collect_weights(
        jnp.concatenate([query2_grad, key2_grad, value2_grad, out2_grad], axis=1), [hb] * 4
    )
    encoder_part = (right_t(grad_key2, key2_w) + right_t(grad_value2, value2_w)).astype(BF)
    encoder_grad = lax.psum_scatter(encoder_part, both, scatter_dimension=0, tiled=True).astype(F32)
    gn2 = add_halves(right_t(grad_query2, query2_w))
    gain2_rows = gn2 * hidden1 * inverse2
    grad_hidden1 = grad_hidden2 + norm_back(hidden1, inverse2, gain_two, gn2)
    grad_hidden1_b = grad_hidden1.astype(BF)
    out_grad = left_t(grad_hidden1_b, attended1).astype(BF)
    grad_attended1 = matmul(grad_hidden1_b, out_w).astype(BF)
    grad_query1, grad_key1, grad_value1 = attend_back(
        limits, seen, query1_t, query1, key1, key1.T, value1, grad_attended1, grad_attended1.T,
        attended1_t, lse1, True, causal_blocks, chunk,
    )
    query_grad = left_t(normed1_pair, grad_query1).astype(BF)
    key_grad = left_t(normed1, grad_key1).astype(BF)
    value_grad = left_t(normed1, grad_value1).astype(BF)
    self_grads = collect_weights(
        jnp.concatenate([query_grad, key_grad, value_grad, out_grad], axis=1), [hb] * 4
    )
    normed1_part = right_t(grad_key1, key_w) + right_t(grad_value1, value_w)
    query_part = right_t(grad_query1, query_w).reshape(ctx, rows, depth)
    cut = normed1_part.reshape(ctx, group, depth)
    old = lax.dynamic_slice_in_dim(cut, place * rows, rows, axis=1)
    cut = lax.dynamic_update_slice_in_dim(cut, old + query_part, place * rows, axis=1)
    gn1 = lax.psum_scatter(
        cut.reshape(total, depth).astype(BF), both, scatter_dimension=0, tiled=True
    ).astype(F32)
    inputs_grad = mine(grad_hidden1) + norm_back(own_f, inverse1_own, gain_one, gn1)
    gain1_sum = jnp.sum(gn1 * own_f * inverse1_own, axis=0)
    gain_sums = jnp.stack(
        [gain1_sum] + [jnp.sum(mine(a), axis=0) for a in (gain2_rows, gain3_rows, gain4_rows)]
    )
    gain_sums = lax.psum(gain_sums, ("shard", "ctx", "tp"))
    part = depth // shards
    gain_grads = lax.dynamic_slice_in_dim(gain_sums, lax.axis_index("shard") * part, part, axis=1)
    return (
        final_own.astype(BF), exit_loss, inputs_grad, encoder_grad,
        gain_grads[0], self_grads[0], self_grads[1], self_grads[2], self_grads[3].T,
        gain_grads[1], cross_grads[0], cross_grads[1], cross_grads[2], cross_grads[3].T,
        gain_grads[2], ff_grads[0], ff_grads[1], ff_grads[2].T,
        gain_grads[3], embedding_grad,
    )


def solution(mesh):
    rows = P(("shard", "ctx", "tp"), None)
    into = P("shard", "tp")
    out = P("tp", "shard")
    gain = P("shard")
    weights = (gain, into, into, into, out, gain, into, into, into, out, gain, into, into, out, gain, out)
    return jax.shard_map(
        per_device,
        mesh=mesh,
        in_specs=(rows, rows, P("shard"), P(("shard", "ctx")), rows) + weights,
        out_specs=(rows, P(("shard", "ctx")), rows, rows) + weights,
        check_vma=False,
    )
```

time: 1860 us -> 1060 us (0.57)
  waiting for transfers between devices: 1170 us -> 484 us
  matrix products: 302 us -> 79.2 us
  Pallas kernels: 0 us -> 150 us
  blocking collectives: 201 us -> 75.4 us
  starting transfers between devices: 2.79 us -> 75.6 us
  local copies, waits for them, and re-layouts: 68 us -> 111 us
  other arithmetic: 90 us -> 65.2 us
    reduce_scatter x20 -> x4, waiting for transfers between devices: 913 us -> 257 us  [the longest x1 78.4 us: per_device(): lax.psum_scatter(cut.reshape(total, depth).astype(BF), both, scatter_dime...]
    dot_general x61 -> x33, matrix products: 297 us -> 79.2 us  [the longest x11 33.4 us: matmul(): return jnp.dot(left, right, preferred_element_type=F32)]
    pallas_call x0 -> x6, Pallas kernels: none -> 150 us  [the longest x1 54.3 us: head_back(): pl.pallas_call(partial(head_back_kernel, vocab=vocab, block=block, rows=r...]
    all_gather x18 -> x2, blocking collectives: 160 us -> 34.7 us  [the longest x1 25.2 us: per_device(): every = lax.all_gather(stats[:3], both, axis=0)]
    ppermute x0 -> x25, starting transfers between devices: none -> 74.6 us  [the longest x3 37.4 us: spread_weights(): second = lax.ppermute(block, both, route_b)]
    all_gather x9 -> x7, waiting for transfers between devices: 210 us -> 140 us  [the longest x1 52.9 us: per_device(): emb_pieces = lax.all_gather(emb_mine, 'shard', axis=0)]
    ppermute x0 -> x25, waiting for transfers between devices: none -> 39.9 us  [the longest x3 28.2 us: spread_weights(): second = lax.ppermute(block, both, route_b)]
    unnamed x2 -> x0, blocking collectives: 27.4 us -> none
  transfers between devices with their start and end apart: 34 -> 39, of which waited for: 25 -> 19; matrix products, arithmetic and copies ran while one was open for 11% -> 19% of each run, Pallas kernels for 0% -> 4%
where the time goes in v1:
time: 1060 us
  waiting for transfers between devices  484 us (46%)
  Pallas kernels  150 us (14%)
  local copies, waits for them, and re-layouts  111 us (10%)
  matrix products  79.2 us (7%)
  starting transfers between devices  75.6 us (7%)
  blocking collectives  75.4 us (7%)
  other arithmetic  65.2 us (6%)
  between operations  16.2 us (2%)
    reduce_scatter x1, waiting for transfers between devices, per_device(): lax.psum_scatter(cut.reshape(total, depth).astype(BF), both, scatter_dime...  78.4 us
    reduce_scatter x1, waiting for transfers between devices, per_device(): lax.psum_scatter(grad_normed4, both, scatter_dimension=0, tiled=True)  67.1 us
    unnamed x169, local copies, waits for them, and re-layouts  58.5 us
    reduce_scatter x1, waiting for transfers between devices, collect_weights(): mine = lax.psum_scatter(grad, 'shard', scatter_dimension=0, tiled=True)  58.1 us
    pallas_call x1, Pallas kernels, head_back(): pl.pallas_call(partial(head_back_kernel, vocab=vocab, block=block, rows=r...  54.3 us
    reduce_scatter x1, waiting for transfers between devices, per_device(): lax.psum_scatter(encoder_part, both, scatter_dimension=0, tiled=True)  53.7 us
    all_gather x1, waiting for transfers between devices, per_device(): emb_pieces = lax.all_gather(emb_mine, 'shard', axis=0)  52.9 us
    unnamed x17, waiting for transfers between devices  47.1 us
  transfers between devices with their start and end apart: 39, of which 19 were waited for; matrix products, arithmetic and copies ran while one was open for 19% of the time, Pallas kernels for 4%

profile of v1, /device:TPU:0, one launch (start us, length us, event | category | flops | bytes accessed | tf_op | source)
XLA Modules:
  0.0 1056.1 jit_solution(14844811888007299279)
XLA Ops:
  10.2 9.5 all-gather.2
  28.1 8.7 collective-permute-done.2
  41.8 23.3 %collective-permute-start.5 = (bf16[192,768]{1,0:T(8,128)(2,1)S(1)}, bf16[192,768]{1,0:T(8,128)(2,1)S(1)}, u32[]{:S(2)}, u32[]{:S(2)}) collective-permute-start(bf16[192,768]{1,0:T(8,128)(2,1)S(1)} %pad_maximum_fusion.11), channel_id=1, source_target_pairs={{1,0},{5,1},{0,2},{4,3},{3,4},{7,5},{2,6},{6,7},{9,8},{13,9},{8,10... | collective-permute-start | bytes 884744 | tf_op jit(solution)/shard_map/ppermute | solution.py:359
  65.8 6.4 collective-permute-done.5
  77.6 11.4 %collective-permute-start.8 = (bf16[192,1536]{1,0:T(8,128)(2,1)S(1)}, bf16[192,1536]{1,0:T(8,128)(2,1)S(1)}, u32[]{:S(2)}, u32[]{:S(2)}) collective-permute-start(bf16[192,1536]{1,0:T(8,128)(2,1)S(1)} %pad_maximum_fusion.3), channel_id=1, source_target_pairs={{1,0},{5,1},{0,2},{4,3},{3,4},{7,5},{2,6},{6,7},{9,8},{13,9},{8,10... | collective-permute-start | bytes 1769480 | tf_op jit(solution)/shard_map/ppermute | solution.py:359
  89.7 13.1 %collective-permute-done.8 = bf16[192,1536]{1,0:T(8,128)(2,1)S(1)} collective-permute-done((bf16[192,1536]{1,0:T(8,128)(2,1)S(1)}, bf16[192,1536]{1,0:T(8,128)(2,1)S(1)}, u32[]{:S(2)}, u32[]{:S(2)}) %collective-permute-start.8) | collective-permute-done | bytes 589856 | tf_op jit(solution)/shard_map/ppermute | solution.py:359
  109.2 12.2 %collective-permute-start = (bf16[256,768]{1,0:T(8,128)(2,1)S(1)}, bf16[256,768]{1,0:T(8,128)(2,1)}, u32[]{:S(2)}, u32[]{:S(2)}) collective-permute-start(bf16[256,768]{1,0:T(8,128)(2,1)S(1)} %copy-done.7), channel_id=1, source_target_pairs={{0,4},{4,0},{1,5},{5,1},{2,6},{6,2},{3,7},{7,3},{8,12},{12,8},{9,1... | collective-permute-start | bytes 1179656 | tf_op jit(solution)/shard_map/ppermute | solution.py:325
  138.2 15.4 %attend.2 = (bf16[512,384]{1,0:T(8,128)(2,1)}, f32[384,512]{1,0:T(8,128)}, f32[3,8,512]{2,1,0:T(8,128)}) custom-call(s32[2]{0:T(128)} %pad_add_fusion.limit_ref, s32[1,512]{1,0:T(1,128)} %fusion.77.seen_ref, bf16[384,512]{1,0:T(8,128)(2,1)} %copy.144.qt_ref, bf16[2048,384]{1,0:T(8,128)(2,1)} %copy.145.k_ref, bf16[384,2048]{1,0:T(8,128)(2,1)} %copy.146.vt_ref), custom_call_target="tpu_custom_call" | custom-call | flops 1610612736 | bytes 4718592 | tf_op jit(solution)/shard_map/attend/pallas_call | solution.py:61
  156.3 38.3 %all-gather.19.cloned.1.call-done = bf16[2048,768]{1,0:T(8,128)(2,1)} async-done(((bf16[256,768]{1,0:T(8,128)(2,1)}), bf16[2048,768]{1,0:T(8,128)(2,1)}) %all-gather.19.cloned.1.call-update) | async-done | bytes 3145744 | tf_op jit(solution)/shard_map/all_gather | solution.py:402
  199.8 5.1 convolution_convert_fusion
  212.6 14.8 %attend.3 = (bf16[512,384]{1,0:T(8,128)(2,1)}, f32[384,512]{1,0:T(8,128)}, f32[3,8,512]{2,1,0:T(8,128)}) custom-call(s32[2]{0:T(128)} %pad_add_fusion.limit_ref, s32[1,512]{1,0:T(1,128)} %fusion.77.seen_ref, bf16[384,512]{1,0:T(8,128)(2,1)} %copy.149.qt_ref, bf16[2048,384]{1,0:T(8,128)(2,1)} %copy.150.k_ref, bf16[384,2048]{1,0:T(8,128)(2,1)} %copy.151.vt_ref), custom_call_target="tpu_custom_call" | custom-call | flops 1610612736 | bytes 4718592 | tf_op jit(solution)/shard_map/attend/pallas_call | solution.py:61
  233.6 18.6 %all-gather.21.cloned.1.call-done = bf16[768,3072]{1,0:T(8,128)(2,1)} async-done(((bf16[192,3072]{1,0:T(8,128)(2,1)}), bf16[768,3072]{1,0:T(8,128)(2,1)}) %all-gather.21.cloned.1.call-update) | async-done | bytes 4718608 | tf_op jit(solution)/shard_map/all_gather | solution.py:366
  271.3 52.9 %all-gather.25.cloned.1.call-done = bf16[4,4016,192]{1,2,0:T(8,128)(2,1)} async-done(((bf16[1,4016,192]{1,2,0:T(8,128)(2,1)}), bf16[4,4016,192]{1,2,0:T(8,128)(2,1)}) %all-gather.25.cloned.1.call-update) | async-done | bytes 6168592 | tf_op jit(solution)/shard_map/all_gather | solution.py:407
  324.1 10.6 %copy.152.pieces_ref = bf16[4,4016,192]{2,1,0:T(8,128)(2,1)} copy(bf16[4,4016,192]{1,2,0:T(8,128)(2,1)} %all-gather.25.cloned.1.call-done) | data formatting | bytes 12337152 | tf_op jit(solution)/shard_map/all_gather | solution.py:407
  334.7 29.9 %all-gather.23.cloned.1.call-done.n_ref = bf16[2048,768]{1,0:T(8,128)(2,1)} async-done(((bf16[256,768]{1,0:T(8,128)(2,1)}), bf16[2048,768]{1,0:T(8,128)(2,1)}) %all-gather.23.cloned.1.call-update) | async-done | bytes 3145744 | tf_op jit(solution)/shard_map/all_gather | solution.py:476
  364.6 4.6 copy.153.nt_ref
  369.3 29.2 %head_stats.1 = (f32[8,2048]{1,0:T(8,128)}, bf16[4096,768]{1,0:T(8,128)(2,1)}) custom-call(bf16[4,4016,192]{2,1,0:T(8,128)(2,1)} %copy.152.pieces_ref, bf16[768,2048]{1,0:T(8,128)(2,1)} %copy.153.nt_ref, s32[1,2048]{1,0:T(1,128)} %fusion.72.target_ref), custom_call_target="tpu_custom_call" | custom-call | flops 12633243648 | bytes 15482880 | tf_op jit(solution)/shard_map/head_stats/pallas_call | solution.py:214
  399.3 25.2 %all-gather.4 = f32[8,3,2048]{2,1,0:T(4,128)S(1)} all-gather(f32[1,3,2048]{2,1,0:T(4,128)S(1)} %slice_bitcast_fusion.3), channel_id=3, replica_groups=mesh['shard'=4,'ctx'=2,'tp'=4] {'ctx','tp'}, dimensions={0}, use_global_device_ids=true | all-gather | bytes 221184 | tf_op jit(solution)/shard_map/all_gather | solution.py:481
  426.0 54.3 %head_back.1 = (bf16[4,4016,192]{2,1,0:T(8,128)(2,1)}, bf16[2048,768]{1,0:T(8,128)(2,1)}) custom-call(bf16[4096,768]{1,0:T(8,128)(2,1)} %get-tuple-element.39.emb_ref, bf16[768,2048]{1,0:T(8,128)(2,1)} %copy.153.nt_ref, bf16[2048,768]{1,0:T(8,128)(2,1)} %all-gather.23.cloned.1.call-done.n_ref, s32[1,2048]{1,0:T(1,128)} %fusion.72.target_ref, f32[1,2048]{1,0:T(1,128)} %bitcast.127), custom_call_target="tpu_custom_call" | custom-call | flops 37899730944 | bytes 21774336 | tf_op jit(solution)/shard_map/head_back/pallas_call | solution.py:273
  480.9 67.1 %reduce-scatter.14.cloned.1.call-done = bf16[256,768]{1,0:T(8,128)(2,1)} async-done(((bf16[2048,768]{1,0:T(8,128)(2,1)}), bf16[256,768]{1,0:T(8,128)(2,1)}) %reduce-scatter.14.cloned.1.call-update) | async-done | bytes 393232 | tf_op jit(solution)/shard_map/reduce_scatter | solution.py:498
  571.2 19.4 %attend_back.2 = (bf16[512,384]{1,0:T(8,128)(2,1)}, bf16[2048,384]{1,0:T(8,128)(2,1)}, bf16[2048,384]{1,0:T(8,128)(2,1)}) custom-call(s32[2]{0:T(128)} %pad_add_fusion.limit_ref, s32[1,512]{1,0:T(1,128)} %fusion.77.seen_ref, bf16[384,512]{1,0:T(8,128)(2,1)} %copy.149.qt_ref, bf16[512,384]{1,0:T(8,128)(2,1)} %copy-done.38, bf16[2048,384]{1,0:T(8,128)(2,1)} %copy.150.k_ref, ...), custom_call_target="tpu_custom_call" | custom-call | flops 4026531840 | bytes 10616832 | tf_op jit(solution)/shard_map/attend_back/pallas_call | solution.py:146
  614.8 16.8 %attend_back.3 = (bf16[512,384]{1,0:T(8,128)(2,1)}, bf16[2048,384]{1,0:T(8,128)(2,1)}, bf16[2048,384]{1,0:T(8,128)(2,1)}) custom-call(s32[2]{0:T(128)} %pad_add_fusion.limit_ref, s32[1,512]{1,0:T(1,128)} %fusion.77.seen_ref, bf16[384,512]{1,0:T(8,128)(2,1)} %copy.144.qt_ref, bf16[512,384]{1,0:T(8,128)(2,1)} %copy-done.37, bf16[2048,384]{1,0:T(8,128)(2,1)} %copy.145.k_ref, ...), custom_call_target="tpu_custom_call" | custom-call | flops 4026531840 | bytes 10616832 | tf_op jit(solution)/shard_map/attend_back/pallas_call | solution.py:146
  649.9 4.6 add_convert_fusion
  708.4 4.6 collective-permute-start.15
  721.6 4.9 collective-permute-start.16
  732.2 45.7 %reduce-scatter.26.cloned.1.call-done = bf16[4016,192]{1,0:T(8,128)(2,1)} async-done(((bf16[16064,192]{1,0:T(8,128)(2,1)}), bf16[4016,192]{1,0:T(8,128)(2,1)}) %reduce-scatter.26.cloned.1.call-update) | async-done | bytes 1542160
  795.0 53.7 %reduce-scatter.18.cloned.1.call-done = bf16[256,768]{1,0:T(8,128)(2,1)} async-done(((bf16[2048,768]{1,0:T(8,128)(2,1)}), bf16[256,768]{1,0:T(8,128)(2,1)}) %reduce-scatter.18.cloned.1.call-update) | async-done | bytes 393232 | tf_op jit(solution)/shard_map/reduce_scatter | solution.py:528
  850.6 58.1 %reduce-scatter.20.cloned.1.call-done = bf16[192,3072]{1,0:T(8,128)(2,1)} async-done(((bf16[768,3072]{1,0:T(8,128)(2,1)}), bf16[192,3072]{1,0:T(8,128)(2,1)}) %reduce-scatter.20.cloned.1.call-update) | async-done | bytes 1179664 | tf_op jit(solution)/shard_map/reduce_scatter | solution.py:369
  911.0 6.0 collective-permute-start.21
  917.8 4.3 fusion
  922.2 78.4 %reduce-scatter.16.cloned.1.call-done = bf16[256,768]{1,0:T(8,128)(2,1)} async-done(((bf16[2048,768]{1,0:T(8,128)(2,1)}), bf16[256,768]{1,0:T(8,128)(2,1)}) %reduce-scatter.16.cloned.1.call-update) | async-done | bytes 393232 | tf_op jit(solution)/shard_map/reduce_scatter | solution.py:550
  1002.7 40.7 %psum.7 = f32[4,768]{1,0:T(4,128)S(1)} all-reduce(f32[4,768]{1,0:T(4,128)S(1)} %pad_maximum_fusion.12), channel_id=1, replica_groups=mesh['shard'=4,'ctx'=2,'tp'=4] {'shard','ctx','tp'}, use_global_device_ids=true, to_apply=%region_18.19 | all-reduce | flops 3072 | bytes 24576 | tf_op jit(solution)/shard_map/psum | solution.py:558
  (370 shorter events, 252.2 us)
Async XLA Ops:
  7.2 116.0 %all-gather.13.cloned.1.call-start = ((), (), s32[]{:S(2)}) async-start(), calls=%async_computation.7 | async-start | bytes 3538944 | tf_op jit(solution)/shard_map/all_gather | solution.py:400
  23.5 101.0 %all-gather.15.cloned.1.call-start = ((), (), s32[]{:S(2)}) async-start(), calls=%async_computation.8 | async-start | bytes 2949120 | tf_op jit(solution)/shard_map/all_gather | solution.py:366
  24.7 12.0 %collective-permute-start.2 = (bf16[192,768]{1,0:T(8,128)(2,1)S(1)}, bf16[192,768]{1,0:T(8,128)(2,1)S(1)}, u32[]{:S(2)}, u32[]{:S(2)}) collective-permute-start(bf16[192,768]{1,0:T(8,128)(2,1)S(1)} %pad_maximum_fusion.10), channel_id=1, source_target_pairs={{1,0},{5,1},{0,2},{4,3},{3,4},{7,5},{2,6},{6,7},{9,8},{13,9},{8,10... | collective-permute-start | bytes 884744 | tf_op jit(solution)/shard_map/ppermute | solution.py:359
  27.4 9.5 collective-permute-start.1
  39.7 116.6 %all-gather.17.cloned.1.call-start = ((), (), s32[]{:S(2)}) async-start(), calls=%async_computation.9 | async-start | bytes 2949120 | tf_op jit(solution)/shard_map/all_gather | solution.py:366
  41.8 30.4 %collective-permute-start.5 = (bf16[192,768]{1,0:T(8,128)(2,1)S(1)}, bf16[192,768]{1,0:T(8,128)(2,1)S(1)}, u32[]{:S(2)}, u32[]{:S(2)}) collective-permute-start(bf16[192,768]{1,0:T(8,128)(2,1)S(1)} %pad_maximum_fusion.11), channel_id=1, source_target_pairs={{1,0},{5,1},{0,2},{4,3},{3,4},{7,5},{2,6},{6,7},{9,8},{13,9},{8,10... | collective-permute-start | bytes 884744 | tf_op jit(solution)/shard_map/ppermute | solution.py:359
  65.1 7.2 collective-permute-start.4
  75.1 119.5 %all-gather.19.cloned.1.call-start = ((), (), s32[]{:S(2)}) async-start(), calls=%async_computation.10 | async-start | bytes 3538944 | tf_op jit(solution)/shard_map/all_gather | solution.py:402
  75.7 176.6 %all-gather.21.cloned.1.call-start = ((), (), s32[]{:S(2)}) async-start(), calls=%async_computation.11 | async-start | bytes 5898240 | tf_op jit(solution)/shard_map/all_gather | solution.py:366
  76.9 12.1 %collective-permute-start.7 = (bf16[192,1536]{1,0:T(8,128)(2,1)S(1)}, bf16[192,1536]{1,0:T(8,128)(2,1)S(1)}, u32[]{:S(2)}, u32[]{:S(2)}) collective-permute-start(bf16[192,1536]{1,0:T(8,128)(2,1)S(1)} %pad_maximum_fusion.3), channel_id=1, source_target_pairs={{0,0},{4,1},{1,2},{5,3},{2,4},{6,5},{3,6},{7,7},{8,8},{12,9},{9,10... | collective-permute-start | bytes 1769480 | tf_op jit(solution)/shard_map/ppermute | solution.py:358
  77.6 25.3 %collective-permute-start.8 = (bf16[192,1536]{1,0:T(8,128)(2,1)S(1)}, bf16[192,1536]{1,0:T(8,128)(2,1)S(1)}, u32[]{:S(2)}, u32[]{:S(2)}) collective-permute-start(bf16[192,1536]{1,0:T(8,128)(2,1)S(1)} %pad_maximum_fusion.3), channel_id=1, source_target_pairs={{1,0},{5,1},{0,2},{4,3},{3,4},{7,5},{2,6},{6,7},{9,8},{13,9},{8,10... | collective-permute-start | bytes 1769480 | tf_op jit(solution)/shard_map/ppermute | solution.py:359
  106.5 217.7 %all-gather.25.cloned.1.call-start = ((), (), s32[]{:S(2)}) async-start(), calls=%async_computation.17 | async-start | bytes 7864320 | tf_op jit(solution)/shard_map/all_gather | solution.py:407
  108.3 256.4 %all-gather.23.cloned.1.call-start = ((), (), s32[]{:S(2)}) async-start(), calls=%async_computation.12 | async-start | bytes 3538944 | tf_op jit(solution)/shard_map/all_gather | solution.py:476
  109.2 98.3 %collective-permute-start = (bf16[256,768]{1,0:T(8,128)(2,1)S(1)}, bf16[256,768]{1,0:T(8,128)(2,1)}, u32[]{:S(2)}, u32[]{:S(2)}) collective-permute-start(bf16[256,768]{1,0:T(8,128)(2,1)S(1)} %copy-done.7), channel_id=1, source_target_pairs={{0,4},{4,0},{1,5},{5,1},{2,6},{6,2},{3,7},{7,3},{8,12},{12,8},{9,1... | collective-permute-start | bytes 1179656 | tf_op jit(solution)/shard_map/ppermute | solution.py:325
  156.3 51.2 %collective-permute-start.3 = (bf16[512,768]{1,0:T(8,128)(2,1)}, bf16[512,768]{1,0:T(8,128)(2,1)}, u32[]{:S(2)}, u32[]{:S(2)}) collective-permute-start(bf16[512,768]{1,0:T(8,128)(2,1)} %get-tuple-element.217), channel_id=1, source_target_pairs={{0,4},{4,0},{1,5},{5,1},{2,6},{6,2},{3,7},{7,3},{8,12},{12,8},{9,1... | collective-permute-start | bytes 2359304 | tf_op jit(solution)/shard_map/ppermute | solution.py:325
  269.4 278.6 %reduce-scatter.14.cloned.1.call-start = ((), (), s32[]{:S(2)}) async-start(), calls=%async_computation.13 | async-start | bytes 3538944 | tf_op jit(solution)/shard_map/reduce_scatter | solution.py:498
  480.3 198.6 %reduce-scatter.24.cloned.1.call-start = ((), (), s32[]{:S(2)}) async-start(), calls=%async_computation.19 | async-start | bytes 2949120
  548.1 3.9 collective-permute-start.11
  603.2 94.2 %reduce-scatter.22.cloned.1.call-start = ((), (), s32[]{:S(2)}) async-start(), calls=%async_computation.18 | async-start | bytes 2949120
  645.6 132.3 %reduce-scatter.26.cloned.1.call-start = ((), (), s32[]{:S(2)}) async-start(), calls=%async_computation.20 | async-start | bytes 10280960
  646.3 202.4 %reduce-scatter.18.cloned.1.call-start = ((), (), s32[]{:S(2)}) async-start(), calls=%async_computation.15 | async-start | bytes 3538944 | tf_op jit(solution)/shard_map/reduce_scatter | solution.py:528
  654.5 254.2 %reduce-scatter.20.cloned.1.call-start = ((), (), s32[]{:S(2)}) async-start(), calls=%async_computation.16 | async-start | bytes 5898240 | tf_op jit(solution)/shard_map/reduce_scatter | solution.py:369
  662.6 338.0 %reduce-scatter.16.cloned.1.call-start = ((), (), s32[]{:S(2)}) async-start(), calls=%async_computation.14 | async-start | bytes 3538944 | tf_op jit(solution)/shard_map/reduce_scatter | solution.py:550
  685.2 41.3 %collective-permute-start.18 = (bf16[192,768]{0,1:T(8,128)(2,1)S(1)}, bf16[192,768]{0,1:T(8,128)(2,1)}, u32[]{:S(2)}, u32[]{:S(2)}) collective-permute-start(bf16[192,768]{0,1:T(8,128)(2,1)S(1)} %pad_maximum_fusion.8), channel_id=1, source_target_pairs={{0,0},{1,4},{2,1},{3,5},{4,2},{5,6},{6,3},{7,7},{8,8},{9,12},{10,9... | collective-permute-start | bytes 884744 | tf_op jit(solution)/shard_map/ppermute | solution.py:378
  695.1 31.5 %collective-permute-start.19 = (bf16[192,768]{0,1:T(8,128)(2,1)}, bf16[192,768]{0,1:T(8,128)(2,1)}, u32[]{:S(2)}, u32[]{:S(2)}) collective-permute-start(bf16[192,768]{0,1:T(8,128)(2,1)} %pad_maximum_fusion.9), channel_id=1, source_target_pairs={{0,1},{1,5},{2,0},{3,4},{4,3},{5,7},{6,2},{7,6},{8,9},{9,13},{10,8... | collective-permute-start | bytes 884744 | tf_op jit(solution)/shard_map/ppermute | solution.py:379
  708.4 72.4 %collective-permute-start.15 = (bf16[192,768]{0,1:T(8,128)(2,1)}, bf16[192,768]{0,1:T(8,128)(2,1)}, u32[]{:S(2)}, u32[]{:S(2)}) collective-permute-start(bf16[192,768]{0,1:T(8,128)(2,1)} %pad_maximum_fusion.6), channel_id=1, source_target_pairs={{0,0},{1,4},{2,1},{3,5},{4,2},{5,6},{6,3},{7,7},{8,8},{9,12},{10,9... | collective-permute-start | bytes 884744 | tf_op jit(solution)/shard_map/ppermute | solution.py:378
  721.6 59.2 %collective-permute-start.16 = (bf16[192,768]{0,1:T(8,128)(2,1)}, bf16[192,768]{0,1:T(8,128)(2,1)}, u32[]{:S(2)}, u32[]{:S(2)}) collective-permute-start(bf16[192,768]{0,1:T(8,128)(2,1)} %pad_maximum_fusion.7), channel_id=1, source_target_pairs={{0,1},{1,5},{2,0},{3,4},{4,3},{5,7},{6,2},{7,6},{8,9},{9,13},{10,8... | collective-permute-start | bytes 884744 | tf_op jit(solution)/shard_map/ppermute | solution.py:379
  728.5 54.1 %collective-permute-start.20 = (bf16[192,768]{0,1:T(8,128)(2,1)}, bf16[192,768]{0,1:T(8,128)(2,1)}, u32[]{:S(2)}, u32[]{:S(2)}) collective-permute-start(bf16[192,768]{0,1:T(8,128)(2,1)} %add_convert_fusion.2), channel_id=1, source_target_pairs={{0,4},{4,0},{1,5},{5,1},{2,6},{6,2},{3,7},{7,3},{8,12},{12,8},{9,1... | collective-permute-start | bytes 884744 | tf_op jit(solution)/shard_map/ppermute | solution.py:325
  780.7 137.1 %collective-permute-start.24 = (bf16[4016,192]{0,1:T(8,128)(2,1)S(1)}, bf16[4016,192]{0,1:T(8,128)(2,1)S(1)}, u32[]{:S(2)}, u32[]{:S(2)}) collective-permute-start(bf16[4016,192]{0,1:T(8,128)(2,1)S(1)} %copy.180), channel_id=1, source_target_pairs={{0,4},{4,0},{1,5},{5,1},{2,6},{6,2},{3,7},{7,3},{8,12},{12,8},{9,1... | collective-permute-start | bytes 4626440 | tf_op jit(solution)/shard_map/ppermute | solution.py:325
  782.0 7.8 collective-permute-start.17
  911.0 132.4 %collective-permute-start.21 = (bf16[192,1536]{1,0:T(8,128)(2,1)}, bf16[192,1536]{1,0:T(8,128)(2,1)}, u32[]{:S(2)}, u32[]{:S(2)}) collective-permute-start(bf16[192,1536]{1,0:T(8,128)(2,1)} %pad_maximum_fusion.4), channel_id=1, source_target_pairs={{0,0},{1,4},{2,1},{3,5},{4,2},{5,6},{6,3},{7,7},{8,8},{9,12},{10,9... | collective-permute-start | bytes 1769480 | tf_op jit(solution)/shard_map/ppermute | solution.py:378
  917.8 125.6 %collective-permute-start.22 = (bf16[192,1536]{1,0:T(8,128)(2,1)}, bf16[192,1536]{1,0:T(8,128)(2,1)}, u32[]{:S(2)}, u32[]{:S(2)}) collective-permute-start(bf16[192,1536]{1,0:T(8,128)(2,1)} %pad_maximum_fusion.5), channel_id=1, source_target_pairs={{0,1},{1,5},{2,0},{3,4},{4,3},{5,7},{6,2},{7,6},{8,9},{9,13},{10,8... | collective-permute-start | bytes 1769480 | tf_op jit(solution)/shard_map/ppermute | solution.py:379
  (74 other events, 1089.6 us)
Sparse Core Ops, SparseCore 0:
  23.6 41.3 all-gather.12
  67.5 47.8 all-gather.14
  117.2 37.4 all-gather.16
  156.2 38.3 all-gather.18
  196.3 55.9 all-gather.20
  253.9 70.1 all-gather.24
  326.3 38.2 all-gather.22
  480.5 67.4 reduce-scatter.13
  603.3 36.6 reduce-scatter.23
  645.7 42.5 reduce-scatter.21
  691.5 86.2 reduce-scatter.25
  780.0 68.6 reduce-scatter.17
  852.3 56.4 reduce-scatter.19
  910.9 89.6 reduce-scatter.15

commit v2 on v1

--- a/solution.py
+++ b/solution.py
@@ -181,11 +181,27 @@
     )(limit, seen, qt, query, keys, keys_t, values, grad, grad_t, out_t, lse)
 
 
+def vocab_ids(step, block, vocab):
+    row = lax.broadcasted_iota(jnp.int32, (block, 1), 0)
+    second = (row >= block // 2).astype(jnp.int32)
+    local = row - second * (block // 2) + step * (block // 2)
+    return local + second * (vocab // 2), local < vocab // 2
+
+
 def head_stats_kernel(pieces_ref, nt_ref, target_ref, stats_ref, emb_ref, *, vocab, block, rows, scale):
     step = pl.program_id(0)
-    ids = lax.broadcasted_iota(jnp.int32, (block, 1), 0) + step * block
-    emb = jnp.concatenate([pieces_ref[g] for g in range(pieces_ref.shape[0])], axis=1)
-    emb = jnp.where(ids < vocab, emb, 0).astype(BF)
+    ids, valid = vocab_ids(step, block, vocab)
+    width = pieces_ref.shape[2] // 2
+    emb = jnp.concatenate(
+        [
+            jnp.concatenate(
+                [pieces_ref[g, :, p * width : (p + 1) * width] for g in range(pieces_ref.shape[0])], axis=1
+            )
+            for p in range(2)
+        ],
+        axis=0,
+    )
+    emb = jnp.where(valid, emb, 0).astype(BF)
     emb_ref[...] = emb
 
     @pl.when(step == 0)
@@ -196,8 +212,8 @@
     for first in range(0, nt_ref.shape[1], rows):
         columns = slice(first, first + rows)
         logits = jnp.dot(emb, nt_ref[:, columns], preferred_element_type=F32) * scale
-        logits = jnp.where(ids < vocab, logits, MASKED)
-        hit = (ids == target_ref[:, columns]) & (ids < vocab)
+        logits = jnp.where(valid, logits, MASKED)
+        hit = (ids == target_ref[:, columns]) & valid
         top = stats_ref[0:1, columns]
         new_top = jnp.maximum(top, jnp.max(logits, axis=0, keepdims=True))
         stats_ref[0:1, columns] = new_top
@@ -209,13 +225,14 @@
 
 def head_stats(pieces, normed_t, target, block, rows):
     groups, vocab, width = pieces.shape
+    vocab *= 2
     depth, total = normed_t.shape
     steps = pl.cdiv(vocab, block)
     return pl.pallas_call(
         partial(head_stats_kernel, vocab=vocab, block=block, rows=rows, scale=depth**-0.5),
         grid=(steps,),
         in_specs=[
-            pl.BlockSpec((groups, block, width), lambda i: (0, i, 0)),
+            pl.BlockSpec((groups, block // 2, width), lambda i: (0, i, 0)),
             pl.BlockSpec((depth, total), lambda i: (0, 0)),
             pl.BlockSpec((1, total), lambda i: (0, 0)),
         ],
@@ -238,7 +255,7 @@
 
 def head_back_kernel(emb_ref, nt_ref, n_ref, target_ref, lse_ref, de_ref, dn_ref, dnt_acc, *, vocab, block, rows, scale):
     step = pl.program_id(0)
-    ids = lax.broadcasted_iota(jnp.int32, (block, 1), 0) + step * block
+    ids, valid = vocab_ids(step, block, vocab)
     emb = emb_ref[...]
     emb_t = jnp.transpose(emb)
 
@@ -252,14 +269,15 @@
         logits = jnp.dot(emb, nt_ref[:, columns], preferred_element_type=F32) * scale
         probs = jnp.exp(logits - lse_ref[:, columns])
         probs = jnp.where(ids == target_ref[:, columns], probs - 1.0, probs)
-        grad = jnp.where(ids < vocab, probs, 0.0).astype(BF)
+        grad = jnp.where(valid, probs, 0.0).astype(BF)
         term = jnp.dot(grad, n_ref[columns, :], preferred_element_type=F32)
         de = term if de is None else de + term
         dnt_acc[:, columns] += jnp.dot(emb_t, grad, preferred_element_type=F32)
     de = (de * scale).astype(BF)
-    width = de_ref.shape[2]
+    width = de_ref.shape[2] // 2
     for g in range(de_ref.shape[0]):
-        de_ref[g] = de[:, g * width : (g + 1) * width]
+        part = de[:, g * width : (g + 1) * width]
+        de_ref[g] = jnp.concatenate([part[: block // 2], part[block // 2 :]], axis=1)
 
     @pl.when(step == pl.num_programs(0) - 1)
     def _():
@@ -281,11 +299,11 @@
             pl.BlockSpec((1, total), lambda i: (0, 0)),
         ],
         out_specs=[
-            pl.BlockSpec((groups, block, width), lambda i: (0, i, 0)),
+            pl.BlockSpec((groups, block // 2, 2 * width), lambda i: (0, i, 0)),
             pl.BlockSpec((total, depth), lambda i: (0, 0)),
         ],
         out_shape=(
-            jax.ShapeDtypeStruct((groups, vocab, width), BF),
+            jax.ShapeDtypeStruct((groups, vocab // 2, 2 * width), BF),
             jax.ShapeDtypeStruct((total, depth), BF),
         ),
         scratch_shapes=[pltpu.VMEM((depth, total), F32)],
@@ -296,6 +314,461 @@
         ),
         name="head_back",
     )(emb, normed_t, normed, target, lse)
+
+
+MESH = pl.DeviceIdType.MESH
+
+
+class Peers:
+    def __init__(self):
+        self.s, self.c, self.t = (lax.axis_index(name) for name in ("shard", "ctx", "tp"))
+        s, c, t = self.s, self.c, self.t
+        self.sx = s + 1 - 2 * lax.rem(s, 2)
+        self.sy = lax.rem(s + 2, 4)
+        self.sd = lax.rem(self.sx + 2, 4)
+        self.x = (self.sx, c, t)
+        self.y = (self.sy, c, t)
+        self.d = (self.sd, c, t)
+        self.core = (s, 1 - c, t)
+        self.z = [(s, c, lax.rem(t + k, 4)) for k in range(4)]
+        self.z_other = [(s, 1 - c, lax.rem(t + k, 4)) for k in range(4)]
+        self.group = self.z[1:] + self.z_other
+        odd = lax.rem(t, 2)
+        self.give = [
+            (s, t // 2, 2 * odd + 1 - c),
+            (s, t // 2, 2 * (1 - odd) + c),
+        ]
+        self.back = [
+            (s, 1 - odd, 2 * c + t // 2),
+            (s, odd, 2 * c + 1 - t // 2),
+        ]
+
+
+def meet(peers):
+    barrier = pltpu.get_barrier_semaphore()
+    for peer in peers:
+        pl.semaphore_signal(barrier, inc=1, device_id=peer, device_id_type=MESH)
+    pl.semaphore_wait(barrier, len(peers))
+
+
+class Sender:
+    def __init__(self, sends, arrivals):
+        self.sends, self.arrivals, self.count = sends, arrivals, 0
+        self.all = []
+
+    def to(self, peer, source, target):
+        copy = pltpu.make_async_remote_copy(
+            src_ref=source, dst_ref=target, send_sem=self.sends.at[self.count],
+            recv_sem=self.arrivals.at[self.count], device_id=peer, device_id_type=MESH,
+        )
+        self.count += 1
+        self.all.append(copy)
+        copy.start()
+        return copy
+
+    def finish(self):
+        for copy in self.all:
+            copy.wait_send()
+
+
+def send_rows(send, me, own, everyone, rows):
+    here = everyone.at[pl.ds((me.c * 4 + me.t) * rows, rows)]
+    over_z = [send.to(me.z[k], own, here) for k in (1, 2, 3)]
+    across = [send.to(me.core, own, here)]
+    return over_z, across
+
+
+def pass_rows(send, me, over_z, across, everyone, rows):
+    for k in (1, 2, 3):
+        over_z[k - 1].wait_recv()
+        there = everyone.at[pl.ds((me.c * 4 + lax.rem(me.t + 4 - k, 4)) * rows, rows)]
+        across.append(send.to(me.core, there, there))
+
+
+def start_kernel(n_ref, e_ref, x_ref, g_ref, t_ref, b0, b1, b2, n_all, e_all, x_pair, g_pair, t_pair, w0, w1, w2, take0, take1, take2, mix0, mix1, mix2, sends, arrivals, local, *, cuts):
+    me = Peers()
+    meet(me.group + [me.x, me.y])
+    send = Sender(sends, arrivals)
+    rows = n_ref.shape[0]
+    own_rows = pl.ds((me.c * 4 + me.t) * rows, rows)
+    locals_ = [
+        pltpu.make_async_copy(n_ref, n_all.at[own_rows], local.at[0]),
+        pltpu.make_async_copy(e_ref, e_all.at[own_rows], local.at[1]),
+    ]
+    pairs = []
+    for ref, pair in ((x_ref, x_pair), (g_ref, g_pair), (t_ref, t_pair)):
+        where = pair.at[pl.ds(me.c * ref.shape[0], ref.shape[0])]
+        locals_.append(pltpu.make_async_copy(ref, where, local.at[len(locals_)]))
+        pairs.append((ref, where))
+    for copy in locals_:
+        copy.start()
+    bundles = [(b0, take0, mix0, w0), (b1, take1, mix1, w1), (b2, take2, mix2, w2)]
+
+    def give(block, take):
+        return [send.to(me.give[i], block, take.at[i]) for i in range(2)]
+
+    given = [give(b0, take0)]
+    n_z, n_c = send_rows(send, me, n_ref, n_all, rows)
+    given.append(give(b1, take1))
+    given.append(give(b2, take2))
+    swapped = [send.to(me.core, ref, where) for ref, where in pairs]
+    e_z, e_c = send_rows(send, me, e_ref, e_all, rows)
+    depth = b0.shape[0]
+    half = depth // 2
+    mine = pl.ds(me.s * depth, depth)
+    over = []
+    for i, (block, take, mix, w) in enumerate(bundles):
+        for copy in given[i]:
+            copy.wait_recv()
+        first = take[0]
+        second = take[1]
+        columns = []
+        for start, stop in cuts[i]:
+            columns += [first[:, start:stop], second[:, start:stop]]
+        mix[...] = jnp.concatenate(columns, axis=1)
+        copy = pltpu.make_async_copy(mix, w.at[mine], local.at[len(locals_)])
+        copy.start()
+        locals_.append(copy)
+        over.append((send.to(me.x, mix, w.at[mine]), send.to(me.y, mix, w.at[mine])))
+    pass_rows(send, me, n_z, n_c, n_all, rows)
+    onward = []
+    for i, (block, take, mix, w) in enumerate(bundles):
+        to_x, to_y = over[i]
+        to_x.wait_recv()
+        part = w.at[pl.ds(me.sx * depth, half)]
+        onward.append(send.to(me.y, part, part))
+        to_y.wait_recv()
+        part = w.at[pl.ds(me.sy * depth + half, half)]
+        onward.append(send.to(me.x, part, part))
+    pass_rows(send, me, e_z, e_c, e_all, rows)
+    for copy in onward + n_c + e_c + swapped:
+        copy.wait_recv()
+    send.finish()
+    for copy in locals_:
+        copy.wait()
+
+
+def start_gather(normed, encoder, inputs, cotangent, targets, bundles, cuts):
+    rows, depth = normed.shape
+    part = bundles[0].shape[0]
+    any_space = pl.BlockSpec(memory_space=pl.ANY)
+    vmem = pl.BlockSpec(memory_space=pltpu.VMEM)
+    return pl.pallas_call(
+        partial(start_kernel, cuts=cuts),
+        in_specs=[vmem] * 8,
+        out_specs=[any_space] * 8,
+        out_shape=[jax.ShapeDtypeStruct((8 * rows, depth), BF)] * 2
+        + [jax.ShapeDtypeStruct((2 * a.shape[0], a.shape[1]), a.dtype) for a in (inputs, cotangent, targets)]
+        + [jax.ShapeDtypeStruct((4 * part, 2 * b.shape[1]), BF) for b in bundles],
+        scratch_shapes=[pltpu.VMEM((2,) + b.shape, BF) for b in bundles]
+        + [pltpu.VMEM((part, 2 * b.shape[1]), BF) for b in bundles]
+        + [pltpu.SemaphoreType.DMA((35,)), pltpu.SemaphoreType.DMA((35,)), pltpu.SemaphoreType.DMA((8,))],
+        compiler_params=pltpu.CompilerParams(collective_id=0, has_side_effects=True, vmem_limit_bytes=VMEM_LIMIT),
+        name="start_gather",
+    )(normed, encoder, inputs, cotangent, targets, *bundles)
+
+
+def rows_kernel(n_ref, n_all, sends, arrivals, local):
+    me = Peers()
+    meet(me.z[1:] + [me.core])
+    send = Sender(sends, arrivals)
+    rows = n_ref.shape[0]
+    copy = pltpu.make_async_copy(n_ref, n_all.at[pl.ds((me.c * 4 + me.t) * rows, rows)], local)
+    copy.start()
+    over_z, across = send_rows(send, me, n_ref, n_all, rows)
+    pass_rows(send, me, over_z, across, n_all, rows)
+    for arriving in across:
+        arriving.wait_recv()
+    send.finish()
+    copy.wait()
+
+
+def gather_rows(normed):
+    rows, depth = normed.shape
+    return pl.pallas_call(
+        rows_kernel,
+        in_specs=[pl.BlockSpec(memory_space=pltpu.VMEM)],
+        out_specs=pl.BlockSpec(memory_space=pl.ANY),
+        out_shape=jax.ShapeDtypeStruct((8 * rows, depth), normed.dtype),
+        scratch_shapes=[pltpu.SemaphoreType.DMA((8,)), pltpu.SemaphoreType.DMA((8,)), pltpu.SemaphoreType.DMA],
+        compiler_params=pltpu.CompilerParams(collective_id=1, has_side_effects=True, vmem_limit_bytes=VMEM_LIMIT),
+        name="gather_rows",
+    )(normed)
+
+
+def stats_kernel(stats_ref, out_ref, slots, sends, arrivals):
+    me = Peers()
+    meet(me.group)
+    send = Sender(sends, arrivals)
+    here = slots.at[me.c * 4 + me.t]
+    slots[me.c * 4 + me.t] = stats_ref[...]
+    copies = [send.to(peer, stats_ref, here) for peer in me.group]
+    for copy in copies:
+        copy.wait_recv()
+    top = slots[0, 0:1]
+    for i in range(1, 8):
+        top = jnp.maximum(top, slots[i, 0:1])
+    total = jnp.zeros_like(top)
+    picked = jnp.zeros_like(top)
+    for i in range(8):
+        total += slots[i, 1:2] * jnp.exp(slots[i, 0:1] - top)
+        picked += slots[i, 2:3]
+    logsum = top + jnp.log(total)
+    out_ref[0:1] = logsum
+    out_ref[1:2] = logsum - picked
+    out_ref[2:8] = jnp.zeros((6, top.shape[1]), F32)
+    send.finish()
+
+
+def combine_stats(stats):
+    return pl.pallas_call(
+        stats_kernel,
+        in_specs=[pl.BlockSpec(memory_space=pltpu.VMEM)],
+        out_specs=pl.BlockSpec(memory_space=pltpu.VMEM),
+        out_shape=jax.ShapeDtypeStruct(stats.shape, F32),
+        scratch_shapes=[pltpu.VMEM((8,) + stats.shape, F32), pltpu.SemaphoreType.DMA((8,)), pltpu.SemaphoreType.DMA((8,))],
+        compiler_params=pltpu.CompilerParams(collective_id=2, has_side_effects=True),
+        name="combine_stats",
+    )(stats)
+
+
+def settle_first(send, me, part_ref, other, half):
+    return send.to(me.core, part_ref.at[pl.ds((1 - me.c) * half, half)], other)
+
+
+def settle_second(send, me, part_ref, other, summed, landed, rows):
+    half = 4 * rows
+    for k in range(4):
+        start = lax.rem(me.t + k, 4) * rows
+        summed[k] = (
+            part_ref[pl.ds(me.c * half + start, rows)].astype(F32) + other[pl.ds(start, rows)].astype(F32)
+        ).astype(BF)
+    return [send.to(me.z[k], summed.at[k], landed.at[k - 1]) for k in (1, 2, 3)]
+
+
+def settle_third(copies, summed, landed):
+    for copy in copies:
+        copy.wait_recv()
+    return (
+        summed[0].astype(F32) + landed[0].astype(F32) + landed[1].astype(F32) + landed[2].astype(F32)
+    )
+
+
+class Planar:
+    def __init__(self, send, me, part, first, second, moving, width):
+        self.send, self.me, self.part = send, me, part
+        self.first, self.second, self.moving = first, second, moving
+
+    def begin(self, chunks):
+        me = self.me
+        self.chunks = chunks
+        self.one = []
+        for start, stop, along_x in chunks:
+            here = slice(start, stop)
+            near, near_block = (me.x, me.sx) if along_x else (me.y, me.sy)
+            self.one.append(
+                (
+                    self.send.to(near, self.part.at[near_block, here], self.first.at[0, here]),
+                    self.send.to(near, self.part.at[me.sd, here], self.first.at[1, here]),
+                )
+            )
+
+    def middle(self):
+        me = self.me
+        self.two = []
+        for (start, stop, along_x), (own, far) in zip(self.chunks, self.one):
+            here = slice(start, stop)
+            peer, block = (me.y, me.sy) if along_x else (me.x, me.sx)
+            far.wait_recv()
+            self.moving[here] = (self.part[block, here].astype(F32) + self.first[1, here].astype(F32)).astype(BF)
+            self.two.append(self.send.to(peer, self.moving.at[here], self.second.at[here]))
+            own.wait_recv()
+
+    def end(self, store):
+        me = self.me
+        for (start, stop, along_x), copy in zip(self.chunks, self.two):
+            here = slice(start, stop)
+            copy.wait_recv()
+            store(
+                here,
+                self.part[me.s, here].astype(F32) + self.first[0, here].astype(F32) + self.second[here].astype(F32),
+            )
+
+
+def halves(count, parts, step):
+    middle = (count // 2 + step - 1) // step * step
+    out = []
+    for low, high, along_x in ((0, middle, True), (middle, count, False)):
+        size = ((high - low) // parts + step - 1) // step * step
+        edges = list(range(low, high, size)) + [high]
+        out.append([(a, b, along_x) for a, b in zip(edges[:-1], edges[1:])])
+    return [chunk for pair in zip(*out) for chunk in pair]
+
+
+def middle_kernel(dn_ref, de_ref, gn_ref, eg_ref, other, summed, landed, first, second, moving, sends, arrivals, *, chunks):
+    me = Peers()
+    meet(me.z[1:] + [me.core, me.x, me.y])
+    send = Sender(sends, arrivals)
+    rows = landed.shape[1]
+    crossing = settle_first(send, me, dn_ref, other, 4 * rows)
+    plane = Planar(send, me, de_ref, first, second, moving, None)
+    plane.begin(chunks)
+    crossing.wait_recv()
+    over_z = settle_second(send, me, dn_ref, other, summed, landed, rows)
+    plane.middle()
+    own = pl.ds(me.c * rows, rows)
+    gn_ref[own] = settle_third(over_z, summed, landed).astype(BF)
+    share = send.to(me.core, gn_ref.at[own], gn_ref.at[own])
+    vocab = de_ref.shape[1]
+
+    def store(here, value):
+        eg_ref[pl.ds(me.c * vocab + here.start, here.stop - here.start)] = value.astype(BF)
+
+    plane.end(store)
+    mine = pl.ds(me.c * vocab, vocab)
+    final = send.to(me.core, eg_ref.at[mine], eg_ref.at[mine])
+    share.wait_recv()
+    final.wait_recv()
+    send.finish()
+
+
+def middle_scatter(dn, de):
+    total, depth = dn.shape
+    rows = total // 8
+    groups, vocab, width = de.shape
+    chunks = halves(vocab, 3, 16)
+    count = 1 + 2 * len(chunks) + 3 + len(chunks) + 2
+    vmem = pl.BlockSpec(memory_space=pltpu.VMEM)
+    return pl.pallas_call(
+        partial(middle_kernel, chunks=chunks),
+        in_specs=[vmem, vmem],
+        out_specs=[vmem, vmem],
+        out_shape=[
+            jax.ShapeDtypeStruct((2 * rows, depth), BF),
+            jax.ShapeDtypeStruct((2 * vocab, width), BF),
+        ],
+        scratch_shapes=[
+            pltpu.VMEM((4 * rows, depth), BF),
+            pltpu.VMEM((4, rows, depth), BF),
+            pltpu.VMEM((3, rows, depth), BF),
+            pltpu.VMEM((2, vocab, width), BF),
+            pltpu.VMEM((vocab, width), BF),
+            pltpu.VMEM((vocab, width), BF),
+            pltpu.SemaphoreType.DMA((count,)),
+            pltpu.SemaphoreType.DMA((count,)),
+        ],
+        compiler_params=pltpu.CompilerParams(collective_id=3, has_side_effects=True, vmem_limit_bytes=VMEM_LIMIT),
+        name="middle_scatter",
+    )(dn, de)
+
+
+def tail_kernel(
+    dn_ref, g0, g1, f_ref, gains_ref, dn_out, o0, o1, o2, gain_out,
+    other, summed, landed, first0, second0, moving0, first1, second1, moving1,
+    ab0, ab1, ab2, in0, in1, in2, swap0, swap1, swap2, slots, plane_sum, plane_slots, sends, arrivals, *, cuts, chunks,
+):
+    me = Peers()
+    meet(me.group + [me.x, me.y, me.d])
+    send = Sender(sends, arrivals)
+    rows = landed.shape[1]
+    crossing = settle_first(send, me, dn_ref, other, 4 * rows)
+    planes = [
+        Planar(send, me, g0, first0, second0, moving0, None),
+        Planar(send, me, g1, first1, second1, moving1, None),
+    ]
+    planes[0].begin(chunks)
+    planes[1].begin(chunks)
+    slots[me.c * 4 + me.t] = gains_ref[...]
+    gain_copies = [send.to(peer, gains_ref, slots.at[me.c * 4 + me.t]) for peer in me.group]
+
+    def split(value, cut, ab):
+        for i in range(2):
+            ab[i] = jnp.concatenate(
+                [value[:, 2 * a + i * (b - a) : 2 * a + (i + 1) * (b - a)] for a, b in cut], axis=1
+            ).astype(BF)
+
+    def deliver(ab, landing):
+        return [send.to(me.back[i], ab.at[i], landing.at[i]) for i in range(2)]
+
+    split(f_ref[...], cuts[2], ab2)
+    third = deliver(ab2, in2)
+    crossing.wait_recv()
+    over_z = settle_second(send, me, dn_ref, other, summed, landed, rows)
+    for copy in gain_copies:
+        copy.wait_recv()
+    total = slots[0]
+    for i in range(1, 8):
+        total += slots[i]
+    plane_sum[...] = total
+    plane_slots[me.s] = total
+    plane_copies = [send.to(peer, plane_sum, plane_slots.at[me.s]) for peer in (me.x, me.y, me.d)]
+    delivered = []
+    for plane, cut, ab, landing, held in (
+        (planes[0], cuts[0], ab0, in0, swap0),
+        (planes[1], cuts[1], ab1, in1, swap1),
+    ):
+        plane.middle()
+
+    for plane, cut, ab, landing in ((planes[0], cuts[0], ab0, in0), (planes[1], cuts[1], ab1, in1)):
+
+        def store(here, value):
+            for i in range(2):
+                ab[i, here] = jnp.concatenate(
+                    [value[:, 2 * a + i * (b - a) : 2 * a + (i + 1) * (b - a)] for a, b in cut], axis=1
+                ).astype(BF)
+
+        plane.end(store)
+        delivered.append(deliver(ab, landing))
+    for copy in plane_copies:
+        copy.wait_recv()
+    gain_out[...] = plane_slots[0] + plane_slots[1] + plane_slots[2] + plane_slots[3]
+    shares = []
+    for copies, landing, held in ((third, in2, swap2), (delivered[0], in0, swap0), (delivered[1], in1, swap1)):
+        for copy in copies:
+            copy.wait_recv()
+        held[0] = (landing[0].astype(F32) + landing[1].astype(F32)).astype(BF)
+        shares.append(send.to(me.core, held.at[0], held.at[1]))
+    dn_out[...] = settle_third(over_z, summed, landed)
+    for share, held, out in zip(shares, (swap2, swap0, swap1), (o2, o0, o1)):
+        share.wait_recv()
+        out[...] = held[0].astype(F32) + held[1].astype(F32)
+    send.finish()
+
+
+def tail_scatter(dn, grads, ff, gains, cuts):
+    total, depth = dn.shape
+    rows = total // 8
+    groups, part, width = grads[0].shape
+    chunks = halves(part, 1, 16)
+    vmem = pl.BlockSpec(memory_space=pltpu.VMEM)
+    widths = [width // 2, width // 2, ff.shape[1] // 2]
+    scratch = [
+        pltpu.VMEM((4 * rows, depth), BF),
+        pltpu.VMEM((4, rows, depth), BF),
+        pltpu.VMEM((3, rows, depth), BF),
+    ]
+    for _ in grads:
+        scratch += [pltpu.VMEM((2, part, width), BF), pltpu.VMEM((part, width), BF), pltpu.VMEM((part, width), BF)]
+    for _ in range(3):
+        scratch += [pltpu.VMEM((2, part, w), BF) for w in widths]
+    scratch += [
+        pltpu.VMEM((8,) + gains.shape, F32),
+        pltpu.VMEM(gains.shape, F32),
+        pltpu.VMEM((4,) + gains.shape, F32),
+        pltpu.SemaphoreType.DMA((48,)),
+        pltpu.SemaphoreType.DMA((48,)),
+    ]
+    return pl.pallas_call(
+        partial(tail_kernel, cuts=cuts, chunks=chunks),
+        in_specs=[vmem] * 5,
+        out_specs=[vmem] * 5,
+        out_shape=[jax.ShapeDtypeStruct((rows, depth), F32)]
+        + [jax.ShapeDtypeStruct((part, w), F32) for w in widths]
+        + [jax.ShapeDtypeStruct(gains.shape, F32)],
+        scratch_shapes=scratch,
+        compiler_params=pltpu.CompilerParams(collective_id=4, has_side_effects=True, vmem_limit_bytes=VMEM_LIMIT),
+        name="tail_scatter",
+    )(dn, *grads, ff, gains)
 
 
 def normalize(hidden, gain):
@@ -391,26 +864,40 @@
             core == 0, jnp.concatenate([own, other], axis=0), jnp.concatenate([other, own], axis=0)
         )
 
+    fast = shards == 4
     gains = lax.all_gather(jnp.stack([gain_self, gain_cross, gain_hidden, gain_exit]), "shard", axis=1, tiled=True)
     gain_one, gain_two, gain_three, gain_four = [gains[i].astype(F32) for i in range(4)]
 
     own_f = inputs.astype(F32)
     normed1_own, inverse1_own = normalize(own_f, gain_one)
     normed1_own = normed1_own.astype(BF)
-    normed1 = lax.all_gather(normed1_own, both, axis=0, tiled=True)
-    weights_self = spread_weights([query_self, key_self, value_self, output_self.T])
-    encoder_all = lax.all_gather(encoder, both, axis=0, tiled=True)
-    weights_cross = spread_weights([query_cross, key_cross, value_cross, output_cross.T])
-    weights_ff = spread_weights([gate_weight, up_weight, down_weight.T])
+    parts_self = [query_self, key_self, value_self, output_self.T]
+    parts_cross = [query_cross, key_cross, value_cross, output_cross.T]
+    parts_ff = [gate_weight, up_weight, down_weight.T]
+    cuts = [[(i * w, (i + 1) * w) for i in range(n)] for n, w in ((4, hb), (4, hb), (3, fb))]
     vocab_half = embedding.shape[0] // ctx
     emb_mine = lax.dynamic_slice_in_dim(embedding, core * vocab_half, vocab_half, axis=0)
-    emb_pieces = lax.all_gather(emb_mine, "shard", axis=0)
-    if shards != 4:
-        emb_pieces = jnp.transpose(emb_pieces, (1, 0, 2)).reshape(1, vocab_half, depth)
-
-    hidden0 = couple(inputs, swap(inputs)).astype(F32)
-    cotangent_pair = couple(cotangent, swap(cotangent)).astype(F32)
-    targets_all = couple(targets, swap(targets))
+    emb_mine = jnp.concatenate([emb_mine[: vocab_half // 2], emb_mine[vocab_half // 2 :]], axis=1)
+    if fast:
+        bundles = [jnp.concatenate(parts, axis=1) for parts in (parts_self, parts_cross, parts_ff)]
+        normed1, encoder_all, x_pair, g_pair, t_pair, weights_self, weights_cross, weights_ff = start_gather(
+            normed1_own, encoder, inputs, cotangent, targets.reshape(8, group // 8), bundles, cuts
+        )
+        hidden0 = x_pair.astype(F32)
+        cotangent_pair = g_pair.astype(F32)
+        targets_all = t_pair.reshape(total)
+        emb_mine, normed1 = lax.optimization_barrier((emb_mine, normed1))
+        emb_pieces = lax.all_gather(emb_mine, "shard", axis=0)
+    else:
+        normed1 = lax.all_gather(normed1_own, both, axis=0, tiled=True)
+        encoder_all = lax.all_gather(encoder, both, axis=0, tiled=True)
+        weights_self, weights_cross, weights_ff = map(spread_weights, (parts_self, parts_cross, parts_ff))
+        hidden0 = couple(inputs, swap(inputs)).astype(F32)
+        cotangent_pair = couple(cotangent, swap(cotangent)).astype(F32)
+        targets_all = couple(targets, swap(targets))
+        emb_pieces = lax.all_gather(emb_mine, "shard", axis=0)
+        emb_pieces = emb_pieces.reshape(shards, vocab_half // 2, 2, depth // shards)
+        emb_pieces = jnp.transpose(emb_pieces, (1, 2, 0, 3)).reshape(1, vocab_half // 2, 2 * depth)
 
     def take_pair(array):
         cut = array.reshape(ctx, group, depth)
@@ -473,30 +960,41 @@
         return lax.dynamic_slice_in_dim(array, core * rows, rows, axis=0)
 
     final_own = mine(final)
-    normed4_all = lax.all_gather(mine(normed4), both, axis=0, tiled=True)
+    if fast:
+        normed4_all = gather_rows(mine(normed4))
+    else:
+        normed4_all = lax.all_gather(mine(normed4), both, axis=0, tiled=True)
     normed4_t = normed4_all.T
     local_target = (targets_all - (place * embedding.shape[0] + core * vocab_half))[None, :].astype(jnp.int32)
     vblock, rblock = 512, 512
     stats, emb = head_stats(emb_pieces, normed4_t, local_target, vblock, rblock)
-    every = lax.all_gather(stats[:3], both, axis=0)
-    top = jnp.max(every[:, 0], axis=0)
-    summed = jnp.sum(every[:, 1] * jnp.exp(every[:, 0] - top[None]), axis=0)
-    picked = jnp.sum(every[:, 2], axis=0)
-    logsum = top + jnp.log(summed)
-    exit_loss = lax.dynamic_slice_in_dim(logsum - picked, core * group, group, axis=0)
+    if fast:
+        combined = combine_stats(stats)
+        logsum = combined[0]
+        loss = combined[1]
+    else:
+        every = lax.all_gather(stats[:3], both, axis=0)
+        top = jnp.max(every[:, 0], axis=0)
+        summed = jnp.sum(every[:, 1] * jnp.exp(every[:, 0] - top[None]), axis=0)
+        logsum = top + jnp.log(summed)
+        loss = logsum - jnp.sum(every[:, 2], axis=0)
+    exit_loss = lax.dynamic_slice_in_dim(loss, core * group, group, axis=0)
     groups = emb_pieces.shape[0]
     emb_grad, grad_normed4 = head_back(
         emb, normed4_t, normed4_all, local_target, logsum[None, :], groups, vocab_half, vblock, rblock
     )
-    if shards != 4:
-        emb_grad = jnp.transpose(emb_grad.reshape(vocab_half, shards, depth // shards), (1, 0, 2))
-    emb_sum = lax.psum_scatter(
-        emb_grad.reshape(shards * vocab_half, depth // shards), "shard", scatter_dimension=0, tiled=True
-    )
-    embedding_grad = couple(emb_sum, swap(emb_sum)).astype(F32)
-
-    gn4_own = lax.psum_scatter(grad_normed4, both, scatter_dimension=0, tiled=True)
-    gn4 = couple(gn4_own, swap(gn4_own)).astype(F32)
+    if fast:
+        gn4, emb_sum = middle_scatter(grad_normed4, emb_grad)
+        gn4 = gn4.astype(F32)
+    else:
+        emb_grad = emb_grad.reshape(vocab_half // 2, 2, shards, depth // shards)
+        emb_grad = jnp.transpose(emb_grad, (2, 0, 1, 3)).reshape(shards * vocab_half // 2, 2 * depth // shards)
+        emb_sum = lax.psum_scatter(emb_grad, "shard", scatter_dimension=0, tiled=True)
+        emb_sum = couple(emb_sum, swap(emb_sum))
+        gn4_own = lax.psum_scatter(grad_normed4, both, scatter_dimension=0, tiled=True)
+        gn4 = couple(gn4_own, swap(gn4_own)).astype(F32)
+    emb_sum = emb_sum.reshape(2, vocab_half // 2, 2, depth // shards)
+    embedding_grad = jnp.transpose(emb_sum, (0, 2, 1, 3)).reshape(embedding.shape).astype(F32)
     gain4_rows = gn4 * final * inverse4
     grad_final = cotangent_pair + norm_back(final, inverse4, gain_four, gn4)
     grad_final_b = grad_final.astype(BF)
@@ -507,7 +1005,9 @@
     grad_upper = (grad_product * active).astype(BF)
     gate_grad = left_t(normed3, grad_gate).astype(BF)
     upper_grad = left_t(normed3, grad_upper).astype(BF)
-    ff_grads = collect_weights(jnp.concatenate([gate_grad, upper_grad, down_grad], axis=1), [fb, fb, fb])
+    ff_part = jnp.concatenate([gate_grad, upper_grad, down_grad], axis=1)
+    if fast:
+        ff_mine = lax.psum_scatter(ff_part, "shard", scatter_dimension=0, tiled=True)
     gn3 = add_halves(right_t(grad_gate, gate_w) + right_t(grad_upper, up_w))
     gain3_rows = gn3 * hidden2 * inverse3
     grad_hidden2 = grad_final + norm_back(hidden2, inverse3, gain_three, gn3)
@@ -521,9 +1021,7 @@
     query2_grad = left_t(normed2, grad_query2).astype(BF)
     key2_grad = left_t(encoder_all, grad_key2).astype(BF)
     value2_grad = left_t(encoder_all, grad_value2).astype(BF)
-    cross_grads = collect_weights(
-        jnp.concatenate([query2_grad, key2_grad, value2_grad, out2_grad], axis=1), [hb] * 4
-    )
+    cross_part = jnp.concatenate([query2_grad, key2_grad, value2_grad, out2_grad], axis=1)
     encoder_part = (right_t(grad_key2, key2_w) + right_t(grad_value2, value2_w)).astype(BF)
     encoder_grad = lax.psum_scatter(encoder_part, both, scatter_dimension=0, tiled=True).astype(F32)
     gn2 = add_halves(right_t(grad_query2, query2_w))
@@ -539,23 +1037,36 @@
     query_grad = left_t(normed1_pair, grad_query1).astype(BF)
     key_grad = left_t(normed1, grad_key1).astype(BF)
     value_grad = left_t(normed1, grad_value1).astype(BF)
-    self_grads = collect_weights(
-        jnp.concatenate([query_grad, key_grad, value_grad, out_grad], axis=1), [hb] * 4
-    )
+    self_part = jnp.concatenate([query_grad, key_grad, value_grad, out_grad], axis=1)
     normed1_part = right_t(grad_key1, key_w) + right_t(grad_value1, value_w)
     query_part = right_t(grad_query1, query_w).reshape(ctx, rows, depth)
     cut = normed1_part.reshape(ctx, group, depth)
     old = lax.dynamic_slice_in_dim(cut, place * rows, rows, axis=1)
     cut = lax.dynamic_update_slice_in_dim(cut, old + query_part, place * rows, axis=1)
-    gn1 = lax.psum_scatter(
-        cut.reshape(total, depth).astype(BF), both, scatter_dimension=0, tiled=True
-    ).astype(F32)
+    cut = cut.reshape(total, depth).astype(BF)
+
+    def gain_rows(gn1):
+        gain1_sum = jnp.sum(gn1 * own_f * inverse1_own, axis=0)
+        return jnp.stack(
+            [gain1_sum] + [jnp.sum(mine(a), axis=0) for a in (gain2_rows, gain3_rows, gain4_rows)]
+        )
+
+    if fast:
+        blocks = [a.reshape(shards, depth // shards, a.shape[1]) for a in (cross_part, self_part)]
+        gain1_part = jnp.sum(cut.astype(F32) * normed1.astype(F32), axis=0) / gain_one
+        gains_part = [gain1_part] + [jnp.sum(mine(a), axis=0) for a in (gain2_rows, gain3_rows, gain4_rows)]
+        gn1, cross_own, self_own, ff_own, gain_sums = tail_scatter(
+            cut, blocks, ff_mine, jnp.stack(gains_part + [jnp.zeros_like(gain1_part)] * 4), [cuts[1], cuts[0], cuts[2]]
+        )
+        take = lambda own, index: [own[:, a:b] for a, b in cuts[index]]
+        self_grads, cross_grads, ff_grads = take(self_own, 0), take(cross_own, 1), take(ff_own, 2)
+    else:
+        gn1 = lax.psum_scatter(cut, both, scatter_dimension=0, tiled=True).astype(F32)
+        ff_grads = collect_weights(ff_part, [fb, fb, fb])
+        cross_grads = collect_weights(cross_part, [hb] * 4)
+        self_grads = collect_weights(self_part, [hb] * 4)
+        gain_sums = lax.psum(gain_rows(gn1), ("shard", "ctx", "tp"))
     inputs_grad = mine(grad_hidden1) + norm_back(own_f, inverse1_own, gain_one, gn1)
-    gain1_sum = jnp.sum(gn1 * own_f * inverse1_own, axis=0)
-    gain_sums = jnp.stack(
-        [gain1_sum] + [jnp.sum(mine(a), axis=0) for a in (gain2_rows, gain3_rows, gain4_rows)]
-    )
-    gain_sums = lax.psum(gain_sums, ("shard", "ctx", "tp"))
     part = depth // shards
     gain_grads = lax.dynamic_slice_in_dim(gain_sums, lax.axis_index("shard") * part, part, axis=1)
     return (

time: 1060 us -> 764 us (0.72)
  waiting for transfers between devices: 484 us -> 13.9 us
  Pallas kernels: 150 us -> 509 us
  blocking collectives: 75.4 us -> 9.52 us
  starting transfers between devices: 75.6 us -> 11 us
  other arithmetic: 65.2 us -> 31.4 us
  local copies, waits for them, and re-layouts: 111 us -> 96.4 us
    pallas_call x0 -> x5, Pallas kernels: none -> 352 us  [the longest x1 126 us: start_gather(): pl.pallas_call(partial(start_kernel, cuts=cuts), in_specs=[vmem] * 8, out...]
    reduce_scatter x3 -> x1, waiting for transfers between devices: 204 us -> 7.76 us  [per_device(): lax.psum_scatter(ff_part, 'shard', scatter_dimension=0, tiled=True)]
    all_gather x6 -> x0, waiting for transfers between devices: 86.9 us -> none  [the longest x1 38.3 us: per_device(): encoder_all = lax.all_gather(encoder, both, axis=0, tiled=True)]
    ppermute x12 -> x0, starting transfers between devices: 58.7 us -> none  [the longest x3 37.4 us: spread_weights(): second = lax.ppermute(block, both, route_b)]
    reduce_scatter x1, waiting for transfers between devices: 53.7 us -> 0.01 us  [per_device(): lax.psum_scatter(encoder_part, both, scatter_dimension=0, tiled=True)]
    all_gather x1, waiting for transfers between devices: 52.9 us -> 0.01 us  [per_device(): emb_pieces = lax.all_gather(emb_mine, 'shard', axis=0)]
    unnamed x17 -> x3, waiting for transfers between devices: 47.1 us -> 0.05 us
    unnamed x169 -> x179, local copies, waits for them, and re-layouts: 58.5 us -> 14.6 us
  transfers between devices with their start and end apart: 39 -> 8, of which waited for: 19 -> 4; matrix products, arithmetic and copies ran while one was open for 19% -> 19% of each run, Pallas kernels for 4% -> 12%
where the time goes in v2:
time: 764 us; the launch traced here: 757 us
  Pallas kernels  509 us (67%)
  local copies, waits for them, and re-layouts  96.4 us (13%)
  matrix products  70.1 us (9%)
  other arithmetic  31.4 us (4%)
  between operations  15.9 us (2%)
  waiting for transfers between devices  13.9 us (2%)
  starting transfers between devices  11 us (1%)
  blocking collectives  9.52 us (1%)
    pallas_call x1, Pallas kernels, start_gather(): pl.pallas_call(partial(start_kernel, cuts=cuts), in_specs=[vmem] * 8, out...  126 us
    pallas_call x1, Pallas kernels, tail_scatter(): pl.pallas_call(partial(tail_kernel, cuts=cuts, chunks=chunks), in_specs=[...  101 us
    pallas_call x1, Pallas kernels, middle_scatter(): pl.pallas_call(partial(middle_kernel, chunks=chunks), in_specs=[vmem, vme...  63.9 us
    pallas_call x1, Pallas kernels, head_back(): pl.pallas_call(partial(head_back_kernel, vocab=vocab, block=block, rows=r...  54.9 us
    pallas_call x2, Pallas kernels, attend_back(): pl.pallas_call(partial(attend_back_kernel, masked=masked, blocks=blocks,...  39.4 us
    pallas_call x1, Pallas kernels, gather_rows(): pl.pallas_call(rows_kernel, in_specs=[pl.BlockSpec(memory_space=pltpu.VME...  37.7 us
    convert_element_type x4, local copies, waits for them, and re-layouts, per_device(): jnp.transpose(emb_sum, (0, 2, 1, 3)).reshape(embedding.shape).astype(F32)  36.5 us
    pallas_call x2, Pallas kernels, attend(): pl.pallas_call(partial(attend_kernel, masked=masked, blocks=blocks, chunk...  33.3 us
  transfers between devices with their start and end apart: 8, of which 4 were waited for; matrix products, arithmetic and copies ran while one was open for 19% of the time, Pallas kernels for 12%

profile of v2, /device:TPU:0, one launch (start us, length us, event | category | flops | bytes accessed | tf_op | source)
XLA Modules:
  0.0 757.3 jit_solution(7367694798562417625)
XLA Ops:
  11.2 9.5 %all-gather.1 = bf16[4,192,4]{1,2,0:T(4,128)(2,1)S(1)} all-gather(bf16[1,192,4]{1,2,0:T(4,128)(2,1)S(1)} %maximum_bitcast_fusion), channel_id=1, replica_groups=mesh['shard'=4,'ctx'=2,'tp'=4] {'shard'}, dimensions={0}, use_global_device_ids=true | all-gather | bytes 7680 | tf_op jit(solution)/shard_map/all_gather | solution.py:868
  27.0 125.9 %start_gather.1 = (bf16[2048,768]{1,0:T(8,128)(2,1)}, bf16[2048,768]{1,0:T(8,128)(2,1)}, bf16[512,768]{1,0:T(8,128)(2,1)}, bf16[512,768]{1,0:T(8,128)(2,1)}, s32...) custom-call(bf16[256,768]{1,0:T(8,128)(2,1)} %fusion.22.n_ref, ...), custom_call_target="tpu_custom_call" | custom-call | tf_op jit(solution)/shard_map/start_gather/pallas_call | solution.py:456
  158.4 3.6 convolution_convert_fusion.3
  162.1 2.9 copy.125.k_ref
  164.9 4.0 convolution_convert_fusion.2.v_ref
  172.7 18.2 %attend.2 = (bf16[512,384]{1,0:T(8,128)(2,1)}, f32[384,512]{1,0:T(8,128)}, f32[3,8,512]{2,1,0:T(8,128)}) custom-call(s32[2]{0:T(128)} %pad_add_fusion.limit_ref, s32[1,512]{1,0:T(1,128)} %fusion.64.seen_ref, bf16[384,512]{1,0:T(8,128)(2,1)} %copy.124.qt_ref, bf16[2048,384]{1,0:T(8,128)(2,1)} %copy.125.k_ref, bf16[384,2048]{1,0:T(8,128)(2,1)} %copy.126.vt_ref), custom_call_target="tpu_custom_call" | custom-call | flops 1610612736 | bytes 4718592 | tf_op jit(solution)/shard_map/attend/pallas_call | solution.py:61
  190.9 2.8 fusion.68
  193.7 9.8 %collective-permute-start = (bf16[512,768]{1,0:T(8,128)(2,1)}, bf16[512,768]{1,0:T(8,128)(2,1)}, u32[]{:S(2)}, u32[]{:S(2)}) collective-permute-start(bf16[512,768]{1,0:T(8,128)(2,1)} %get-tuple-element.211), channel_id=1, source_target_pairs={{0,4},{4,0},{1,5},{5,1},{2,6},{6,2},{3,7},{7,3},{8,12},{12,8},{9,1... | collective-permute-start | bytes 2359304 | tf_op jit(solution)/shard_map/ppermute | solution.py:798
  207.6 5.0 convolution_convert_fusion.v_ref
  220.2 15.1 %attend.3 = (bf16[512,384]{1,0:T(8,128)(2,1)}, f32[384,512]{1,0:T(8,128)}, f32[3,8,512]{2,1,0:T(8,128)}) custom-call(s32[2]{0:T(128)} %pad_add_fusion.limit_ref, s32[1,512]{1,0:T(1,128)} %fusion.64.seen_ref, bf16[384,512]{1,0:T(8,128)(2,1)} %copy.128.qt_ref, bf16[2048,384]{1,0:T(8,128)(2,1)} %copy.129.k_ref, bf16[384,2048]{1,0:T(8,128)(2,1)} %copy.130.vt_ref), custom_call_target="tpu_custom_call" | custom-call | flops 1610612736 | bytes 4718592 | tf_op jit(solution)/shard_map/attend/pallas_call | solution.py:61
  253.4 37.7 %gather_rows.1.n_ref = bf16[2048,768]{1,0:T(8,128)(2,1)} custom-call(bf16[256,768]{1,0:T(8,128)(2,1)} %multiply_convert_fusion.4.n_ref), custom_call_target="tpu_custom_call" | custom-call | tf_op jit(solution)/shard_map/gather_rows/pallas_call | solution.py:488
  291.1 4.8 copy.131
  295.9 29.4 %head_stats.1 = (f32[8,2048]{1,0:T(8,128)}, bf16[4096,768]{1,0:T(8,128)(2,1)}) custom-call(bf16[4,2008,384]{2,1,0:T(8,128)(2,1)} %bitcast.128, bf16[768,2048]{1,0:T(8,128)(2,1)} %bitcast.99, s32[1,2048]{1,0:T(1,128)} %bitcast.118), custom_call_target="tpu_custom_call" | custom-call | flops 12633243648 | bytes 15482880 | tf_op jit(solution)/shard_map/head_stats/pallas_call | solution.py:231
  325.3 23.7 %combine_stats.1 = f32[8,2048]{1,0:T(8,128)} custom-call(f32[8,2048]{1,0:T(8,128)} %get-tuple-element.64.stats_ref), custom_call_target="tpu_custom_call" | custom-call | tf_op jit(solution)/shard_map/combine_stats/pallas_call | solution.py:524
  350.5 54.9 %head_back.1 = (bf16[4,2008,384]{2,1,0:T(8,128)(2,1)}, bf16[2048,768]{1,0:T(8,128)(2,1)}) custom-call(bf16[4096,768]{1,0:T(8,128)(2,1)} %get-tuple-element.66.emb_ref, bf16[768,2048]{1,0:T(8,128)(2,1)} %bitcast.100, bf16[2048,768]{1,0:T(8,128)(2,1)} %gather_rows.1.n_ref, s32[1,2048]{1,0:T(1,128)} %bitcast.119, f32[1,2048]{1,0:T(1,128)} %get-tuple-element.197.lse_ref), custom_call_target="tpu_custom_call" | custom-call | flops 37899730944 | bytes 21774336 | tf_op jit(solution)/shard_map/head_back/pallas_call | solution.py:291
  405.4 63.9 %middle_scatter.1 = (bf16[512,768]{1,0:T(8,128)(2,1)}, bf16[4016,384]{1,0:T(8,128)(2,1)}) custom-call(bf16[2048,768]{1,0:T(8,128)(2,1)} %get-tuple-element.67.dn_ref, bf16[4,2008,384]{2,1,0:T(8,128)(2,1)} %get-tuple-element.68.de_ref), custom_call_target="tpu_custom_call" | custom-call | tf_op jit(solution)/shard_map/middle_scatter/pallas_call | solution.py:642
  472.3 4.5 multiply_convert_fusion
  486.8 19.6 %attend_back.2 = (bf16[512,384]{1,0:T(8,128)(2,1)}, bf16[2048,384]{1,0:T(8,128)(2,1)}, bf16[2048,384]{1,0:T(8,128)(2,1)}) custom-call(s32[2]{0:T(128)} %pad_add_fusion.limit_ref, s32[1,512]{1,0:T(1,128)} %fusion.64.seen_ref, bf16[384,512]{1,0:T(8,128)(2,1)} %copy.128.qt_ref, bf16[512,384]{1,0:T(8,128)(2,1)} %copy-done.40, bf16[2048,384]{1,0:T(8,128)(2,1)} %copy.129.k_ref, ...), custom_call_target="tpu_custom_call" | custom-call | flops 4026531840 | bytes 10616832 | tf_op jit(solution)/shard_map/attend_back/pallas_call | solution.py:146
  506.4 3.3 fusion.38
  509.8 3.6 add_convert_fusion
  518.9 2.8 pad_maximum_fusion
  526.5 5.4 copy.142
  531.9 9.8 %reshape.193 = f32[2,2008,2,192]{1,0,3,2:T(2,128)} reshape(f32[4016,384]{0,1:T(8,128)} %copy.142) | data formatting | bytes 12337152 | tf_op jit(solution)/shard_map/convert_element_type | solution.py:997
  541.7 11.7 %copy.143 = f32[2,2,2008,192]{2,1,0,3:T(2,128)} copy(f32[2,2,2008,192]{2,0,3,1:T(2,128)} %bitcast.91) | data formatting | bytes 12337152 | tf_op jit(solution)/shard_map/convert_element_type | solution.py:997
  553.4 9.6 %reshape.192 = f32[8032,192]{0,1:T(8,128)} reshape(f32[2,2,2008,192]{2,1,0,3:T(2,128)} %copy.143) | data formatting | bytes 12337152 | tf_op jit(solution)/shard_map/convert_element_type | solution.py:997
  564.3 3.2 fusion.72
  576.5 4.4 copy.140
  586.8 19.8 %attend_back.3 = (bf16[512,384]{1,0:T(8,128)(2,1)}, bf16[2048,384]{1,0:T(8,128)(2,1)}, bf16[2048,384]{1,0:T(8,128)(2,1)}) custom-call(s32[2]{0:T(128)} %pad_add_fusion.limit_ref, s32[1,512]{1,0:T(1,128)} %fusion.64.seen_ref, bf16[384,512]{1,0:T(8,128)(2,1)} %copy.124.qt_ref, bf16[512,384]{1,0:T(8,128)(2,1)} %copy-done.39, bf16[2048,384]{1,0:T(8,128)(2,1)} %copy.125.k_ref, ...), custom_call_target="tpu_custom_call" | custom-call | flops 4026531840 | bytes 10616832 | tf_op jit(solution)/shard_map/attend_back/pallas_call | solution.py:146
  608.9 3.0 convolution_convert_fusion.7
  615.0 4.6 copy.141
  632.1 7.8 %reduce-scatter.3.cloned.1.call-done.f_ref = bf16[192,3072]{1,0:T(8,128)(2,1)} async-done(((bf16[768,3072]{1,0:T(8,128)(2,1)}), bf16[192,3072]{1,0:T(8,128)(2,1)}) %reduce-scatter.3.cloned.1.call-update) | async-done | bytes 1179664 | tf_op jit(solution)/shard_map/reduce_scatter | solution.py:1010
  639.9 100.8 %tail_scatter.1 = (f32[256,768]{1,0:T(8,128)}, f32[192,768]{1,0:T(8,128)}, f32[192,768]{1,0:T(8,128)}, f32[192,1536]{1,0:T(8,128)}, f32[8,768]{1,0:T(8,128)}) custom-call(bf16[2048,768]{1,0:T(8,128)(2,1)} %bitcast.92, bf16[4,192,1536]{2,1,0:T(8,128)(2,1)} %bitcast.93, bf16[4,192,1536]{2,1,0:T(8,128)(2,1)} %bitcast.94, ...), custom_call_target="tpu_custom_call" | custom-call | tf_op jit(solution)/shard_map/tail_scatter/pallas_call | solution.py:761
  (294 shorter events, 116.4 us)
Async XLA Ops:
  7.2 288.7 %all-gather.4.cloned.1.call-start = ((), (), s32[]{:S(2)}) async-start(), calls=%async_computation.4 | async-start | bytes 7710720 | tf_op jit(solution)/shard_map/all_gather | solution.py:890
  9.3 11.6 %copy-start.8 = (bf16[256,768]{1,0:T(8,128)(2,1)S(1)}, bf16[256,768]{1,0:T(8,128)(2,1)}, u32[]{:S(2)}) copy-start(bf16[256,768]{1,0:T(8,128)(2,1)} %x_ref.1) | copy-start | bytes 1179652
  10.2 11.8 %copy-start.44 = (bf16[192,192]{1,0:T(8,128)(2,1)S(1)}, bf16[192,192]{1,0:T(8,128)(2,1)}, u32[]{:S(2)}) copy-start(bf16[192,192]{1,0:T(8,128)(2,1)} %param.30) | copy-start | bytes 221188
  10.2 11.9 %copy-start.45 = (bf16[192,192]{1,0:T(8,128)(2,1)S(1)}, bf16[192,192]{1,0:T(8,128)(2,1)}, u32[]{:S(2)}) copy-start(bf16[192,192]{1,0:T(8,128)(2,1)} %param.35) | copy-start | bytes 221188
  152.8 477.3 %reduce-scatter.5.cloned.1.call-start = ((), (), s32[]{:S(2)}) async-start(), calls=%async_computation.3 | async-start | bytes 3538944 | tf_op jit(solution)/shard_map/reduce_scatter | solution.py:1026
  153.6 4.8 copy-start.14
  157.5 4.6 copy-start.39
  190.9 12.6 %copy-start.69 = (bf16[2048,768]{1,0:T(8,128)(2,1)S(1)}, bf16[2048,768]{1,0:T(8,128)(2,1)}, u32[]{:S(2)}) copy-start(bf16[2048,768]{1,0:T(8,128)(2,1)} %get-tuple-element.59) | copy-start | bytes 9437188
  193.7 21.5 %collective-permute-start = (bf16[512,768]{1,0:T(8,128)(2,1)}, bf16[512,768]{1,0:T(8,128)(2,1)}, u32[]{:S(2)}, u32[]{:S(2)}) collective-permute-start(bf16[512,768]{1,0:T(8,128)(2,1)} %get-tuple-element.211), channel_id=1, source_target_pairs={{0,4},{4,0},{1,5},{5,1},{2,6},{6,2},{3,7},{7,3},{8,12},{12,8},{9,1... | collective-permute-start | bytes 2359304 | tf_op jit(solution)/shard_map/ppermute | solution.py:798
  219.2 16.0 %copy-start.40 = (bf16[512,384]{1,0:T(8,128)(2,1)}, bf16[512,384]{1,0:T(8,128)(2,1)S(1)}, u32[]{:S(2)}) copy-start(bf16[512,384]{1,0:T(8,128)(2,1)S(1)} %fusion.19.q_ref) | copy-start | bytes 1179652
  235.3 4.9 slice-start
  237.2 2.4 collective-permute-start.1
  240.0 242.0 %copy-start.56 = (f32[512]{0:T(512)}, f32[512]{0:T(512)S(1)}, u32[]{:S(2)}) copy-start(f32[512]{0:T(512)S(1)} %get-tuple-element.206) | copy-start | bytes 6148
  246.7 2.6 collective-permute-start.2
  251.4 39.7 %copy-start.62 = (f32[256]{0:T(256)}, f32[256]{0:T(256)S(1)}, u32[]{:S(2)}) copy-start(f32[256]{0:T(256)S(1)} %dynamic-slice.3) | copy-start | bytes 3076
  405.4 63.9 %copy-start.1 = (f32[512,768]{1,0:T(8,128)S(1)}, f32[512,768]{1,0:T(8,128)}, u32[]{:S(2)}) copy-start(f32[512,768]{1,0:T(8,128)} %copy-done) | copy-start | bytes 4718596
  470.9 5.8 slice-start.2
  471.4 10.5 %copy-start.12 = (f32[512,768]{1,0:T(8,128)}, f32[512,768]{1,0:T(8,128)S(1)}, u32[]{:S(2)}) copy-start(f32[512,768]{1,0:T(8,128)S(1)} %subtract_add_fusion.2) | copy-start | bytes 4718596
  472.3 4.5 slice-start.3
  479.1 2.4 collective-permute-start.3
  486.8 19.6 %copy-start.18 = (bf16[768,1536]{1,0:T(8,128)(2,1)S(1)}, bf16[768,1536]{1,0:T(8,128)(2,1)}, u32[]{:S(2)}) copy-start(bf16[768,1536]{1,0:T(8,128)(2,1)} %get-tuple-element.58) | copy-start | bytes 7077892
  513.4 126.4 %reduce-scatter.3.cloned.1.call-start = ((), (), s32[]{:S(2)}) async-start(), calls=%async_computation.2 | async-start | bytes 5898240 | tf_op jit(solution)/shard_map/reduce_scatter | solution.py:1010
  553.4 10.9 %copy-start.31 = (bf16[512,384]{1,0:T(8,128)(2,1)S(1)}, bf16[512,384]{1,0:T(8,128)(2,1)}, u32[]{:S(2)}) copy-start(bf16[512,384]{1,0:T(8,128)(2,1)} %get-tuple-element.72) | copy-start | bytes 1179652
  564.3 3.6 copy-start.4
  564.3 3.6 copy-start.26
  567.5 13.5 %collective-permute-start.4 = (bf16[512,768]{1,0:T(8,128)(2,1)}, bf16[512,768]{1,0:T(8,128)(2,1)}, u32[]{:S(2)}, u32[]{:S(2)}) collective-permute-start(bf16[512,768]{1,0:T(8,128)(2,1)} %get-tuple-element.221), channel_id=1, source_target_pairs={{0,4},{4,0},{1,5},{5,1},{2,6},{6,2},{3,7},{7,3},{8,12},{12,8},{9,1... | collective-permute-start | bytes 2359304 | tf_op jit(solution)/shard_map/ppermute | solution.py:798
  576.5 4.4 copy-start.11
  586.8 19.8 %copy-start.20 = (bf16[2,256,768]{2,1,0:T(8,128)(2,1)S(1)}, bf16[2,256,768]{2,1,0:T(8,128)(2,1)}, u32[]{:S(2)}) copy-start(bf16[2,256,768]{2,1,0:T(8,128)(2,1)} %copy-done.19) | copy-start | bytes 2359300
  615.0 4.6 copy-start.27
  744.0 3.7 copy-start.9
  744.0 3.7 copy-start.21
  744.0 3.7 copy-start.55
  (62 other events, 121.9 us)
Sparse Core Ops, SparseCore 0:
  153.0 80.0 all-gather.3
  513.6 66.8 reduce-scatter.4
  583.4 56.3 reduce-scatter.2

commit v3 on v2

v3 whole, which is shorter than its diff:
```python
from functools import partial

import jax
import jax.numpy as jnp
from jax import lax
from jax.experimental import pallas as pl
from jax.experimental.pallas import tpu as pltpu
from jax.sharding import PartitionSpec as P

HEAD_DIM = 64
EPS = 1e-06
MASKED = -1e30
BF = jnp.bfloat16
F32 = jnp.float32
VMEM_LIMIT = 58 * 2**20


def attend_kernel(limit_ref, seen_ref, q_ref, k_ref, v_ref, o_ref, ot_ref, lse_ref, vt_ref, *, masked, blocks, chunk):
    half = lax.broadcasted_iota(jnp.int32, (2 * HEAD_DIM, 1), 0) // HEAD_DIM
    vt_ref[...] = jnp.transpose(v_ref[...])
    q_t = jnp.transpose(q_ref[...])
    for head in range(2):
        part = slice(head * HEAD_DIM, (head + 1) * HEAD_DIM)
        for index, (first, count) in enumerate(blocks):
            columns = slice(first, first + count)
            qt = jnp.where(half == head, q_t[:, columns], 0).astype(BF)

            def step(i, carry):
                top, total, acc = carry
                start = pl.multiple_of(i * chunk, chunk)
                scores = jnp.dot(k_ref[pl.ds(start, chunk), :], qt, preferred_element_type=F32)
                if masked:
                    key = lax.broadcasted_iota(jnp.int32, (chunk, 1), 0) + start
                    scores = jnp.where(key < seen_ref[:, columns], scores, MASKED)
                new_top = jnp.maximum(top, jnp.max(scores, axis=0, keepdims=True))
                expo = jnp.exp(scores - new_top)
                shrink = jnp.exp(top - new_top)
                total = total * shrink + jnp.sum(expo, axis=0, keepdims=True)
                acc = acc * shrink + jnp.dot(
                    vt_ref[part, pl.ds(start, chunk)], expo.astype(BF), preferred_element_type=F32
                )
                return (new_top, total, acc)

            init = (
                jnp.full((1, count), MASKED, F32),
                jnp.zeros((1, count), F32),
                jnp.zeros((HEAD_DIM, count), F32),
            )
            if masked:
                top, total, acc = lax.fori_loop(0, limit_ref[index], step, init)
            else:
                top, total, acc = lax.fori_loop(0, k_ref.shape[0] // chunk, step, init, unroll=True)
            ot_ref[part, columns] = acc / total
            lse_ref[0, head : head + 1, columns] = top + jnp.log(total)
    o_ref[...] = jnp.transpose(ot_ref[...]).astype(BF)


def attend(limit, seen, query, kv, masked, blocks, chunk):
    rows, width = query.shape
    count = kv.shape[0]
    pair = 2 * HEAD_DIM
    pairs = width // pair
    return pl.pallas_call(
        partial(attend_kernel, masked=masked, blocks=blocks, chunk=chunk),
        grid_spec=pltpu.PrefetchScalarGridSpec(
            num_scalar_prefetch=1,
            grid=(pairs,),
            in_specs=[
                pl.BlockSpec((1, rows), lambda p, lim: (0, 0)),
                pl.BlockSpec((rows, pair), lambda p, lim: (0, p)),
                pl.BlockSpec((count, pair), lambda p, lim: (0, p)),
                pl.BlockSpec((count, pair), lambda p, lim: (0, p + pairs)),
            ],
            out_specs=[
                pl.BlockSpec((rows, pair), lambda p, lim: (0, p)),
                pl.BlockSpec((pair, rows), lambda p, lim: (p, 0)),
                pl.BlockSpec((1, 8, rows), lambda p, lim: (p, 0, 0)),
            ],
            scratch_shapes=[pltpu.VMEM((pair, count), BF)],
        ),
        out_shape=(
            jax.ShapeDtypeStruct((rows, width), BF),
            jax.ShapeDtypeStruct((width, rows), F32),
            jax.ShapeDtypeStruct((pairs, 8, rows), F32),
        ),
        compiler_params=pltpu.CompilerParams(vmem_limit_bytes=VMEM_LIMIT),
        cost_estimate=pl.CostEstimate(
            flops=4 * rows * count * width, transcendentals=rows * count * width // HEAD_DIM,
            bytes_accessed=2 * count * width * 2 + 8 * rows * width,
        ),
        name="attend",
    )(limit, seen, query, kv, kv)


def attend_back_kernel(
    limit_ref, seen_ref, q_ref, k_ref, v_ref, do_ref, ot_ref, lse_ref,
    dq_ref, dk_ref, dv_ref, dk_acc, dv_acc, dqt_acc, kt_ref, *, masked, blocks, chunk,
):
    half = lax.broadcasted_iota(jnp.int32, (2 * HEAD_DIM, 1), 0) // HEAD_DIM
    lane = lax.broadcasted_iota(jnp.int32, (1, 2 * HEAD_DIM), 1) // HEAD_DIM
    kt_ref[...] = jnp.transpose(k_ref[...])
    q_t = jnp.transpose(q_ref[...])
    do_t = jnp.transpose(do_ref[...])
    dk_acc[...] = jnp.zeros_like(dk_acc)
    dv_acc[...] = jnp.zeros_like(dv_acc)
    for head in range(2):
        part = slice(head * HEAD_DIM, (head + 1) * HEAD_DIM)
        for index, (first, count) in enumerate(blocks):
            columns = slice(first, first + count)
            qt = jnp.where(half == head, q_t[:, columns], 0).astype(BF)
            dot_t = jnp.where(half == head, do_t[:, columns], 0).astype(BF)
            q = jnp.where(lane == head, q_ref[columns, :], 0).astype(BF)
            do = jnp.where(lane == head, do_ref[columns, :], 0).astype(BF)
            inner = jnp.sum(
                do_t[part, columns].astype(F32) * ot_ref[part, columns], axis=0, keepdims=True
            )
            lse = lse_ref[0, head : head + 1, columns]

            def step(i, acc):
                start = pl.multiple_of(i * chunk, chunk)
                here = pl.ds(start, chunk)
                scores = jnp.dot(k_ref[here, :], qt, preferred_element_type=F32)
                probs = jnp.exp(scores - lse)
                if masked:
                    key = lax.broadcasted_iota(jnp.int32, (chunk, 1), 0) + start
                    probs = jnp.where(key < seen_ref[:, columns], probs, 0.0)
                grad_probs = jnp.dot(v_ref[here, :], dot_t, preferred_element_type=F32)
                grad_scores = (probs * (grad_probs - inner)).astype(BF)
                dv_acc[here, :] += jnp.dot(probs.astype(BF), do, preferred_element_type=F32)
                dk_acc[here, :] += jnp.dot(grad_scores, q, preferred_element_type=F32)
                return acc + jnp.dot(kt_ref[part, here], grad_scores, preferred_element_type=F32)

            init = jnp.zeros((HEAD_DIM, count), F32)
            if masked:
                acc = lax.fori_loop(0, limit_ref[index], step, init)
            else:
                acc = lax.fori_loop(0, k_ref.shape[0] // chunk, step, init, unroll=True)
            dqt_acc[part, columns] = acc * HEAD_DIM**-0.5
    dq_ref[...] = jnp.transpose(dqt_acc[...]).astype(BF)
    dk_ref[...] = dk_acc[...].astype(BF)
    dv_ref[...] = dv_acc[...].astype(BF)


def attend_back(limit, seen, query, kv, grad, out_t, lse, masked, blocks, chunk):
    rows, width = query.shape
    count = kv.shape[0]
    pair = 2 * HEAD_DIM
    pairs = width // pair
    by_column = pl.BlockSpec((rows, pair), lambda p, lim: (0, p))
    key_spec = pl.BlockSpec((count, pair), lambda p, lim: (0, p))
    return pl.pallas_call(
        partial(attend_back_kernel, masked=masked, blocks=blocks, chunk=chunk),
        grid_spec=pltpu.PrefetchScalarGridSpec(
            num_scalar_prefetch=1,
            grid=(pairs,),
            in_specs=[
                pl.BlockSpec((1, rows), lambda p, lim: (0, 0)),
                by_column,
                key_spec,
                pl.BlockSpec((count, pair), lambda p, lim: (0, p + pairs)),
                by_column,
                pl.BlockSpec((pair, rows), lambda p, lim: (p, 0)),
                pl.BlockSpec((1, 8, rows), lambda p, lim: (p, 0, 0)),
            ],
            out_specs=[by_column, key_spec, key_spec],
            scratch_shapes=[
                pltpu.VMEM((count, pair), F32),
                pltpu.VMEM((count, pair), F32),
                pltpu.VMEM((pair, rows), F32),
                pltpu.VMEM((pair, count), BF),
            ],
        ),
        out_shape=(
            jax.ShapeDtypeStruct((rows, width), BF),
            jax.ShapeDtypeStruct((count, width), BF),
            jax.ShapeDtypeStruct((count, width), BF),
        ),
        compiler_params=pltpu.CompilerParams(vmem_limit_bytes=VMEM_LIMIT),
        cost_estimate=pl.CostEstimate(
            flops=10 * rows * count * width, transcendentals=rows * count * width // HEAD_DIM,
            bytes_accessed=5 * count * width * 2 + 14 * rows * width,
        ),
        name="attend_back",
    )(limit, seen, query, kv, kv, grad, out_t, lse)


def vocab_ids(step, block, vocab):
    row = lax.broadcasted_iota(jnp.int32, (block, 1), 0)
    second = (row >= block // 2).astype(jnp.int32)
    local = row - second * (block // 2) + step * (block // 2)
    valid = local < vocab // 2
    return jnp.where(valid, local + second * (vocab // 2), 2**30), valid


def head_stats_kernel(
    pieces_ref, n_ref, target_ref, stats_ref, emb_ref, expo_ref, tops_ref, nt_ref, run_ref, *, vocab, block, rows, scale
):
    step = pl.program_id(0)
    ids, valid = vocab_ids(step, block, vocab)
    width = pieces_ref.shape[2] // 2
    emb = jnp.concatenate(
        [
            jnp.concatenate(
                [pieces_ref[g, :, p * width : (p + 1) * width] for g in range(pieces_ref.shape[0])], axis=1
            )
            for p in range(2)
        ],
        axis=0,
    )
    emb = jnp.where(valid, emb, 0).astype(BF)
    emb_ref[...] = emb
    total = n_ref.shape[0]

    @pl.when(step == 0)
    def _():
        run_ref[0:1, :] = jnp.full((1, total), MASKED, F32)
        run_ref[1:8, :] = jnp.zeros((7, total), F32)
        for first in range(0, total, rows):
            nt_ref[:, first : first + rows] = jnp.transpose(n_ref[first : first + rows, :])

    for first in range(0, total, rows):
        columns = slice(first, first + rows)
        logits = jnp.dot(emb, nt_ref[:, columns], preferred_element_type=F32) * scale
        logits = jnp.where(valid, logits, MASKED)
        top = run_ref[0:1, columns]
        new_top = jnp.maximum(top, jnp.max(logits, axis=0, keepdims=True))
        expo = jnp.exp(logits - new_top)
        expo_ref[:, columns] = expo.astype(BF)
        run_ref[0:1, columns] = new_top
        run_ref[1:2, columns] = run_ref[1:2, columns] * jnp.exp(top - new_top) + jnp.sum(expo, axis=0, keepdims=True)
        run_ref[2:3, columns] += jnp.sum(jnp.where(ids == target_ref[:, columns], logits, 0.0), axis=0, keepdims=True)
    tops_ref[pl.ds(step, 1), :] = run_ref[0:1, :]

    @pl.when(step == pl.num_programs(0) - 1)
    def _():
        lines = total // 128
        for k in range(3):
            for i in range(lines):
                stats_ref[k * lines + i : k * lines + i + 1, :] = run_ref[k : k + 1, i * 128 : (i + 1) * 128]


def head_stats(pieces, normed, target, block, rows):
    groups, vocab, width = pieces.shape
    vocab *= 2
    total, depth = normed.shape
    steps = pl.cdiv(vocab, block)
    lines = (steps + 7) // 8 * 8
    return pl.pallas_call(
        partial(head_stats_kernel, vocab=vocab, block=block, rows=rows, scale=depth**-0.5),
        grid=(steps,),
        in_specs=[
            pl.BlockSpec((groups, block // 2, width), lambda i: (0, i, 0)),
            pl.BlockSpec((total, depth), lambda i: (0, 0)),
            pl.BlockSpec((1, total), lambda i: (0, 0)),
        ],
        out_specs=[
            pl.BlockSpec((3 * total // 128, 128), lambda i: (0, 0)),
            pl.BlockSpec((block, depth), lambda i: (i, 0)),
            pl.BlockSpec((block, total), lambda i: (i, 0)),
            pl.BlockSpec((lines, total), lambda i: (0, 0)),
        ],
        out_shape=(
            jax.ShapeDtypeStruct((3 * total // 128, 128), F32),
            jax.ShapeDtypeStruct((steps * block, depth), BF),
            jax.ShapeDtypeStruct((steps * block, total), BF),
            jax.ShapeDtypeStruct((lines, total), F32),
        ),
        scratch_shapes=[pltpu.VMEM((depth, total), BF), pltpu.VMEM((8, total), F32)],
        compiler_params=pltpu.CompilerParams(vmem_limit_bytes=VMEM_LIMIT),
        cost_estimate=pl.CostEstimate(
            flops=2 * vocab * depth * total, transcendentals=vocab * total,
            bytes_accessed=4 * vocab * depth + 2 * depth * total + 2 * vocab * total,
        ),
        name="head_stats",
    )(pieces, normed, target)


def head_back_kernel(
    emb_ref, expo_ref, tops_ref, n_ref, target_ref, lse_ref, de_ref, dn_ref, dnt_acc, *, vocab, block, rows, scale
):
    step = pl.program_id(0)
    ids, valid = vocab_ids(step, block, vocab)
    emb_t = jnp.transpose(emb_ref[...])
    factor = jnp.exp(tops_ref[pl.ds(step, 1), :] - lse_ref[...])

    @pl.when(step == 0)
    def _():
        dnt_acc[...] = jnp.zeros_like(dnt_acc)

    de = None
    for first in range(0, n_ref.shape[0], rows):
        columns = slice(first, first + rows)
        probs = expo_ref[:, columns].astype(F32) * factor[:, columns]
        grad = jnp.where(ids == target_ref[:, columns], probs - 1.0, probs).astype(BF)
        term = jnp.dot(grad, n_ref[columns, :], preferred_element_type=F32)
        de = term if de is None else de + term
        dnt_acc[:, columns] += jnp.dot(emb_t, grad, preferred_element_type=F32)
    de = (de * scale).astype(BF)
    width = de_ref.shape[2] // 2
    for g in range(de_ref.shape[0]):
        part = de[:, g * width : (g + 1) * width]
        de_ref[g] = jnp.concatenate([part[: block // 2], part[block // 2 :]], axis=1)

    @pl.when(step == pl.num_programs(0) - 1)
    def _():
        dn_ref[...] = (jnp.transpose(dnt_acc[...]) * scale).astype(BF)


def head_back(emb, expo, tops, normed, target, lse, groups, vocab, block, rows):
    total, depth = normed.shape
    steps = pl.cdiv(vocab, block)
    width = depth // groups
    return pl.pallas_call(
        partial(head_back_kernel, vocab=vocab, block=block, rows=rows, scale=depth**-0.5),
        grid=(steps,),
        in_specs=[
            pl.BlockSpec((block, depth), lambda i: (i, 0)),
            pl.BlockSpec((block, total), lambda i: (i, 0)),
            pl.BlockSpec(tops.shape, lambda i: (0, 0)),
            pl.BlockSpec((total, depth), lambda i: (0, 0)),
            pl.BlockSpec((1, total), lambda i: (0, 0)),
            pl.BlockSpec((1, total), lambda i: (0, 0)),
        ],
        out_specs=[
            pl.BlockSpec((groups, block // 2, 2 * width), lambda i: (0, i, 0)),
            pl.BlockSpec((total, depth), lambda i: (0, 0)),
        ],
        out_shape=(
            jax.ShapeDtypeStruct((groups, steps * block // 2, 2 * width), BF),
            jax.ShapeDtypeStruct((total, depth), BF),
        ),
        scratch_shapes=[pltpu.VMEM((depth, total), F32)],
        compiler_params=pltpu.CompilerParams(vmem_limit_bytes=VMEM_LIMIT),
        cost_estimate=pl.CostEstimate(
            flops=4 * vocab * depth * total, transcendentals=0,
            bytes_accessed=4 * vocab * depth + 6 * depth * total + 2 * vocab * total,
        ),
        name="head_back",
    )(emb, expo, tops, normed, target, lse)


MESH = pl.DeviceIdType.MESH


class Peers:
    def __init__(self):
        self.s, self.c, self.t = (lax.axis_index(name) for name in ("shard", "ctx", "tp"))
        s, c, t = self.s, self.c, self.t
        self.sx = s + 1 - 2 * lax.rem(s, 2)
        self.sy = lax.rem(s + 2, 4)
        self.sd = lax.rem(self.sx + 2, 4)
        self.x = (self.sx, c, t)
        self.y = (self.sy, c, t)
        self.d = (self.sd, c, t)
        self.core = (s, 1 - c, t)
        self.z = [(s, c, lax.rem(t + k, 4)) for k in range(4)]
        self.z_other = [(s, 1 - c, lax.rem(t + k, 4)) for k in range(4)]
        self.group = self.z[1:] + self.z_other


def meet(peers):
    barrier = pltpu.get_barrier_semaphore()
    for peer in peers:
        pl.semaphore_signal(barrier, inc=1, device_id=peer, device_id_type=MESH)
    pl.semaphore_wait(barrier, len(peers))


class Pool:
    def __init__(self, sends, arrivals):
        self.sends, self.arrivals, self.count = sends, arrivals, 0

    def take(self, count):
        first = self.count
        self.count += count
        return first

    def copy(self, index, peer, source, target):
        return pltpu.make_async_remote_copy(
            src_ref=source, dst_ref=target, send_sem=self.sends.at[index],
            recv_sem=self.arrivals.at[index], device_id=peer, device_id_type=MESH,
        )


class Sender:
    def __init__(self, pool):
        self.pool, self.all = pool, []

    def to(self, peer, source, target):
        copy = self.pool.copy(self.pool.take(1), peer, source, target)
        self.all.append(copy)
        copy.start()
        return copy

    def finish(self):
        for copy in self.all:
            copy.wait_send()


class RowLine:
    def __init__(self, pool, me, own, everyone, rows, pieces=2):
        self.pool, self.me, self.own, self.everyone = pool, me, own, everyone
        self.rows, self.pieces, self.sub = rows, pieces, rows // pieces
        self.first = pool.take(13 * pieces)

    def block(self, chip, piece):
        return self.everyone.at[pl.ds((self.me.c * 4 + chip) * self.rows + piece * self.sub, self.sub)]

    def source(self, own, chip, piece):
        return self.own.at[pl.ds(piece * self.sub, self.sub)] if own else self.block(chip, piece)

    def make(self, slot, piece, peer, chip, own=False):
        index = self.first + slot * self.pieces + piece
        return self.pool.copy(index, peer, self.source(own, chip, piece), self.block(chip, piece))

    def right(self, k, piece):
        return self.make(k, piece, self.me.z[1], self.me.t - k, k == 0)

    def left(self, k, piece):
        return self.make(3 + k, piece, self.me.z[3], self.me.t + k, k == 0)

    def across(self, slot, piece, chip, own=False):
        return self.make(6 + slot, piece, self.me.core, chip, own)

    def begin(self):
        t = self.me.t
        for p in range(self.pieces):
            pl.when(t < 3)(lambda: self.right(0, p).start())
            pl.when(t > 0)(lambda: self.left(0, p).start())
        for p in range(self.pieces):
            self.across(0, p, t, True).start()

    def step(self, k):
        t = self.me.t
        for p in range(self.pieces):

            @pl.when(t > k)
            def _():
                chip = t - 1 - k
                self.make(k, p, self.me.z[1], chip).wait_recv()
                if k < 2:
                    pl.when(t < 3)(lambda: self.right(k + 1, p).start())
                self.across(1 + k, p, chip).start()

            @pl.when(t + k < 3)
            def _():
                chip = t + 1 + k
                self.make(3 + k, p, self.me.z[3], chip).wait_recv()
                if k < 2:
                    pl.when(t > 0)(lambda: self.left(k + 1, p).start())
                self.across(4 + k, p, chip).start()

    def finish(self):
        t = self.me.t
        for p in range(self.pieces):
            pl.when(t < 3)(lambda: self.right(0, p).wait_send())
            pl.when(t > 0)(lambda: self.left(0, p).wait_send())
            self.across(0, p, t, True).wait()
            for k in range(3):

                @pl.when(t > k)
                def _():
                    if k < 2:
                        pl.when(t < 3)(lambda: self.right(k + 1, p).wait_send())
                    self.across(1 + k, p, t - 1 - k).wait()

                @pl.when(t + k < 3)
                def _():
                    if k < 2:
                        pl.when(t > 0)(lambda: self.left(k + 1, p).wait_send())
                    self.across(4 + k, p, t + 1 + k).wait()


class BlockLine:
    def __init__(self, pool, me, own, take):
        self.pool, self.me, self.own, self.take = pool, me, own, take
        self.first = pool.take(4)
        self.where = [(me.c + 1, 1 - me.c), (3 * me.c, me.c)]

    def right(self, i):
        here = self.take.at[self.where[i][1]]
        return self.pool.copy(self.first + i, self.me.z[1], here, here)

    def left(self, i):
        here = self.take.at[self.where[i][1]]
        return self.pool.copy(self.first + 2 + i, self.me.z[3], here, here)

    def begin(self):
        t = self.me.t
        for i, (block, slot) in enumerate(self.where):

            @pl.when(t == block)
            def _():
                self.take[slot] = self.own[...]
                pl.when(t < 3)(lambda: self.right(i).start())
                pl.when(t > 0)(lambda: self.left(i).start())

    def arrive(self, distance):
        t = self.me.t
        for i, (block, slot) in enumerate(self.where):

            @pl.when(t - block == distance)
            def _():
                self.right(i).wait_recv()
                pl.when(t < 3)(lambda: self.right(i).start())

            @pl.when(block - t == distance)
            def _():
                self.left(i).wait_recv()
                pl.when(t > 0)(lambda: self.left(i).start())

    def finish(self):
        t = self.me.t
        for i, (block, slot) in enumerate(self.where):
            pl.when((t >= block) & (t < 3))(lambda: self.right(i).wait_send())
            pl.when((t <= block) & (t > 0))(lambda: self.left(i).wait_send())


class SumLine:
    def __init__(self, pool, me, own, coming, going, pieces=2):
        self.pool, self.me, self.own, self.coming, self.going = pool, me, own, coming, going
        self.pieces, self.sub = pieces, own.shape[1] // pieces
        self.first = pool.take(6 * pieces)

    def copy(self, slot, piece, source):
        here = pl.ds(piece * self.sub, self.sub)
        peer = self.me.z[1] if slot < 3 else self.me.z[3]
        return self.pool.copy(
            self.first + slot * self.pieces + piece, peer, source.at[here], self.coming.at[slot, here]
        )

    def dest(self, slot):
        return 3 - slot if slot < 3 else slot - 3

    def direct(self, slot):
        return self.me.t == (0 if slot < 3 else 3)

    def start(self):
        for slot in (0, 3, 1, 4, 2, 5):

            @pl.when(self.direct(slot))
            def _():
                for p in range(self.pieces):
                    self.copy(slot, p, self.own.at[self.dest(slot)]).start()

    passing = ((0, 1), (3, 2), (1, 1), (4, 2), (0, 2), (3, 1))

    def add(self, part):
        for slot, chip in self.passing[2 * part : 2 * part + 2]:

            @pl.when(self.me.t == chip)
            def _():
                for p in range(self.pieces):
                    here = pl.ds(p * self.sub, self.sub)
                    self.copy(slot, p, self.going.at[slot]).wait_recv()
                    self.going[slot, here] = (
                        self.own[self.dest(slot), here].astype(F32) + self.coming[slot, here].astype(F32)
                    ).astype(BF)
                    self.copy(slot, p, self.going.at[slot]).start()

    def result(self, out):
        t = self.me.t
        for slot in range(6):

            @pl.when(t == self.dest(slot))
            def _():
                for p in range(self.pieces):
                    self.copy(slot, p, self.going.at[slot]).wait_recv()

        out[...] = self.own[t].astype(F32)

        @pl.when(t > 0)
        def _():
            out[...] += self.coming[3 - t].astype(F32)

        @pl.when(t < 3)
        def _():
            out[...] += self.coming[3 + t].astype(F32)

    def finish(self):
        for slot in range(6):

            @pl.when(self.direct(slot))
            def _():
                for p in range(self.pieces):
                    self.copy(slot, p, self.own.at[self.dest(slot)]).wait_send()

        for slot, chip in self.passing:

            @pl.when(self.me.t == chip)
            def _():
                for p in range(self.pieces):
                    self.copy(slot, p, self.going.at[slot]).wait_send()


class GradLine:
    def __init__(self, pool, me, own, coming, going, shared):
        self.pool, self.me, self.own, self.coming, self.going, self.shared = pool, me, own, coming, going, shared
        self.first = pool.take(5)
        self.home = me.c == me.t // 2

    def copy(self, slot, source):
        peer = self.me.z[1] if slot < 2 else self.me.z[3]
        return self.pool.copy(self.first + slot, peer, source, self.coming.at[slot])

    def index(self, slot):
        return (1, 0, 0, 1)[slot]

    def block(self, slot):
        return 2 * self.me.c + self.index(slot)

    def direct(self, slot):
        t = self.me.t
        return (t == 0) & (self.block(slot) > 0) if slot < 2 else (t == 3) & (self.block(slot) < 3)

    def start(self):
        for slot in (0, 2, 1, 3):
            pl.when(self.direct(slot))(lambda: self.copy(slot, self.own.at[self.index(slot)]).start())

    passing = ((0, 1), (2, 2), (1, 1), (3, 2), (0, 2), (2, 1))

    def adds(self, slot, chip):
        return (self.me.t == chip) & ((chip < self.block(slot)) if slot < 2 else (chip > self.block(slot)))

    def add(self, part):
        for slot, chip in self.passing[2 * part : 2 * part + 2]:

            @pl.when(self.adds(slot, chip))
            def _():
                self.copy(slot, self.going.at[slot]).wait_recv()
                self.going[slot] = (
                    self.own[self.index(slot)].astype(F32) + self.coming[slot].astype(F32)
                ).astype(BF)
                self.copy(slot, self.going.at[slot]).start()

    def share(self):
        return self.pool.copy(self.first + 4, self.me.core, self.shared, self.shared)

    def settle(self, total):
        t = self.me.t

        for slot in range(4):
            ends = (t == self.block(slot)) & (t > 0 if slot < 2 else t < 3)
            pl.when(ends)(lambda: self.copy(slot, self.going.at[slot]).wait_recv())

        @pl.when(self.home)
        def _():
            j = lax.rem(t, 2)
            total[...] = self.own[j].astype(F32)

            @pl.when(t > 0)
            def _():
                total[...] += self.coming[1 - j].astype(F32)

            @pl.when(t < 3)
            def _():
                total[...] += self.coming[2 + j].astype(F32)

            self.shared[...] = total[...].astype(BF)
            self.share().start()

    def finish(self, out):
        for slot in range(4):
            pl.when(self.direct(slot))(lambda: self.copy(slot, self.own.at[self.index(slot)]).wait_send())
        for slot, chip in self.passing:
            pl.when(self.adds(slot, chip))(lambda: self.copy(slot, self.going.at[slot]).wait_send())
        pl.when(self.home)(lambda: self.share().wait_send())
        pl.when(jnp.logical_not(self.home))(lambda: self.share().wait_recv())
        out[...] = self.shared[...].astype(F32)


def start_kernel(
    gains_ref, x_ref, e_ref, g_ref, t_ref, emb_ref, b0, b1, b2,
    gains_out, n_all, e_all, n_pair, x_pair, g_pair, t_pair, emb_all, w0, w1, mix2,
    gain_slots, n_ref, take0, take1, take2, mix0, mix1, sends, arrivals, local, *, cuts,
):
    me = Peers()
    meet([me.z[1], me.z[3], me.core, me.x, me.y, me.d])
    pool = Pool(sends, arrivals)
    send = Sender(pool)
    rows = x_ref.shape[0]
    locals_ = []

    def copy_here(source, target):
        copy = pltpu.make_async_copy(source, target, local.at[len(locals_)])
        copy.start()
        locals_.append(copy)

    emb_rows = emb_ref.shape[0]
    emb_half = emb_rows // 16 * 8
    copy_here(emb_ref, emb_all.at[me.s])
    emb_x = send.to(me.x, emb_ref, emb_all.at[me.s])
    emb_y = send.to(me.y, emb_ref, emb_all.at[me.s])
    gain_slots[me.s] = gains_ref[...]
    gain_copies = [send.to(peer, gains_ref, gain_slots.at[me.s]) for peer in (me.x, me.y, me.d)]
    bundles = [(b0, take0, mix0), (b1, take1, mix1), (b2, take2, mix2)]
    lines = [BlockLine(pool, me, block, take) for block, take, mix in bundles]

    def interleave(i):
        block, take, mix = bundles[i]
        first = take[0]
        second = take[1]
        columns = []
        for start, stop in cuts[i]:
            columns += [first[:, start:stop], second[:, start:stop]]
        mix[...] = jnp.concatenate(columns, axis=1)

    depth = b0.shape[0]
    half = depth // 2
    mine = pl.ds(me.s * depth, depth)

    def share(i, w):
        mix = bundles[i][2]
        copy_here(mix, w.at[mine])
        return send.to(me.x, mix, w.at[mine]), send.to(me.y, mix, w.at[mine])

    onward = []

    def pass_on(to_x, to_y, x_part, y_part):
        to_x.wait_recv()
        onward.append(send.to(me.y, x_part, x_part))
        to_y.wait_recv()
        onward.append(send.to(me.x, y_part, y_part))

    def pass_weights(over, w):
        pass_on(*over, w.at[pl.ds(me.sx * depth, half)], w.at[pl.ds(me.sy * depth + half, half)])

    lines[0].begin()
    lines[1].begin()
    for copy in gain_copies:
        copy.wait_recv()
    width = x_ref.shape[1] // 4
    gains = jnp.concatenate([gain_slots[i][:, :width] for i in range(4)], axis=1)
    gains_out[...] = gains
    n_ref[...] = normalize(x_ref[...].astype(F32), gains[0:1])[0].astype(BF)
    n_line = RowLine(pool, me, n_ref, n_all, rows)
    e_line = RowLine(pool, me, e_ref, e_all, rows)
    n_line.begin()
    copy_here(n_ref, n_all.at[pl.ds((me.c * 4 + me.t) * rows, rows)])
    copy_here(e_ref, e_all.at[pl.ds((me.c * 4 + me.t) * rows, rows)])
    swapped = []
    for ref, pair in ((n_ref, n_pair), (x_ref, x_pair), (g_ref, g_pair), (t_ref, t_pair)):
        where = pair.at[pl.ds(me.c * ref.shape[0], ref.shape[0])]
        swapped.append(send.to(me.core, ref, where))
        copy_here(ref, where)
    lines[0].arrive(1)
    lines[1].arrive(1)
    lines[0].arrive(2)
    lines[1].arrive(2)
    n_line.step(0)
    lines[0].arrive(3)
    interleave(0)
    over0 = share(0, w0)
    lines[1].arrive(3)
    interleave(1)
    over1 = share(1, w1)
    lines[2].begin()
    e_line.begin()
    n_line.step(1)
    n_line.step(2)
    lines[2].arrive(1)
    e_line.step(0)
    pass_on(
        emb_x, emb_y, emb_all.at[me.sx, pl.ds(0, emb_half)],
        emb_all.at[me.sy, pl.ds(emb_half, emb_rows - emb_half)],
    )
    pass_weights(over0, w0)
    lines[2].arrive(2)
    e_line.step(1)
    pass_weights(over1, w1)
    lines[2].arrive(3)
    e_line.step(2)
    interleave(2)
    for copy in onward + swapped:
        copy.wait_recv()
    for line in lines + [n_line, e_line]:
        line.finish()
    send.finish()
    for copy in locals_:
        copy.wait()


def start_gather(gains, inputs, encoder, cotangent, targets, emb, bundles, cuts):
    rows, depth = inputs.shape
    part = bundles[0].shape[0]
    any_space = pl.BlockSpec(memory_space=pl.ANY)
    vmem = pl.BlockSpec(memory_space=pltpu.VMEM)
    return pl.pallas_call(
        partial(start_kernel, cuts=cuts),
        in_specs=[vmem] * 5 + [any_space] + [vmem] * 3,
        out_specs=[vmem] + [any_space] * 9 + [vmem],
        out_shape=[
            jax.ShapeDtypeStruct((gains.shape[0], depth), F32),
            jax.ShapeDtypeStruct((8 * rows, depth), BF),
            jax.ShapeDtypeStruct((8 * rows, depth), BF),
        ]
        + [jax.ShapeDtypeStruct((2 * a.shape[0], a.shape[1]), a.dtype) for a in (inputs, inputs, cotangent, targets)]
        + [jax.ShapeDtypeStruct((4,) + emb.shape, BF)]
        + [jax.ShapeDtypeStruct((4 * part, 2 * b.shape[1]), BF) for b in bundles[:2]]
        + [jax.ShapeDtypeStruct((part, 2 * bundles[2].shape[1]), BF)],
        scratch_shapes=[pltpu.VMEM((4,) + gains.shape, F32), pltpu.VMEM((rows, depth), BF)]
        + [pltpu.VMEM((2,) + b.shape, BF) for b in bundles]
        + [pltpu.VMEM((part, 2 * b.shape[1]), BF) for b in bundles[:2]]
        + [pltpu.SemaphoreType.DMA((96,)), pltpu.SemaphoreType.DMA((96,)), pltpu.SemaphoreType.DMA((16,))],
        compiler_params=pltpu.CompilerParams(collective_id=0, has_side_effects=True, vmem_limit_bytes=VMEM_LIMIT),
        name="start_gather",
    )(gains, inputs, encoder, cotangent, targets, emb, *bundles)


def rows_kernel(n_ref, n_all, sends, arrivals, local):
    me = Peers()
    meet([me.z[1], me.z[3], me.core])
    rows = n_ref.shape[0]
    copy = pltpu.make_async_copy(n_ref, n_all.at[pl.ds((me.c * 4 + me.t) * rows, rows)], local)
    copy.start()
    line = RowLine(Pool(sends, arrivals), me, n_ref, n_all, rows)
    line.begin()
    for k in range(3):
        line.step(k)
    line.finish()
    copy.wait()


def gather_rows(normed):
    rows, depth = normed.shape
    return pl.pallas_call(
        rows_kernel,
        in_specs=[pl.BlockSpec(memory_space=pltpu.VMEM)],
        out_specs=pl.BlockSpec(memory_space=pl.ANY),
        out_shape=jax.ShapeDtypeStruct((8 * rows, depth), normed.dtype),
        scratch_shapes=[pltpu.SemaphoreType.DMA((26,)), pltpu.SemaphoreType.DMA((26,)), pltpu.SemaphoreType.DMA],
        compiler_params=pltpu.CompilerParams(collective_id=1, has_side_effects=True, vmem_limit_bytes=VMEM_LIMIT),
        name="gather_rows",
    )(normed)


def stats_kernel(stats_ref, out_ref, slots, sends, arrivals):
    me = Peers()
    meet(me.group)
    send = Sender(Pool(sends, arrivals))
    here = slots.at[me.c * 4 + me.t]
    slots[me.c * 4 + me.t] = stats_ref[...]
    copies = [send.to(peer, stats_ref, here) for peer in me.group]
    for copy in copies:
        copy.wait_recv()
    lines = stats_ref.shape[0] // 3
    top = slots[0, 0:lines]
    for i in range(1, 8):
        top = jnp.maximum(top, slots[i, 0:lines])
    total = jnp.zeros_like(top)
    picked = jnp.zeros_like(top)
    for i in range(8):
        total += slots[i, lines : 2 * lines] * jnp.exp(slots[i, 0:lines] - top)
        picked += slots[i, 2 * lines : 3 * lines]
    logsum = top + jnp.log(total)
    out_ref[0] = logsum
    out_ref[1] = logsum - picked
    send.finish()


def combine_stats(stats):
    return pl.pallas_call(
        stats_kernel,
        in_specs=[pl.BlockSpec(memory_space=pltpu.VMEM)],
        out_specs=pl.BlockSpec(memory_space=pltpu.VMEM),
        out_shape=jax.ShapeDtypeStruct((2, stats.shape[0] // 3, stats.shape[1]), F32),
        scratch_shapes=[pltpu.VMEM((8,) + stats.shape, F32), pltpu.SemaphoreType.DMA((8,)), pltpu.SemaphoreType.DMA((8,))],
        compiler_params=pltpu.CompilerParams(collective_id=2, has_side_effects=True),
        name="combine_stats",
    )(stats)


def settle_first(send, me, part_ref, other, half):
    return send.to(me.core, part_ref.at[pl.ds((1 - me.c) * half, half)], other)


def settle_second(me, part_ref, other, summed, rows):
    half = 4 * rows
    for k in range(4):
        summed[k] = (
            part_ref[pl.ds(me.c * half + k * rows, rows)].astype(F32) + other[k * rows : (k + 1) * rows].astype(F32)
        ).astype(BF)


class Planar:
    def __init__(self, send, me, part, first, second, moving, chunks):
        self.send, self.me, self.part = send, me, part
        self.first, self.second, self.moving, self.chunks = first, second, moving, chunks

    def begin(self):
        me = self.me
        self.one = []
        for start, stop, along_x in self.chunks:
            here = slice(start, stop)
            near, near_block = (me.x, me.sx) if along_x else (me.y, me.sy)
            self.one.append(
                (
                    self.send.to(near, self.part.at[me.sd, here], self.first.at[1, here]),
                    self.send.to(near, self.part.at[near_block, here], self.first.at[0, here]),
                )
            )

    def gather(self, i):
        me = self.me
        start, stop, along_x = self.chunks[i]
        here = slice(start, stop)
        self.one[i][0].wait_recv()
        self.moving[here] = (
            self.part[me.sy if along_x else me.sx, here].astype(F32) + self.first[1, here].astype(F32)
        ).astype(BF)
        return here

    def own(self, i):
        start, stop, along_x = self.chunks[i]
        here = slice(start, stop)
        self.one[i][1].wait_recv()
        return self.part[self.me.s, here].astype(F32) + self.first[0, here].astype(F32)

    def go_on(self):
        self.two = []
        for start, stop, along_x in self.chunks:
            here = slice(start, stop)
            self.two.append(
                self.send.to(self.me.y if along_x else self.me.x, self.moving.at[here], self.second.at[here])
            )

    def middle(self):
        for i in range(len(self.chunks)):
            self.gather(i)
        self.go_on()

    def end(self, store):
        for i, copy in enumerate(self.two):
            start, stop, along_x = self.chunks[i]
            here = slice(start, stop)
            copy.wait_recv()
            store(here, self.own(i) + self.second[here].astype(F32))


def halves(count, parts, step):
    middle = (count // 2 + step - 1) // step * step
    out = []
    for low, high, along_x in ((0, middle, True), (middle, count, False)):
        size = ((high - low) // parts + step - 1) // step * step
        edges = list(range(low, high, size)) + [high]
        out.append([(a, b, along_x) for a, b in zip(edges[:-1], edges[1:])])
    return [chunk for pair in zip(*out) for chunk in pair]


def middle_kernel(dn_ref, de_ref, gn_ref, own_ref, move_ref, other, summed, coming, going, total, first, sends, arrivals, *, chunks):
    me = Peers()
    meet([me.z[1], me.z[3], me.core, me.x, me.y])
    pool = Pool(sends, arrivals)
    send = Sender(pool)
    rows = summed.shape[1]
    crossing = settle_first(send, me, dn_ref, other, 4 * rows)
    plane = Planar(send, me, de_ref, first, None, move_ref, chunks)
    plane.begin()
    crossing.wait_recv()
    settle_second(me, dn_ref, other, summed, rows)
    line = SumLine(pool, me, summed, coming, going)
    line.start()
    for part in range(3):
        line.add(part)
    line.result(total)
    own = pl.ds(me.c * rows, rows)
    gn_ref[own] = total[...].astype(BF)
    share = send.to(me.core, gn_ref.at[own], gn_ref.at[own])
    for i in range(len(chunks)):
        here = plane.gather(i)
        own_ref[here] = plane.own(i).astype(BF)
    share.wait_recv()
    line.finish()
    send.finish()


def middle_scatter(dn, de, vocab):
    total, depth = dn.shape
    rows = total // 8
    width = de.shape[2]
    chunks = halves(vocab, 3, 16)
    count = 2 + 12 + 2 * len(chunks)
    vmem = pl.BlockSpec(memory_space=pltpu.VMEM)
    return pl.pallas_call(
        partial(middle_kernel, chunks=chunks),
        in_specs=[vmem] * 2,
        out_specs=[vmem] * 3,
        out_shape=[
            jax.ShapeDtypeStruct((2 * rows, depth), BF),
            jax.ShapeDtypeStruct((vocab, width), BF),
            jax.ShapeDtypeStruct((vocab, width), BF),
        ],
        scratch_shapes=[
            pltpu.VMEM((4 * rows, depth), BF),
            pltpu.VMEM((4, rows, depth), BF),
            pltpu.VMEM((6, rows, depth), BF),
            pltpu.VMEM((6, rows, depth), BF),
            pltpu.VMEM((rows, depth), F32),
            pltpu.VMEM((2, vocab, width), BF),
            pltpu.SemaphoreType.DMA((count,)),
            pltpu.SemaphoreType.DMA((count,)),
        ],
        compiler_params=pltpu.CompilerParams(collective_id=3, has_side_effects=True, vmem_limit_bytes=VMEM_LIMIT),
        name="middle_scatter",
    )(dn, de)


def tail_kernel(
    dn_ref, c0, c1, c2, c3, s0, s1, s2, s3, f_ref, gains_ref, eo_ref, em_ref,
    dn_out, o0, o1, o2, gain_out, eg_out,
    g0, g1, e_second, e_sum, other, summed, coming, going, first0, second0, moving0, first1, second1, moving1,
    ab0, ab1, ab2, in0, in1, in2, out0, out1, out2, held0, held1, held2,
    slots, plane_sum, plane_slots, sends, arrivals, *, cuts, chunks,
):
    me = Peers()
    meet(me.group + [me.x, me.y, me.d])
    pool = Pool(sends, arrivals)
    send = Sender(pool)
    rows = summed.shape[1]
    crossing = settle_first(send, me, dn_ref, other, 4 * rows)
    for i, piece in enumerate((c0, c1, c2, c3)):
        g0[:, :, i * piece.shape[2] : (i + 1) * piece.shape[2]] = piece[...]
    for i, piece in enumerate((s0, s1, s2, s3)):
        g1[:, :, i * piece.shape[2] : (i + 1) * piece.shape[2]] = piece[...]
    planes = [
        Planar(send, me, g0, first0, second0, moving0, chunks),
        Planar(send, me, g1, first1, second1, moving1, chunks),
    ]
    planes[0].begin()
    planes[1].begin()
    slots[me.c * 4 + me.t] = gains_ref[...]
    gain_copies = [send.to(peer, gains_ref, slots.at[me.c * 4 + me.t]) for peer in me.group]

    def split(value, cut):
        return [
            jnp.concatenate([value[:, 2 * a + i * (b - a) : 2 * a + (i + 1) * (b - a)] for a, b in cut], axis=1).astype(BF)
            for i in range(2)
        ]

    ff_line = GradLine(pool, me, ab2, in2, out2, held2)
    lines = [GradLine(pool, me, ab0, in0, out0, held0), GradLine(pool, me, ab1, in1, out1, held1)]
    for i, half in enumerate(split(f_ref[...], cuts[2])):
        ab2[i] = half
    crossing.wait_recv()
    settle_second(me, dn_ref, other, summed, rows)
    row_line = SumLine(pool, me, summed, coming, going)
    ff_line.start()
    row_line.start()
    for part in range(3):
        ff_line.add(part)
        row_line.add(part)
    planes[0].middle()
    planes[1].middle()
    vocab, wide = eo_ref.shape
    e_half = halves(vocab, 1, 16)
    e_copies = [
        send.to(me.y if along_x else me.x, em_ref.at[start:stop], e_second.at[start:stop])
        for start, stop, along_x in e_half
    ]
    for copy in gain_copies:
        copy.wait_recv()
    total = slots[0]
    for i in range(1, 8):
        total += slots[i]
    plane_sum[...] = total
    plane_slots[me.s] = total
    plane_copies = [send.to(peer, plane_sum, plane_slots.at[me.s]) for peer in (me.x, me.y, me.d)]
    for plane, cut, ab, line in ((planes[0], cuts[0], ab0, lines[0]), (planes[1], cuts[1], ab1, lines[1])):

        def store(here, value):
            for i, half in enumerate(split(value, cut)):
                ab[i, here] = half

        plane.end(store)
        line.start()
    for part in range(3):
        lines[0].add(part)
        lines[1].add(part)
    row_line.result(dn_out)
    ff_line.settle(o2)
    for copy in e_copies:
        copy.wait_recv()
    e_sum[me.c] = (eo_ref[...].astype(F32) + e_second[...].astype(F32)).astype(BF)
    e_share = send.to(me.core, e_sum.at[me.c], e_sum.at[me.c])
    for copy in plane_copies:
        copy.wait_recv()
    gain_out[...] = plane_slots[0] + plane_slots[1] + plane_slots[2] + plane_slots[3]
    lines[0].settle(o0)
    e_share.wait_recv()
    for c in range(2):
        for p in range(2):
            first_row = (2 * c + p) * vocab
            eg_out[first_row : first_row + vocab, :] = e_sum[c, :, p * wide // 2 : (p + 1) * wide // 2]
    lines[1].settle(o1)
    for line, out in ((ff_line, o2), (lines[0], o0), (lines[1], o1)):
        line.finish(out)
    row_line.finish()
    send.finish()


def tail_scatter(dn, grads, ff, gains, emb_own, emb_move, cuts):
    total, depth = dn.shape
    rows = total // 8
    groups, part, width = grads[0][0].shape
    width *= 4
    chunks = halves(part, 1, 16)
    vmem = pl.BlockSpec(memory_space=pltpu.VMEM)
    widths = [width // 2, width // 2, ff.shape[1] // 2]
    scratch = [
        pltpu.VMEM((groups, part, width), BF),
        pltpu.VMEM((groups, part, width), BF),
        pltpu.VMEM(emb_own.shape, BF),
        pltpu.VMEM((2,) + emb_own.shape, BF),
        pltpu.VMEM((4 * rows, depth), BF),
        pltpu.VMEM((4, rows, depth), BF),
        pltpu.VMEM((6, rows, depth), BF),
        pltpu.VMEM((6, rows, depth), BF),
    ]
    for _ in grads:
        scratch += [pltpu.VMEM((2, part, width), BF), pltpu.VMEM((part, width), BF), pltpu.VMEM((part, width), BF)]
    for count in (2, 4, 4):
        scratch += [pltpu.VMEM((count, part, w), BF) for w in widths]
    scratch += [pltpu.VMEM((part, w), BF) for w in widths]
    scratch += [
        pltpu.VMEM((8,) + gains.shape, F32),
        pltpu.VMEM(gains.shape, F32),
        pltpu.VMEM((4,) + gains.shape, F32),
        pltpu.SemaphoreType.DMA((64,)),
        pltpu.SemaphoreType.DMA((64,)),
    ]
    return pl.pallas_call(
        partial(tail_kernel, cuts=cuts, chunks=chunks),
        in_specs=[vmem] * 13,
        out_specs=[vmem] * 6,
        out_shape=[jax.ShapeDtypeStruct((rows, depth), F32)]
        + [jax.ShapeDtypeStruct((part, w), F32) for w in widths]
        + [jax.ShapeDtypeStruct(gains.shape, F32)]
        + [jax.ShapeDtypeStruct((4 * emb_own.shape[0], emb_own.shape[1] // 2), BF)],
        scratch_shapes=scratch,
        compiler_params=pltpu.CompilerParams(collective_id=4, has_side_effects=True, vmem_limit_bytes=VMEM_LIMIT),
        name="tail_scatter",
    )(dn, *grads[0], *grads[1], ff, gains, emb_own, emb_move)


def normalize(hidden, gain):
    inverse = lax.rsqrt(jnp.mean(hidden * hidden, axis=-1, keepdims=True) + EPS)
    return (hidden * inverse * gain, inverse)


def norm_back(hidden, inverse, gain, upstream):
    scaled = upstream * gain
    inner = jnp.mean(scaled * hidden, axis=-1, keepdims=True)
    return inverse * scaled - hidden * (inverse * inverse * inverse) * inner


def matmul(left, right):
    return jnp.dot(left, right, preferred_element_type=F32)


def left_t(left, right):
    return jnp.einsum("ra,rb->ab", left, right, preferred_element_type=F32)


def right_t(left, right):
    return jnp.einsum("ra,ba->rb", left, right, preferred_element_type=F32)


def swap(array):
    return lax.ppermute(array, "ctx", [(0, 1), (1, 0)])


def per_device(
    inputs, encoder, prefix, targets, cotangent, gain_self, query_self, key_self, value_self, output_self,
    gain_cross, query_cross, key_cross, value_cross, output_cross, gain_hidden, gate_weight, up_weight,
    down_weight, gain_exit, embedding,
):
    tp = lax.axis_size("tp")
    ctx = lax.axis_size("ctx")
    shards = lax.axis_size("shard")
    assert tp == 4 and ctx == 2
    core = lax.axis_index("ctx")
    place = lax.axis_index("tp")
    rows, depth = inputs.shape
    group = rows * tp
    total = group * ctx
    hb = query_self.shape[1]
    width = 2 * hb
    fb = gate_weight.shape[1]
    pair = rows * ctx

    route_a = []
    route_b = []
    for c in range(2):
        for z in range(4):
            dest = c * 4 + z
            route_a.append(((z % 2) * 4 + 2 * c + z // 2, dest))
            route_b.append(((z % 2) * 4 + 2 * c + 1 - z // 2, dest))
    both = ("ctx", "tp")

    def spread_weights(parts):
        block = jnp.concatenate(parts, axis=1)
        first = lax.ppermute(block, both, route_a)
        second = lax.ppermute(block, both, route_b)
        columns = []
        start = 0
        for piece in parts:
            stop = start + piece.shape[1]
            columns += [first[:, start:stop], second[:, start:stop]]
            start = stop
        return lax.all_gather(jnp.concatenate(columns, axis=1), "shard", axis=0, tiled=True)

    def collect_weights(grad, widths):
        mine = lax.psum_scatter(grad, "shard", scatter_dimension=0, tiled=True)
        first = []
        second = []
        start = 0
        for size in widths:
            first.append(mine[:, start : start + size])
            second.append(mine[:, start + size : start + 2 * size])
            start += 2 * size
        back = lambda route: [(dest, source) for source, dest in route]
        one = lax.ppermute(jnp.concatenate(first, axis=1), both, back(route_a))
        two = lax.ppermute(jnp.concatenate(second, axis=1), both, back(route_b))
        part = (one.astype(F32) + two.astype(F32)).astype(BF)
        whole = part.astype(F32) + swap(part).astype(F32)
        outs = []
        start = 0
        for size in widths:
            outs.append(whole[:, start : start + size])
            start += size
        return outs

    def couple(own, other):
        return jnp.where(
            core == 0, jnp.concatenate([own, other], axis=0), jnp.concatenate([other, own], axis=0)
        )

    fast = shards == 4
    own_f = inputs.astype(F32)
    parts_self = [query_self, key_self, value_self, output_self.T]
    parts_cross = [query_cross, key_cross, value_cross, output_cross.T]
    parts_ff = [gate_weight, up_weight, down_weight.T]
    gain_parts = jnp.stack([gain_self, gain_cross, gain_hidden, gain_exit])
    cuts = [[(i * w, (i + 1) * w) for i in range(n)] for n, w in ((4, hb), (4, hb), (3, fb))]
    vocab_half = embedding.shape[0] // ctx
    emb_mine = lax.dynamic_slice_in_dim(embedding, core * vocab_half, vocab_half, axis=0)
    emb_mine = jnp.concatenate([emb_mine[: vocab_half // 2], emb_mine[vocab_half // 2 :]], axis=1)

    def take_pair(array):
        cut = array.reshape(ctx, group, depth)
        return lax.dynamic_slice_in_dim(cut, place * rows, rows, axis=1).reshape(pair, depth)

    if fast:
        bundles = [jnp.concatenate(parts, axis=1) for parts in (parts_self, parts_cross, parts_ff)]
        spare = -(depth // shards) % 128
        gain_block = jnp.pad(gain_parts.astype(F32), ((0, 4), (0, spare)))
        (
            gains, normed1, encoder_all, normed1_pair, x_pair, g_pair, t_pair, emb_pieces, weights_self, weights_cross,
            ff_mix,
        ) = start_gather(
            gain_block, inputs, encoder, cotangent, targets.reshape(8, group // 8), emb_mine, bundles, cuts
        )
        hidden0 = x_pair.astype(F32)
        cotangent_pair = g_pair.astype(F32)
        targets_all = t_pair.reshape(total)
        weights_ff = lax.all_gather(ff_mix, "shard", axis=0, tiled=True)
    else:
        gains = lax.all_gather(gain_parts, "shard", axis=1, tiled=True).astype(F32)
        normed1_own = normalize(own_f, gains[0])[0].astype(BF)
        normed1 = lax.all_gather(normed1_own, both, axis=0, tiled=True)
        normed1_pair = take_pair(normed1)
        encoder_all = lax.all_gather(encoder, both, axis=0, tiled=True)
        weights_self, weights_cross, weights_ff = map(spread_weights, (parts_self, parts_cross, parts_ff))
        hidden0 = couple(inputs, swap(inputs)).astype(F32)
        cotangent_pair = couple(cotangent, swap(cotangent)).astype(F32)
        targets_all = couple(targets, swap(targets))
        emb_pieces = lax.all_gather(emb_mine, "shard", axis=0)
        emb_pieces = emb_pieces.reshape(shards, vocab_half // 2, 2, depth // shards)
        emb_pieces = jnp.transpose(emb_pieces, (1, 2, 0, 3)).reshape(1, vocab_half // 2, 2 * depth)

    gain_one, gain_two, gain_three, gain_four = [gains[i] for i in range(4)]
    inverse1_own = normalize(own_f, gain_one)[1]
    query_w, key_w, value_w, out_w = [weights_self[:, i * width : (i + 1) * width] for i in range(4)]
    scale = HEAD_DIM**-0.5

    def project_q(normed, weight):
        return matmul(normed, weight).astype(BF) * jnp.asarray(scale, BF)

    positions = jnp.concatenate(
        [c * group + place * rows + jnp.arange(rows, dtype=jnp.int32) for c in range(2)]
    )
    limit = prefix[0]
    seen = jnp.maximum(positions + 1, limit)[None, :]
    chunk = 512
    last0 = jnp.maximum((place + 1) * rows, limit)
    last1 = jnp.maximum(group + (place + 1) * rows, limit)
    limits = jnp.stack([(last0 + chunk - 1) // chunk, (last1 + chunk - 1) // chunk]).astype(jnp.int32)
    causal_blocks = ((0, rows), (rows, rows))
    open_blocks = ((0, pair),)

    query1 = project_q(normed1_pair, query_w)
    kv1 = matmul(normed1, weights_self[:, width : 3 * width]).astype(BF)
    attended1, attended1_t, lse1 = attend(limits, seen, query1, kv1, True, causal_blocks, chunk)

    def add_halves(partial_sum):
        part = partial_sum.astype(BF)
        return partial_sum + swap(part).astype(F32)

    hidden1 = hidden0 + add_halves(right_t(attended1, out_w))
    query2_w, key2_w, value2_w, out2_w = [weights_cross[:, i * width : (i + 1) * width] for i in range(4)]
    kv2 = matmul(encoder_all, weights_cross[:, width : 3 * width]).astype(BF)
    normed2, inverse2 = normalize(hidden1, gain_two)
    normed2 = normed2.astype(BF)
    query2 = project_q(normed2, query2_w)
    attended2, attended2_t, lse2 = attend(limits, seen, query2, kv2, False, open_blocks, chunk)
    hidden2 = hidden1 + add_halves(right_t(attended2, out2_w))
    normed3, inverse3 = normalize(hidden2, gain_three)
    normed3 = normed3.astype(BF)
    gate_w, up_w, down_w = [weights_ff[:, i * 2 * fb : (i + 1) * 2 * fb] for i in range(3)]
    gate = matmul(normed3, gate_w)
    upper = matmul(normed3, up_w)
    active = jax.nn.gelu(gate, approximate=True)
    product = (active * upper).astype(BF)
    final = hidden2 + add_halves(right_t(product, down_w))
    normed4, inverse4 = normalize(final, gain_four)
    normed4 = normed4.astype(BF)

    def mine(array):
        return lax.dynamic_slice_in_dim(array, core * rows, rows, axis=0)

    final_own = mine(final)
    if fast:
        normed4_all = gather_rows(mine(normed4))
    else:
        normed4_all = lax.all_gather(mine(normed4), both, axis=0, tiled=True)
    local_target = (targets_all - (place * embedding.shape[0] + core * vocab_half))[None, :].astype(jnp.int32)
    vblock, rblock = 512, 512
    stats, emb, expo, tops = head_stats(emb_pieces, normed4_all, local_target, vblock, rblock)
    if fast:
        combined = combine_stats(stats)
        logsum = combined[0].reshape(total)
        loss = combined[1].reshape(total)
    else:
        every = lax.all_gather(stats.reshape(3, total), both, axis=0)
        top = jnp.max(every[:, 0], axis=0)
        summed = jnp.sum(every[:, 1] * jnp.exp(every[:, 0] - top[None]), axis=0)
        logsum = top + jnp.log(summed)
        loss = logsum - jnp.sum(every[:, 2], axis=0)
    exit_loss = lax.dynamic_slice_in_dim(loss, core * group, group, axis=0)
    groups = emb_pieces.shape[0]
    emb_grad, grad_normed4 = head_back(
        emb, expo, tops, normed4_all, local_target, logsum[None, :], groups, vocab_half, vblock, rblock
    )
    if fast:
        gn4, emb_own, emb_move = middle_scatter(grad_normed4, emb_grad, vocab_half // 2)
        gn4 = gn4.astype(F32)
    else:
        emb_grad = emb_grad[0, : vocab_half // 2].reshape(vocab_half // 2, 2, shards, depth // shards)
        emb_grad = jnp.transpose(emb_grad, (2, 0, 1, 3)).reshape(shards * vocab_half // 2, 2 * depth // shards)
        emb_sum = lax.psum_scatter(emb_grad, "shard", scatter_dimension=0, tiled=True)
        gn4_own = lax.psum_scatter(grad_normed4, both, scatter_dimension=0, tiled=True)
        gn4 = couple(gn4_own, swap(gn4_own)).astype(F32)
    gain4_rows = gn4 * final * inverse4
    grad_final = cotangent_pair + norm_back(final, inverse4, gain_four, gn4)
    grad_final_b = grad_final.astype(BF)
    down_grad = left_t(grad_final_b, product).astype(BF)
    grad_product = matmul(grad_final_b, down_w)
    unused, gelu_pull = jax.vjp(partial(jax.nn.gelu, approximate=True), gate)
    grad_gate = gelu_pull(grad_product * upper)[0].astype(BF)
    grad_upper = (grad_product * active).astype(BF)
    gate_grad = left_t(normed3, grad_gate).astype(BF)
    upper_grad = left_t(normed3, grad_upper).astype(BF)
    ff_part = jnp.concatenate([gate_grad, upper_grad, down_grad], axis=1)
    gn3 = add_halves(right_t(grad_gate, gate_w) + right_t(grad_upper, up_w))
    gain3_rows = gn3 * hidden2 * inverse3
    grad_hidden2 = grad_final + norm_back(hidden2, inverse3, gain_three, gn3)
    grad_hidden2_b = grad_hidden2.astype(BF)
    out2_grad = left_t(grad_hidden2_b, attended2).astype(BF)
    grad_attended2 = matmul(grad_hidden2_b, out2_w).astype(BF)
    if fast:
        ff_mine = lax.psum_scatter(ff_part, "shard", scatter_dimension=0, tiled=True)
    grad_query2, grad_key2, grad_value2 = attend_back(
        limits, seen, query2, kv2, grad_attended2, attended2_t, lse2, False, open_blocks, chunk
    )
    query2_grad = left_t(normed2, grad_query2).astype(BF)
    key2_grad = left_t(encoder_all, grad_key2).astype(BF)
    value2_grad = left_t(encoder_all, grad_value2).astype(BF)
    cross_parts = [query2_grad, key2_grad, value2_grad, out2_grad]
    encoder_part = (right_t(grad_key2, key2_w) + right_t(grad_value2, value2_w)).astype(BF)
    if fast:
        encoder_part, ff_mine = lax.optimization_barrier((encoder_part, ff_mine))
    encoder_grad = lax.psum_scatter(encoder_part, both, scatter_dimension=0, tiled=True).astype(F32)
    gn2 = add_halves(right_t(grad_query2, query2_w))
    gain2_rows = gn2 * hidden1 * inverse2
    grad_hidden1 = grad_hidden2 + norm_back(hidden1, inverse2, gain_two, gn2)
    grad_hidden1_b = grad_hidden1.astype(BF)
    out_grad = left_t(grad_hidden1_b, attended1).astype(BF)
    grad_attended1 = matmul(grad_hidden1_b, out_w).astype(BF)
    grad_query1, grad_key1, grad_value1 = attend_back(
        limits, seen, query1, kv1, grad_attended1, attended1_t, lse1, True, causal_blocks, chunk
    )
    query_grad = left_t(normed1_pair, grad_query1).astype(BF)
    key_grad = left_t(normed1, grad_key1).astype(BF)
    value_grad = left_t(normed1, grad_value1).astype(BF)
    self_parts = [query_grad, key_grad, value_grad, out_grad]
    normed1_part = right_t(grad_key1, key_w) + right_t(grad_value1, value_w)
    query_part = right_t(grad_query1, query_w).reshape(ctx, rows, depth)
    cut = normed1_part.reshape(ctx, group, depth)
    old = lax.dynamic_slice_in_dim(cut, place * rows, rows, axis=1)
    cut = lax.dynamic_update_slice_in_dim(cut, old + query_part, place * rows, axis=1)
    cut = cut.reshape(total, depth).astype(BF)

    def gain_rows(gn1):
        gain1_sum = jnp.sum(gn1 * own_f * inverse1_own, axis=0)
        return jnp.stack(
            [gain1_sum] + [jnp.sum(mine(a), axis=0) for a in (gain2_rows, gain3_rows, gain4_rows)]
        )

    if fast:
        blocks = [
            [a.reshape(shards, depth // shards, a.shape[1]) for a in parts] for parts in (cross_parts, self_parts)
        ]
        cut, encoder_grad = lax.optimization_barrier((cut, encoder_grad))
        gain1_part = jnp.sum(cut.astype(F32) * normed1.astype(F32), axis=0) / gain_one
        gains_part = [gain1_part] + [jnp.sum(mine(a), axis=0) for a in (gain2_rows, gain3_rows, gain4_rows)]
        gain_pad = jnp.stack(gains_part + [jnp.zeros_like(gain1_part)] * 4)
        gn1, cross_own, self_own, ff_own, gain_sums, embedding_grad = tail_scatter(
            cut, blocks, ff_mine, gain_pad, emb_own, emb_move, [cuts[1], cuts[0], cuts[2]]
        )
        embedding_grad = embedding_grad.astype(F32)
        take = lambda own, index: [own[:, a:b] for a, b in cuts[index]]
        self_grads, cross_grads, ff_grads = take(self_own, 0), take(cross_own, 1), take(ff_own, 2)
    else:
        emb_other = swap(emb_sum)
        emb_halves = [jnp.where(core == 0, emb_sum, emb_other), jnp.where(core == 0, emb_other, emb_sum)]
        slim = depth // shards
        embedding_grad = jnp.concatenate(
            [half[:, p * slim : (p + 1) * slim] for half in emb_halves for p in range(2)], axis=0
        ).astype(F32)
        gn1 = lax.psum_scatter(cut, both, scatter_dimension=0, tiled=True).astype(F32)
        ff_grads = collect_weights(ff_part, [fb, fb, fb])
        cross_grads = collect_weights(jnp.concatenate(cross_parts, axis=1), [hb] * 4)
        self_grads = collect_weights(jnp.concatenate(self_parts, axis=1), [hb] * 4)
        gain_sums = lax.psum(gain_rows(gn1), ("shard", "ctx", "tp"))
    inputs_grad = mine(grad_hidden1) + norm_back(own_f, inverse1_own, gain_one, gn1)
    part = depth // shards
    gain_grads = lax.dynamic_slice_in_dim(gain_sums, lax.axis_index("shard") * part, part, axis=1)
    return (
        final_own.astype(BF), exit_loss, inputs_grad, encoder_grad,
        gain_grads[0], self_grads[0], self_grads[1], self_grads[2], self_grads[3].T,
        gain_grads[1], cross_grads[0], cross_grads[1], cross_grads[2], cross_grads[3].T,
        gain_grads[2], ff_grads[0], ff_grads[1], ff_grads[2].T,
        gain_grads[3], embedding_grad,
    )


def solution(mesh):
    rows = P(("shard", "ctx", "tp"), None)
    into = P("shard", "tp")
    out = P("tp", "shard")
    gain = P("shard")
    weights = (gain, into, into, into, out, gain, into, into, into, out, gain, into, into, out, gain, out)
    return jax.shard_map(
        per_device,
        mesh=mesh,
        in_specs=(rows, rows, P("shard"), P(("shard", "ctx")), rows) + weights,
        out_specs=(rows, P(("shard", "ctx")), rows, rows) + weights,
        check_vma=False,
    )
```

time: 764 us -> 640 us (0.84)
  local copies, waits for them, and re-layouts: 96.4 us -> 30.6 us
  Pallas kernels: 509 us -> 444 us
  waiting for transfers between devices: 13.9 us -> 36.5 us
  starting transfers between devices: 11 us -> 1.12 us
  blocking collectives: 9.52 us -> 0 us
    convert_element_type x10 -> x0, local copies, waits for them, and re-layouts: 47.9 us -> none  [the longest x4 36.5 us: per_device(): jnp.transpose(emb_sum, (0, 2, 1, 3)).reshape(embedding.shape).astype(F32)]
    reduce_scatter x1, waiting for transfers between devices: 0.01 us -> 20.5 us  [per_device(): lax.psum_scatter(encoder_part, both, scatter_dimension=0, tiled=True)]
    pallas_call x1, Pallas kernels: 54.9 us -> 37.2 us  [head_back(): pl.pallas_call(partial(head_back_kernel, vocab=vocab, block=block, rows=r...]
    pallas_call x2, Pallas kernels: 190 us -> 173 us  [the longest x1 129 us: start_gather(): pl.pallas_call(partial(start_kernel, cuts=cuts), in_specs=[vmem] * 5 + [a...]
    pallas_call x1, Pallas kernels: 23.7 us -> 10.2 us  [combine_stats(): pl.pallas_call(stats_kernel, in_specs=[pl.BlockSpec(memory_space=pltpu.VM...]
    ppermute x5, starting transfers between devices: 10.9 us -> 0.61 us  [swap(): return lax.ppermute(array, 'ctx', [(0, 1), (1, 0)])]
    all_gather x1 -> x0, blocking collectives: 9.52 us -> none  [per_device(): lax.all_gather(jnp.stack([gain_self, gain_cross, gain_hidden, gain_exit])...]
    pallas_call x1, Pallas kernels: 101 us -> 91.4 us  [tail_scatter(): pl.pallas_call(partial(tail_kernel, cuts=cuts, chunks=chunks), in_specs=[...]
  transfers between devices with their start and end apart: 8 -> 8, of which waited for: 4 -> 5; matrix products, arithmetic and copies ran while one was open for 19% -> 12% of each run, Pallas kernels for 12% -> 11%
where the time goes in v3:
time: 640 us; the launch traced here: 634 us
  Pallas kernels  444 us (69%)
  matrix products  76.2 us (12%)
  waiting for transfers between devices  36.5 us (6%)
  local copies, waits for them, and re-layouts  30.6 us (5%)
  other arithmetic  29.6 us (5%)
  between operations  16 us (2%)
    pallas_call x1, Pallas kernels, start_gather(): pl.pallas_call(partial(start_kernel, cuts=cuts), in_specs=[vmem] * 5 + [a...  129 us
    pallas_call x1, Pallas kernels, tail_scatter(): pl.pallas_call(partial(tail_kernel, cuts=cuts, chunks=chunks), in_specs=[...  91.4 us
    pallas_call x1, Pallas kernels, middle_scatter(): pl.pallas_call(partial(middle_kernel, chunks=chunks), in_specs=[vmem] * 2...  44.2 us
    pallas_call x1, Pallas kernels, head_back(): pl.pallas_call(partial(head_back_kernel, vocab=vocab, block=block, rows=r...  37.2 us
    pallas_call x2, Pallas kernels, attend_back(): pl.pallas_call(partial(attend_back_kernel, masked=masked, blocks=blocks,...  35.5 us
    pallas_call x1, Pallas kernels, gather_rows(): pl.pallas_call(rows_kernel, in_specs=[pl.BlockSpec(memory_space=pltpu.VME...  35 us
    pallas_call x2, Pallas kernels, attend(): pl.pallas_call(partial(attend_kernel, masked=masked, blocks=blocks, chunk...  31.1 us
    pallas_call x1, Pallas kernels, head_stats(): pl.pallas_call(partial(head_stats_kernel, vocab=vocab, block=block, rows=...  30.8 us
  transfers between devices with their start and end apart: 8, of which 5 were waited for; matrix products, arithmetic and copies ran while one was open for 12% of the time, Pallas kernels for 11%

profile of v3, /device:TPU:0, one launch (start us, length us, event | category | flops | bytes accessed | tf_op | source)
XLA Modules:
  0.0 634.0 jit_solution(4399108411425889120)
XLA Ops:
  15.9 128.7 %start_gather.1 = (f32[8,768]{1,0:T(8,128)}, bf16[2048,768]{1,0:T(8,128)(2,1)}, bf16[2048,768]{1,0:T(8,128)(2,1)}, bf16[512,768]{1,0:T(8,128)(2,1)}, bf16[512,76...) custom-call(f32[8,256]{1,0:T(8,128)} %fusion.66.gains_ref, ...), custom_call_target="tpu_custom_call" | custom-call | tf_op jit(solution)/shard_map/start_gather/pallas_call | solution.py:787
  146.9 2.6 fusion.18.q_ref
  149.5 5.3 convolution_convert_fusion.1.k_ref.v_ref
  154.9 15.8 %attend.2 = (bf16[512,384]{1,0:T(8,128)(2,1)}, f32[384,512]{1,0:T(8,128)}, f32[3,8,512]{2,1,0:T(8,128)}) custom-call(s32[2]{0:T(128)} %pad_add_fusion.limit_ref, s32[1,512]{1,0:T(1,128)} %fusion.70.seen_ref, bf16[512,384]{1,0:T(8,128)(2,1)} %fusion.18.q_ref, bf16[2048,768]{1,0:T(8,128)(2,1)} %convolution_convert_fusion.1.k_ref.v_ref, ...), custom_call_target="tpu_custom_call" | custom-call | flops 1610612736 | bytes 4718592 | tf_op jit(solution)/shard_map/attend/pallas_call | solution.py:63
  172.9 4.0 convolution_convert_fusion.k_ref.v_ref
  179.2 15.3 %attend.3 = (bf16[512,384]{1,0:T(8,128)(2,1)}, f32[384,512]{1,0:T(8,128)}, f32[3,8,512]{2,1,0:T(8,128)}) custom-call(s32[2]{0:T(128)} %pad_add_fusion.limit_ref, s32[1,512]{1,0:T(1,128)} %fusion.70.seen_ref, bf16[512,384]{1,0:T(8,128)(2,1)} %fusion.19.q_ref, bf16[2048,768]{1,0:T(8,128)(2,1)} %convolution_convert_fusion.k_ref.v_ref, ...), custom_call_target="tpu_custom_call" | custom-call | flops 1610612736 | bytes 4718592 | tf_op jit(solution)/shard_map/attend/pallas_call | solution.py:63
  201.2 2.8 fusion.16
  204.5 2.6 multiply_convert_fusion.1
  207.1 2.5 fusion.75
  216.2 35.0 %gather_rows.1.n_ref = bf16[2048,768]{1,0:T(8,128)(2,1)} custom-call(bf16[256,768]{1,0:T(8,128)(2,1)} %multiply_convert_fusion.4.n_ref), custom_call_target="tpu_custom_call" | custom-call | tf_op jit(solution)/shard_map/gather_rows/pallas_call | solution.py:825
  251.2 30.8 %head_stats.1 = (f32[48,128]{1,0:T(8,128)}, bf16[4096,768]{1,0:T(8,128)(2,1)}, bf16[4096,2048]{1,0:T(8,128)(2,1)}, f32[8,2048]{1,0:T(8,128)}) custom-call(bf16[4,2008,384]{2,1,0:T(8,128)(2,1)} %get-tuple-element.72.pieces_ref, bf16[2048,768]{1,0:T(8,128)(2,1)} %gather_rows.1.n_ref, s32[1,2048]{1,0:T(1,128)} %bitcast.86), custom_call_target="tpu_custom_call" | custom-call | flops 12633243648 | bytes 31932416 | tf_op jit(solution)/shard_map/head_stats/pallas_call | solution.py:248
  282.0 10.2 %combine_stats.1 = f32[2,16,128]{2,1,0:T(8,128)} custom-call(f32[48,128]{1,0:T(8,128)} %get-tuple-element.74.stats_ref), custom_call_target="tpu_custom_call" | custom-call | tf_op jit(solution)/shard_map/combine_stats/pallas_call | solution.py:861
  293.4 37.2 %head_back.1 = (bf16[4,2048,384]{2,1,0:T(8,128)(2,1)}, bf16[2048,768]{1,0:T(8,128)(2,1)}) custom-call(bf16[4096,768]{1,0:T(8,128)(2,1)} %get-tuple-element.76.emb_ref, bf16[4096,2048]{1,0:T(8,128)(2,1)} %get-tuple-element.77.expo_ref, f32[8,2048]{1,0:T(8,128)} %get-tuple-element.78.tops_ref, bf16[2048,768]{1,0:T(8,128)(2,1)} %gather_rows.1.n_ref, ...), custom_call_target="tpu_custom_call" | custom-call | flops 25266487296 | bytes 38223872 | tf_op jit(solution)/shard_map/head_back/pallas_call | solution.py:313
  330.6 44.2 %middle_scatter.1 = (bf16[512,768]{1,0:T(8,128)(2,1)}, bf16[2008,384]{1,0:T(8,128)(2,1)}, bf16[2008,384]{1,0:T(8,128)(2,1)}) custom-call(bf16[2048,768]{1,0:T(8,128)(2,1)} %get-tuple-element.79.dn_ref, bf16[4,2048,384]{2,1,0:T(8,128)(2,1)} %get-tuple-element.80.de_ref), custom_call_target="tpu_custom_call" | custom-call | tf_op jit(solution)/shard_map/middle_scatter/pallas_call | solution.py:983
  380.5 3.8 multiply_convert_fusion
  389.3 2.8 fusion.14
  392.1 3.9 fusion.76
  406.1 18.8 %attend_back.2 = (bf16[512,384]{1,0:T(8,128)(2,1)}, bf16[2048,384]{1,0:T(8,128)(2,1)}, bf16[2048,384]{1,0:T(8,128)(2,1)}) custom-call(s32[2]{0:T(128)} %pad_add_fusion.limit_ref, s32[1,512]{1,0:T(1,128)} %fusion.70.seen_ref, bf16[512,384]{1,0:T(8,128)(2,1)} %fusion.19.q_ref, bf16[2048,768]{1,0:T(8,128)(2,1)} %convolution_convert_fusion.k_ref.v_ref, ...), custom_call_target="tpu_custom_call" | custom-call | flops 4026531840 | bytes 10616832 | tf_op jit(solution)/shard_map/attend_back/pallas_call | solution.py:151
  424.9 3.1 fusion.77
  429.9 3.5 add_convert_fusion
  433.3 10.8 %reduce-scatter.3.cloned.1.call-done.f_ref = bf16[192,3072]{1,0:T(8,128)(2,1)} async-done(((bf16[768,3072]{1,0:T(8,128)(2,1)}), bf16[192,3072]{1,0:T(8,128)(2,1)}) %reduce-scatter.3.cloned.1.call-update) | async-done | bytes 1179664 | tf_op jit(solution)/shard_map/reduce_scatter | solution.py:1380
  444.2 3.0 convolution_convert_fusion.11
  447.2 4.7 convolution_convert_fusion.8
  454.1 2.7 convolution_convert_fusion.7
  459.1 2.8 convolution_convert_fusion.13.do_ref
  461.9 16.7 %attend_back.3 = (bf16[512,384]{1,0:T(8,128)(2,1)}, bf16[2048,384]{1,0:T(8,128)(2,1)}, bf16[2048,384]{1,0:T(8,128)(2,1)}) custom-call(s32[2]{0:T(128)} %pad_add_fusion.limit_ref, s32[1,512]{1,0:T(1,128)} %fusion.70.seen_ref, bf16[512,384]{1,0:T(8,128)(2,1)} %fusion.18.q_ref, bf16[2048,768]{1,0:T(8,128)(2,1)} %convolution_convert_fusion.1.k_ref.v_ref, ...), custom_call_target="tpu_custom_call" | custom-call | flops 4026531840 | bytes 10616832 | tf_op jit(solution)/shard_map/attend_back/pallas_call | solution.py:151
  489.3 2.6 convolution_convert_fusion.6
  492.0 2.7 convolution_convert_fusion.5
  494.6 20.5 %reduce-scatter.5.cloned.1.call-done = bf16[256,768]{1,0:T(8,128)(2,1)} async-done(((bf16[2048,768]{1,0:T(8,128)(2,1)}), bf16[256,768]{1,0:T(8,128)(2,1)}) %reduce-scatter.5.cloned.1.call-update) | async-done | bytes 393232 | tf_op jit(solution)/shard_map/reduce_scatter | solution.py:1391
  517.0 2.8 multiply_reduce_fusion
  521.2 91.4 %tail_scatter.1 = (f32[256,768]{1,0:T(8,128)}, f32[192,768]{1,0:T(8,128)}, f32[192,768]{1,0:T(8,128)}, f32[192,1536]{1,0:T(8,128)}, f32[8,768]{1,0:T(8,128)}, /*index=5*/bf16[8032,192]{1,0:T(8,128)(2,1)}) custom-call(bf16[2048,768]{1,0:T(8,128)(2,1)} %bitcast.73, bf16[4,192,384]{2,1,0:T(8,128)(2,1)} %bitcast.78, bf16[4,192,384]{2,1,0:T(8,128)(2,1)} %bitcast.77, ...), custom_call_target="tpu_custom_call" | custom-call | tf_op jit(solution)/shard_map/tail_scatter/pallas_call | solution.py:1130
  612.6 6.6 %copy.46 = f32[8032,192]{0,1:T(8,128)} copy(bf16[8032,192]{1,0:T(8,128)(2,1)} %get-tuple-element.103) | data formatting | bytes 9252864
  (239 shorter events, 77.9 us)
Async XLA Ops:
  7.2 194.0 %all-gather.2.cloned.1.call-start = ((), (), s32[]{:S(2)}) async-start(), calls=%async_computation.2 | async-start | bytes 5898240 | tf_op jit(solution)/shard_map/all_gather | solution.py:1265
  11.5 3.3 copy-start.49
  11.5 3.3 copy-start.50
  11.5 3.3 copy-start.51
  11.5 3.2 copy-start.52
  11.5 3.2 copy-start.53
  11.5 3.2 copy-start.54
  144.6 5.0 copy-start.3
  144.6 299.5 %reduce-scatter.3.cloned.1.call-start = ((), (), s32[]{:S(2)}) async-start(), calls=%async_computation.3 | async-start | bytes 5898240 | tf_op jit(solution)/shard_map/reduce_scatter | solution.py:1380
  154.9 17.9 %copy-start.25 = (bf16[768,1536]{1,0:T(8,128)(2,1)S(1)}, bf16[768,1536]{1,0:T(8,128)(2,1)}, u32[]{:S(2)}) copy-start(bf16[768,1536]{1,0:T(8,128)(2,1)} %get-tuple-element.68) | copy-start | bytes 7077892
  172.6 4.2 collective-permute-start
  172.9 4.0 copy-start.41
  196.1 2.4 collective-permute-start.1
  201.2 3.3 copy-start.42
  209.6 2.6 collective-permute-start.2
  330.6 44.3 %copy-start.1 = (f32[512,768]{1,0:T(8,128)S(1)}, f32[512,768]{1,0:T(8,128)}, u32[]{:S(2)}) copy-start(f32[512,768]{1,0:T(8,128)} %copy-done) | copy-start | bytes 4718596
  380.5 3.8 copy-start.38
  389.0 126.1 %reduce-scatter.5.cloned.1.call-start = ((), (), s32[]{:S(2)}) async-start(), calls=%async_computation.4 | async-start | bytes 3538944 | tf_op jit(solution)/shard_map/reduce_scatter | solution.py:1391
  396.0 4.1 collective-permute-start.3
  424.9 3.1 copy-start.13
  433.3 10.8 %copy-start.30 = (bf16[512,384]{1,0:T(8,128)(2,1)S(1)}, bf16[512,384]{1,0:T(8,128)(2,1)}, u32[]{:S(2)}) copy-start(bf16[512,384]{1,0:T(8,128)(2,1)} %get-tuple-element.70) | copy-start | bytes 1179652
  444.1 3.0 copy-start.39
  444.1 3.0 copy-start.14
  447.2 4.7 copy-start.12
  447.2 4.7 copy-start.59
  447.2 9.6 %collective-permute-start.4 = (bf16[512,768]{1,0:T(8,128)(2,1)S(1)}, bf16[512,768]{1,0:T(8,128)(2,1)S(1)}, u32[]{:S(2)}, u32[]{:S(2)}) collective-permute-start(bf16[512,768]{1,0:T(8,128)(2,1)S(1)} %copy-done.39), channel_id=1, source_target_pairs={{0,4},{4,0},{1,5},{5,1},{2,6},{6,2},{3,7},{7,3},{8,12},{12,8},{9,1... | collective-permute-start | bytes 2359304 | tf_op jit(solution)/shard_map/ppermute | solution.py:1168
  447.2 4.9 copy-start.31
  447.2 6.4 %copy-start.23 = (bf16[2048,384]{1,0:T(8,128)(2,1)S(1)}, bf16[2048,384]{1,0:T(8,128)(2,1)}, u32[]{:S(2)}) copy-start(bf16[2048,384]{1,0:T(8,128)(2,1)} %get-tuple-element.91) | copy-start | bytes 4718596
  459.1 28.8 %copy-start.7 = (f32[512,768]{1,0:T(8,128)}, f32[512,768]{1,0:T(8,128)S(1)}, u32[]{:S(2)}) copy-start(f32[512,768]{1,0:T(8,128)S(1)} %subtract_add_fusion) | copy-start | bytes 4718596
  461.9 16.7 %copy-start.24 = (bf16[768,1536]{1,0:T(8,128)(2,1)S(1)}, bf16[768,1536]{1,0:T(8,128)(2,1)}, u32[]{:S(2)}) copy-start(bf16[768,1536]{1,0:T(8,128)(2,1)} %get-tuple-element.64) | copy-start | bytes 7077892
  484.4 3.4 copy-start.29
  612.6 6.6 %copy-start.32 = (f32[192,1536]{1,0:T(8,128)S(1)}, f32[192,1536]{1,0:T(8,128)}, u32[]{:S(2)}) copy-start(f32[192,1536]{1,0:T(8,128)} %get-tuple-element.102) | copy-start | bytes 3538948
  (47 other events, 91.4 us)
Sparse Core Ops, SparseCore 0:
  144.7 56.4 all-gather.1
  389.2 54.9 reduce-scatter.2
  446.4 68.6 reduce-scatter.4

commit v4 on v3

--- a/solution.py
+++ b/solution.py
@@ -15,69 +15,57 @@
 VMEM_LIMIT = 58 * 2**20
 
 
-def attend_kernel(limit_ref, seen_ref, q_ref, k_ref, v_ref, o_ref, ot_ref, lse_ref, vt_ref, *, masked, blocks, chunk):
+def attend_kernel(seen_ref, q_ref, k_ref, v_ref, o_ref, ot_ref, lse_ref, vt_ref, *, tiles):
     half = lax.broadcasted_iota(jnp.int32, (2 * HEAD_DIM, 1), 0) // HEAD_DIM
     vt_ref[...] = jnp.transpose(v_ref[...])
     q_t = jnp.transpose(q_ref[...])
     for head in range(2):
         part = slice(head * HEAD_DIM, (head + 1) * HEAD_DIM)
-        for index, (first, count) in enumerate(blocks):
-            columns = slice(first, first + count)
-            qt = jnp.where(half == head, q_t[:, columns], 0).astype(BF)
-
-            def step(i, carry):
-                top, total, acc = carry
-                start = pl.multiple_of(i * chunk, chunk)
-                scores = jnp.dot(k_ref[pl.ds(start, chunk), :], qt, preferred_element_type=F32)
-                if masked:
-                    key = lax.broadcasted_iota(jnp.int32, (chunk, 1), 0) + start
-                    scores = jnp.where(key < seen_ref[:, columns], scores, MASKED)
-                new_top = jnp.maximum(top, jnp.max(scores, axis=0, keepdims=True))
-                expo = jnp.exp(scores - new_top)
-                shrink = jnp.exp(top - new_top)
-                total = total * shrink + jnp.sum(expo, axis=0, keepdims=True)
-                acc = acc * shrink + jnp.dot(
-                    vt_ref[part, pl.ds(start, chunk)], expo.astype(BF), preferred_element_type=F32
-                )
-                return (new_top, total, acc)
-
-            init = (
-                jnp.full((1, count), MASKED, F32),
-                jnp.zeros((1, count), F32),
-                jnp.zeros((HEAD_DIM, count), F32),
-            )
+        state = None
+        for rows, keys, masked in tiles:
+            qt = jnp.where(half == head, q_t[:, rows[0] : rows[1]], 0).astype(BF)
+            scores = jnp.dot(k_ref[keys[0] : keys[1], :], qt, preferred_element_type=F32)
             if masked:
-                top, total, acc = lax.fori_loop(0, limit_ref[index], step, init)
-            else:
-                top, total, acc = lax.fori_loop(0, k_ref.shape[0] // chunk, step, init, unroll=True)
-            ot_ref[part, columns] = acc / total
-            lse_ref[0, head : head + 1, columns] = top + jnp.log(total)
+                key = lax.broadcasted_iota(jnp.int32, (keys[1] - keys[0], 1), 0) + keys[0]
+                scores = jnp.where(key < seen_ref[:, rows[0] : rows[1]], scores, MASKED)
+            top = jnp.max(scores, axis=0, keepdims=True)
+            if state is not None:
+                base, old_top, old_total, old_acc = state
+                cut = slice(rows[0] - base, rows[1] - base)
+                top = jnp.maximum(top, old_top[:, cut])
+                shrink = jnp.exp(old_top[:, cut] - top)
+            expo = jnp.exp(scores - top)
+            total = jnp.sum(expo, axis=0, keepdims=True)
+            acc = jnp.dot(vt_ref[part, keys[0] : keys[1]], expo.astype(BF), preferred_element_type=F32)
+            if state is not None:
+                total += old_total[:, cut] * shrink
+                acc += old_acc[:, cut] * shrink
+            state = (rows[0], top, total, acc)
+            ot_ref[part, rows[0] : rows[1]] = acc / total
+            lse_ref[0, head : head + 1, rows[0] : rows[1]] = top + jnp.log(total)
     o_ref[...] = jnp.transpose(ot_ref[...]).astype(BF)
 
 
-def attend(limit, seen, query, kv, masked, blocks, chunk):
+def attend(seen, query, kv, tiles):
     rows, width = query.shape
     count = kv.shape[0]
     pair = 2 * HEAD_DIM
     pairs = width // pair
     return pl.pallas_call(
-        partial(attend_kernel, masked=masked, blocks=blocks, chunk=chunk),
-        grid_spec=pltpu.PrefetchScalarGridSpec(
-            num_scalar_prefetch=1,
-            grid=(pairs,),
-            in_specs=[
-                pl.BlockSpec((1, rows), lambda p, lim: (0, 0)),
-                pl.BlockSpec((rows, pair), lambda p, lim: (0, p)),
-                pl.BlockSpec((count, pair), lambda p, lim: (0, p)),
-                pl.BlockSpec((count, pair), lambda p, lim: (0, p + pairs)),
-            ],
-            out_specs=[
-                pl.BlockSpec((rows, pair), lambda p, lim: (0, p)),
-                pl.BlockSpec((pair, rows), lambda p, lim: (p, 0)),
-                pl.BlockSpec((1, 8, rows), lambda p, lim: (p, 0, 0)),
-            ],
-            scratch_shapes=[pltpu.VMEM((pair, count), BF)],
-        ),
+        partial(attend_kernel, tiles=tiles),
+        grid=(pairs,),
+        in_specs=[
+            pl.BlockSpec((1, rows), lambda p: (0, 0)),
+            pl.BlockSpec((rows, pair), lambda p: (0, p)),
+            pl.BlockSpec((count, pair), lambda p: (0, p)),
+            pl.BlockSpec((count, pair), lambda p: (0, p + pairs)),
+        ],
+        out_specs=[
+            pl.BlockSpec((rows, pair), lambda p: (0, p)),
+            pl.BlockSpec((pair, rows), lambda p: (p, 0)),
+            pl.BlockSpec((1, 8, rows), lambda p: (p, 0, 0)),
+        ],
+        scratch_shapes=[pltpu.VMEM((pair, count), BF)],
         out_shape=(
             jax.ShapeDtypeStruct((rows, width), BF),
             jax.ShapeDtypeStruct((width, rows), F32),
@@ -89,87 +77,77 @@
             bytes_accessed=2 * count * width * 2 + 8 * rows * width,
         ),
         name="attend",
-    )(limit, seen, query, kv, kv)
+    )(seen, query, kv, kv)
 
 
 def attend_back_kernel(
-    limit_ref, seen_ref, q_ref, k_ref, v_ref, do_ref, ot_ref, lse_ref,
-    dq_ref, dk_ref, dv_ref, dk_acc, dv_acc, dqt_acc, kt_ref, *, masked, blocks, chunk,
+    seen_ref, q_ref, k_ref, v_ref, do_ref, ot_ref, lse_ref, dq_ref, dk_ref, dv_ref, dk_acc, dv_acc, dqt_acc, kt_ref, *, tiles
 ):
     half = lax.broadcasted_iota(jnp.int32, (2 * HEAD_DIM, 1), 0) // HEAD_DIM
     lane = lax.broadcasted_iota(jnp.int32, (1, 2 * HEAD_DIM), 1) // HEAD_DIM
     kt_ref[...] = jnp.transpose(k_ref[...])
     q_t = jnp.transpose(q_ref[...])
     do_t = jnp.transpose(do_ref[...])
-    dk_acc[...] = jnp.zeros_like(dk_acc)
-    dv_acc[...] = jnp.zeros_like(dv_acc)
+    dqt_acc[...] = jnp.zeros_like(dqt_acc)
+    done = []
     for head in range(2):
         part = slice(head * HEAD_DIM, (head + 1) * HEAD_DIM)
-        for index, (first, count) in enumerate(blocks):
-            columns = slice(first, first + count)
-            qt = jnp.where(half == head, q_t[:, columns], 0).astype(BF)
-            dot_t = jnp.where(half == head, do_t[:, columns], 0).astype(BF)
-            q = jnp.where(lane == head, q_ref[columns, :], 0).astype(BF)
-            do = jnp.where(lane == head, do_ref[columns, :], 0).astype(BF)
-            inner = jnp.sum(
-                do_t[part, columns].astype(F32) * ot_ref[part, columns], axis=0, keepdims=True
-            )
-            lse = lse_ref[0, head : head + 1, columns]
-
-            def step(i, acc):
-                start = pl.multiple_of(i * chunk, chunk)
-                here = pl.ds(start, chunk)
-                scores = jnp.dot(k_ref[here, :], qt, preferred_element_type=F32)
-                probs = jnp.exp(scores - lse)
-                if masked:
-                    key = lax.broadcasted_iota(jnp.int32, (chunk, 1), 0) + start
-                    probs = jnp.where(key < seen_ref[:, columns], probs, 0.0)
-                grad_probs = jnp.dot(v_ref[here, :], dot_t, preferred_element_type=F32)
-                grad_scores = (probs * (grad_probs - inner)).astype(BF)
-                dv_acc[here, :] += jnp.dot(probs.astype(BF), do, preferred_element_type=F32)
-                dk_acc[here, :] += jnp.dot(grad_scores, q, preferred_element_type=F32)
-                return acc + jnp.dot(kt_ref[part, here], grad_scores, preferred_element_type=F32)
-
-            init = jnp.zeros((HEAD_DIM, count), F32)
+        inner_all = jnp.sum(do_t[part].astype(F32) * ot_ref[part], axis=0, keepdims=True)
+        for rows, keys, masked in tiles:
+            cut = slice(rows[0], rows[1])
+            here = slice(keys[0], keys[1])
+            qt = jnp.where(half == head, q_t[:, cut], 0).astype(BF)
+            dot_t = jnp.where(half == head, do_t[:, cut], 0).astype(BF)
+            q = jnp.where(lane == head, q_ref[cut, :], 0).astype(BF)
+            do = jnp.where(lane == head, do_ref[cut, :], 0).astype(BF)
+            scores = jnp.dot(k_ref[here, :], qt, preferred_element_type=F32)
+            probs = jnp.exp(scores - lse_ref[0, head : head + 1, cut])
             if masked:
-                acc = lax.fori_loop(0, limit_ref[index], step, init)
+                key = lax.broadcasted_iota(jnp.int32, (keys[1] - keys[0], 1), 0) + keys[0]
+                probs = jnp.where(key < seen_ref[:, cut], probs, 0.0)
+            grad_probs = jnp.dot(v_ref[here, :], dot_t, preferred_element_type=F32)
+            grad_scores = (probs * (grad_probs - inner_all[:, cut])).astype(BF)
+            dv = jnp.dot(probs.astype(BF), do, preferred_element_type=F32)
+            dk = jnp.dot(grad_scores, q, preferred_element_type=F32)
+            if keys in done:
+                dv_acc[here, :] += dv
+                dk_acc[here, :] += dk
             else:
-                acc = lax.fori_loop(0, k_ref.shape[0] // chunk, step, init, unroll=True)
-            dqt_acc[part, columns] = acc * HEAD_DIM**-0.5
-    dq_ref[...] = jnp.transpose(dqt_acc[...]).astype(BF)
+                dv_acc[here, :] = dv
+                dk_acc[here, :] = dk
+                done.append(keys)
+            dqt_acc[part, cut] += jnp.dot(kt_ref[part, here], grad_scores, preferred_element_type=F32)
+    dq_ref[...] = jnp.transpose(dqt_acc[...] * HEAD_DIM**-0.5).astype(BF)
     dk_ref[...] = dk_acc[...].astype(BF)
     dv_ref[...] = dv_acc[...].astype(BF)
 
 
-def attend_back(limit, seen, query, kv, grad, out_t, lse, masked, blocks, chunk):
+def attend_back(seen, query, kv, grad, out_t, lse, tiles):
     rows, width = query.shape
     count = kv.shape[0]
     pair = 2 * HEAD_DIM
     pairs = width // pair
-    by_column = pl.BlockSpec((rows, pair), lambda p, lim: (0, p))
-    key_spec = pl.BlockSpec((count, pair), lambda p, lim: (0, p))
+    by_column = pl.BlockSpec((rows, pair), lambda p: (0, p))
+    key_spec = pl.BlockSpec((count, pair), lambda p: (0, p))
     return pl.pallas_call(
-        partial(attend_back_kernel, masked=masked, blocks=blocks, chunk=chunk),
-        grid_spec=pltpu.PrefetchScalarGridSpec(
-            num_scalar_prefetch=1,
-            grid=(pairs,),
-            in_specs=[
-                pl.BlockSpec((1, rows), lambda p, lim: (0, 0)),
-                by_column,
-                key_spec,
-                pl.BlockSpec((count, pair), lambda p, lim: (0, p + pairs)),
-                by_column,
-                pl.BlockSpec((pair, rows), lambda p, lim: (p, 0)),
-                pl.BlockSpec((1, 8, rows), lambda p, lim: (p, 0, 0)),
-            ],
-            out_specs=[by_column, key_spec, key_spec],
-            scratch_shapes=[
-                pltpu.VMEM((count, pair), F32),
-                pltpu.VMEM((count, pair), F32),
-                pltpu.VMEM((pair, rows), F32),
-                pltpu.VMEM((pair, count), BF),
-            ],
-        ),
+        partial(attend_back_kernel, tiles=tiles),
+        grid=(pairs,),
+        in_specs=[
+            pl.BlockSpec((1, rows), lambda p: (0, 0)),
+            by_column,
+            key_spec,
+            pl.BlockSpec((count, pair), lambda p: (0, p + pairs)),
+            by_column,
+            pl.BlockSpec((pair, rows), lambda p: (p, 0)),
+            pl.BlockSpec((1, 8, rows), lambda p: (p, 0, 0)),
+        ],
+        out_specs=[by_column, key_spec, key_spec],
+        scratch_shapes=[
+            pltpu.VMEM((count, pair), F32),
+            pltpu.VMEM((count, pair), F32),
+            pltpu.VMEM((pair, rows), F32),
+            pltpu.VMEM((pair, count), BF),
+        ],
         out_shape=(
             jax.ShapeDtypeStruct((rows, width), BF),
             jax.ShapeDtypeStruct((count, width), BF),
@@ -181,34 +159,19 @@
             bytes_accessed=5 * count * width * 2 + 14 * rows * width,
         ),
         name="attend_back",
-    )(limit, seen, query, kv, kv, grad, out_t, lse)
+    )(seen, query, kv, kv, grad, out_t, lse)
 
 
 def vocab_ids(step, block, vocab):
-    row = lax.broadcasted_iota(jnp.int32, (block, 1), 0)
-    second = (row >= block // 2).astype(jnp.int32)
-    local = row - second * (block // 2) + step * (block // 2)
-    valid = local < vocab // 2
-    return jnp.where(valid, local + second * (vocab // 2), 2**30), valid
-
-
-def head_stats_kernel(
-    pieces_ref, n_ref, target_ref, stats_ref, emb_ref, expo_ref, tops_ref, nt_ref, run_ref, *, vocab, block, rows, scale
-):
+    ids = lax.broadcasted_iota(jnp.int32, (block, 1), 0) + step * block
+    valid = ids < vocab
+    return jnp.where(valid, ids, 2**30), valid
+
+
+def head_stats_kernel(emb_ref, n_ref, target_ref, stats_ref, expo_ref, tops_ref, nt_ref, run_ref, *, vocab, block, rows, scale):
     step = pl.program_id(0)
     ids, valid = vocab_ids(step, block, vocab)
-    width = pieces_ref.shape[2] // 2
-    emb = jnp.concatenate(
-        [
-            jnp.concatenate(
-                [pieces_ref[g, :, p * width : (p + 1) * width] for g in range(pieces_ref.shape[0])], axis=1
-            )
-            for p in range(2)
-        ],
-        axis=0,
-    )
-    emb = jnp.where(valid, emb, 0).astype(BF)
-    emb_ref[...] = emb
+    emb = jnp.transpose(emb_ref[...])
     total = n_ref.shape[0]
 
     @pl.when(step == 0)
@@ -239,29 +202,25 @@
                 stats_ref[k * lines + i : k * lines + i + 1, :] = run_ref[k : k + 1, i * 128 : (i + 1) * 128]
 
 
-def head_stats(pieces, normed, target, block, rows):
-    groups, vocab, width = pieces.shape
-    vocab *= 2
+def head_stats(emb_t, normed, target, vocab, block, rows):
     total, depth = normed.shape
-    steps = pl.cdiv(vocab, block)
+    steps = emb_t.shape[1] // block
     lines = (steps + 7) // 8 * 8
     return pl.pallas_call(
         partial(head_stats_kernel, vocab=vocab, block=block, rows=rows, scale=depth**-0.5),
         grid=(steps,),
         in_specs=[
-            pl.BlockSpec((groups, block // 2, width), lambda i: (0, i, 0)),
+            pl.BlockSpec((depth, block), lambda i: (0, i)),
             pl.BlockSpec((total, depth), lambda i: (0, 0)),
             pl.BlockSpec((1, total), lambda i: (0, 0)),
         ],
         out_specs=[
             pl.BlockSpec((3 * total // 128, 128), lambda i: (0, 0)),
-            pl.BlockSpec((block, depth), lambda i: (i, 0)),
             pl.BlockSpec((block, total), lambda i: (i, 0)),
             pl.BlockSpec((lines, total), lambda i: (0, 0)),
         ],
         out_shape=(
             jax.ShapeDtypeStruct((3 * total // 128, 128), F32),
-            jax.ShapeDtypeStruct((steps * block, depth), BF),
             jax.ShapeDtypeStruct((steps * block, total), BF),
             jax.ShapeDtypeStruct((lines, total), F32),
         ),
@@ -269,10 +228,10 @@
         compiler_params=pltpu.CompilerParams(vmem_limit_bytes=VMEM_LIMIT),
         cost_estimate=pl.CostEstimate(
             flops=2 * vocab * depth * total, transcendentals=vocab * total,
-            bytes_accessed=4 * vocab * depth + 2 * depth * total + 2 * vocab * total,
+            bytes_accessed=2 * vocab * depth + 2 * depth * total + 2 * vocab * total,
         ),
         name="head_stats",
-    )(pieces, normed, target)
+    )(emb_t, normed, target)
 
 
 def head_back_kernel(
@@ -280,7 +239,6 @@
 ):
     step = pl.program_id(0)
     ids, valid = vocab_ids(step, block, vocab)
-    emb_t = jnp.transpose(emb_ref[...])
     factor = jnp.exp(tops_ref[pl.ds(step, 1), :] - lse_ref[...])
 
     @pl.when(step == 0)
@@ -294,27 +252,22 @@
         grad = jnp.where(ids == target_ref[:, columns], probs - 1.0, probs).astype(BF)
         term = jnp.dot(grad, n_ref[columns, :], preferred_element_type=F32)
         de = term if de is None else de + term
-        dnt_acc[:, columns] += jnp.dot(emb_t, grad, preferred_element_type=F32)
-    de = (de * scale).astype(BF)
-    width = de_ref.shape[2] // 2
-    for g in range(de_ref.shape[0]):
-        part = de[:, g * width : (g + 1) * width]
-        de_ref[g] = jnp.concatenate([part[: block // 2], part[block // 2 :]], axis=1)
+        dnt_acc[:, columns] += jnp.dot(emb_ref[...], grad, preferred_element_type=F32)
+    de_ref[...] = jnp.transpose((de * scale).astype(BF))
 
     @pl.when(step == pl.num_programs(0) - 1)
     def _():
         dn_ref[...] = (jnp.transpose(dnt_acc[...]) * scale).astype(BF)
 
 
-def head_back(emb, expo, tops, normed, target, lse, groups, vocab, block, rows):
+def head_back(emb_t, expo, tops, normed, target, lse, vocab, block, rows):
     total, depth = normed.shape
-    steps = pl.cdiv(vocab, block)
-    width = depth // groups
+    steps = emb_t.shape[1] // block
     return pl.pallas_call(
         partial(head_back_kernel, vocab=vocab, block=block, rows=rows, scale=depth**-0.5),
         grid=(steps,),
         in_specs=[
-            pl.BlockSpec((block, depth), lambda i: (i, 0)),
+            pl.BlockSpec((depth, block), lambda i: (0, i)),
             pl.BlockSpec((block, total), lambda i: (i, 0)),
             pl.BlockSpec(tops.shape, lambda i: (0, 0)),
             pl.BlockSpec((total, depth), lambda i: (0, 0)),
@@ -322,11 +275,11 @@
             pl.BlockSpec((1, total), lambda i: (0, 0)),
         ],
         out_specs=[
-            pl.BlockSpec((groups, block // 2, 2 * width), lambda i: (0, i, 0)),
+            pl.BlockSpec((depth, block), lambda i: (0, i)),
             pl.BlockSpec((total, depth), lambda i: (0, 0)),
         ],
         out_shape=(
-            jax.ShapeDtypeStruct((groups, steps * block // 2, 2 * width), BF),
+            jax.ShapeDtypeStruct(emb_t.shape, BF),
             jax.ShapeDtypeStruct((total, depth), BF),
         ),
         scratch_shapes=[pltpu.VMEM((depth, total), F32)],
@@ -336,7 +289,7 @@
             bytes_accessed=4 * vocab * depth + 6 * depth * total + 2 * vocab * total,
         ),
         name="head_back",
-    )(emb, expo, tops, normed, target, lse)
+    )(emb_t, expo, tops, normed, target, lse)
 
 
 MESH = pl.DeviceIdType.MESH
@@ -658,19 +611,17 @@
             self.shared[...] = total[...].astype(BF)
             self.share().start()
 
-    def finish(self, out):
+    def finish(self):
         for slot in range(4):
             pl.when(self.direct(slot))(lambda: self.copy(slot, self.own.at[self.index(slot)]).wait_send())
         for slot, chip in self.passing:
             pl.when(self.adds(slot, chip))(lambda: self.copy(slot, self.going.at[slot]).wait_send())
         pl.when(self.home)(lambda: self.share().wait_send())
         pl.when(jnp.logical_not(self.home))(lambda: self.share().wait_recv())
-        out[...] = self.shared[...].astype(F32)
 
 
 def start_kernel(
-    gains_ref, x_ref, e_ref, g_ref, t_ref, emb_ref, b0, b1, b2,
-    gains_out, n_all, e_all, n_pair, x_pair, g_pair, t_pair, emb_all, w0, w1, mix2,
+    gains_ref, x_ref, e_ref, g_ref, t_ref, b0, b1, b2, gains_out, n_all, e_all, n_pair, x_pair, g_pair, t_pair, w0, w1, mix2,
     gain_slots, n_ref, take0, take1, take2, mix0, mix1, sends, arrivals, local, *, cuts,
 ):
     me = Peers()
@@ -685,11 +636,6 @@
         copy.start()
         locals_.append(copy)
 
-    emb_rows = emb_ref.shape[0]
-    emb_half = emb_rows // 16 * 8
-    copy_here(emb_ref, emb_all.at[me.s])
-    emb_x = send.to(me.x, emb_ref, emb_all.at[me.s])
-    emb_y = send.to(me.y, emb_ref, emb_all.at[me.s])
     gain_slots[me.s] = gains_ref[...]
     gain_copies = [send.to(peer, gains_ref, gain_slots.at[me.s]) for peer in (me.x, me.y, me.d)]
     bundles = [(b0, take0, mix0), (b1, take1, mix1), (b2, take2, mix2)]
@@ -759,10 +705,6 @@
     n_line.step(2)
     lines[2].arrive(1)
     e_line.step(0)
-    pass_on(
-        emb_x, emb_y, emb_all.at[me.sx, pl.ds(0, emb_half)],
-        emb_all.at[me.sy, pl.ds(emb_half, emb_rows - emb_half)],
-    )
     pass_weights(over0, w0)
     lines[2].arrive(2)
     e_line.step(1)
@@ -779,22 +721,21 @@
         copy.wait()
 
 
-def start_gather(gains, inputs, encoder, cotangent, targets, emb, bundles, cuts):
+def start_gather(gains, inputs, encoder, cotangent, targets, bundles, cuts):
     rows, depth = inputs.shape
     part = bundles[0].shape[0]
     any_space = pl.BlockSpec(memory_space=pl.ANY)
     vmem = pl.BlockSpec(memory_space=pltpu.VMEM)
     return pl.pallas_call(
         partial(start_kernel, cuts=cuts),
-        in_specs=[vmem] * 5 + [any_space] + [vmem] * 3,
-        out_specs=[vmem] + [any_space] * 9 + [vmem],
+        in_specs=[vmem] * 8,
+        out_specs=[vmem] + [any_space] * 8 + [vmem],
         out_shape=[
             jax.ShapeDtypeStruct((gains.shape[0], depth), F32),
             jax.ShapeDtypeStruct((8 * rows, depth), BF),
             jax.ShapeDtypeStruct((8 * rows, depth), BF),
         ]
         + [jax.ShapeDtypeStruct((2 * a.shape[0], a.shape[1]), a.dtype) for a in (inputs, inputs, cotangent, targets)]
-        + [jax.ShapeDtypeStruct((4,) + emb.shape, BF)]
         + [jax.ShapeDtypeStruct((4 * part, 2 * b.shape[1]), BF) for b in bundles[:2]]
         + [jax.ShapeDtypeStruct((part, 2 * bundles[2].shape[1]), BF)],
         scratch_shapes=[pltpu.VMEM((4,) + gains.shape, F32), pltpu.VMEM((rows, depth), BF)]
@@ -803,7 +744,7 @@
         + [pltpu.SemaphoreType.DMA((96,)), pltpu.SemaphoreType.DMA((96,)), pltpu.SemaphoreType.DMA((16,))],
         compiler_params=pltpu.CompilerParams(collective_id=0, has_side_effects=True, vmem_limit_bytes=VMEM_LIMIT),
         name="start_gather",
-    )(gains, inputs, encoder, cotangent, targets, emb, *bundles)
+    )(gains, inputs, encoder, cotangent, targets, *bundles)
 
 
 def rows_kernel(n_ref, n_all, sends, arrivals, local):
@@ -954,11 +895,11 @@
     rows = summed.shape[1]
     crossing = settle_first(send, me, dn_ref, other, 4 * rows)
     plane = Planar(send, me, de_ref, first, None, move_ref, chunks)
-    plane.begin()
     crossing.wait_recv()
     settle_second(me, dn_ref, other, summed, rows)
     line = SumLine(pool, me, summed, coming, going)
     line.start()
+    plane.begin()
     for part in range(3):
         line.add(part)
     line.result(total)
@@ -973,12 +914,12 @@
     send.finish()
 
 
-def middle_scatter(dn, de, vocab):
+def middle_scatter(dn, de):
     total, depth = dn.shape
     rows = total // 8
-    width = de.shape[2]
-    chunks = halves(vocab, 3, 16)
-    count = 2 + 12 + 2 * len(chunks)
+    groups, part, wide = de.shape
+    chunks = halves(part, 3, 16)
+    count = 14 + 2 * len(chunks)
     vmem = pl.BlockSpec(memory_space=pltpu.VMEM)
     return pl.pallas_call(
         partial(middle_kernel, chunks=chunks),
@@ -986,8 +927,8 @@
         out_specs=[vmem] * 3,
         out_shape=[
             jax.ShapeDtypeStruct((2 * rows, depth), BF),
-            jax.ShapeDtypeStruct((vocab, width), BF),
-            jax.ShapeDtypeStruct((vocab, width), BF),
+            jax.ShapeDtypeStruct((part, wide), BF),
+            jax.ShapeDtypeStruct((part, wide), BF),
         ],
         scratch_shapes=[
             pltpu.VMEM((4 * rows, depth), BF),
@@ -995,7 +936,7 @@
             pltpu.VMEM((6, rows, depth), BF),
             pltpu.VMEM((6, rows, depth), BF),
             pltpu.VMEM((rows, depth), F32),
-            pltpu.VMEM((2, vocab, width), BF),
+            pltpu.VMEM((2, part, wide), BF),
             pltpu.SemaphoreType.DMA((count,)),
             pltpu.SemaphoreType.DMA((count,)),
         ],
@@ -1006,10 +947,8 @@
 
 def tail_kernel(
     dn_ref, c0, c1, c2, c3, s0, s1, s2, s3, f_ref, gains_ref, eo_ref, em_ref,
-    dn_out, o0, o1, o2, gain_out, eg_out,
-    g0, g1, e_second, e_sum, other, summed, coming, going, first0, second0, moving0, first1, second1, moving1,
-    ab0, ab1, ab2, in0, in1, in2, out0, out1, out2, held0, held1, held2,
-    slots, plane_sum, plane_slots, sends, arrivals, *, cuts, chunks,
+    dn_out, held0, held1, held2, gain_out, e_sum, g0, g1, e_second, other, summed, coming, going, first0, second0, moving0, first1, second1, moving1,
+    ab0, ab1, ab2, in0, in1, in2, out0, out1, out2, sum0, sum1, sum2, slots, plane_sum, plane_slots, sends, arrivals, *, cuts, chunks,
 ):
     me = Peers()
     meet(me.group + [me.x, me.y, me.d])
@@ -1050,11 +989,9 @@
         row_line.add(part)
     planes[0].middle()
     planes[1].middle()
-    vocab, wide = eo_ref.shape
-    e_half = halves(vocab, 1, 16)
     e_copies = [
         send.to(me.y if along_x else me.x, em_ref.at[start:stop], e_second.at[start:stop])
-        for start, stop, along_x in e_half
+        for start, stop, along_x in halves(eo_ref.shape[0], 1, 16)
     ]
     for copy in gain_copies:
         copy.wait_recv()
@@ -1076,7 +1013,7 @@
         lines[0].add(part)
         lines[1].add(part)
     row_line.result(dn_out)
-    ff_line.settle(o2)
+    ff_line.settle(sum2)
     for copy in e_copies:
         copy.wait_recv()
     e_sum[me.c] = (eo_ref[...].astype(F32) + e_second[...].astype(F32)).astype(BF)
@@ -1084,15 +1021,11 @@
     for copy in plane_copies:
         copy.wait_recv()
     gain_out[...] = plane_slots[0] + plane_slots[1] + plane_slots[2] + plane_slots[3]
-    lines[0].settle(o0)
+    lines[0].settle(sum0)
+    lines[1].settle(sum1)
+    for line in (ff_line, lines[0], lines[1]):
+        line.finish()
     e_share.wait_recv()
-    for c in range(2):
-        for p in range(2):
-            first_row = (2 * c + p) * vocab
-            eg_out[first_row : first_row + vocab, :] = e_sum[c, :, p * wide // 2 : (p + 1) * wide // 2]
-    lines[1].settle(o1)
-    for line, out in ((ff_line, o2), (lines[0], o0), (lines[1], o1)):
-        line.finish(out)
     row_line.finish()
     send.finish()
 
@@ -1109,7 +1042,6 @@
         pltpu.VMEM((groups, part, width), BF),
         pltpu.VMEM((groups, part, width), BF),
         pltpu.VMEM(emb_own.shape, BF),
-        pltpu.VMEM((2,) + emb_own.shape, BF),
         pltpu.VMEM((4 * rows, depth), BF),
         pltpu.VMEM((4, rows, depth), BF),
         pltpu.VMEM((6, rows, depth), BF),
@@ -1119,7 +1051,7 @@
         scratch += [pltpu.VMEM((2, part, width), BF), pltpu.VMEM((part, width), BF), pltpu.VMEM((part, width), BF)]
     for count in (2, 4, 4):
         scratch += [pltpu.VMEM((count, part, w), BF) for w in widths]
-    scratch += [pltpu.VMEM((part, w), BF) for w in widths]
+    scratch += [pltpu.VMEM((part, w), F32) for w in widths]
     scratch += [
         pltpu.VMEM((8,) + gains.shape, F32),
         pltpu.VMEM(gains.shape, F32),
@@ -1132,13 +1064,47 @@
         in_specs=[vmem] * 13,
         out_specs=[vmem] * 6,
         out_shape=[jax.ShapeDtypeStruct((rows, depth), F32)]
-        + [jax.ShapeDtypeStruct((part, w), F32) for w in widths]
-        + [jax.ShapeDtypeStruct(gains.shape, F32)]
-        + [jax.ShapeDtypeStruct((4 * emb_own.shape[0], emb_own.shape[1] // 2), BF)],
+        + [jax.ShapeDtypeStruct((part, w), BF) for w in widths]
+        + [jax.ShapeDtypeStruct(gains.shape, F32), jax.ShapeDtypeStruct((2,) + emb_own.shape, BF)],
         scratch_shapes=scratch,
         compiler_params=pltpu.CompilerParams(collective_id=4, has_side_effects=True, vmem_limit_bytes=VMEM_LIMIT),
         name="tail_scatter",
     )(dn, *grads[0], *grads[1], ff, gains, emb_own, emb_move)
+
+
+def finish_kernel(
+    emb_ref, self_ref, cross_ref, ff_ref, x_ref, gh_ref, gn_ref, gain_ref, eg_ref, dx_ref, *outs
+):
+    half = eg_ref.shape[1] // 2
+    for c in range(2):
+        eg_ref[:, c * half : (c + 1) * half] = emb_ref[c, :, :half].astype(F32)
+    x = x_ref[...].astype(F32)
+    inverse = lax.rsqrt(jnp.mean(x * x, axis=-1, keepdims=True) + EPS)
+    dx_ref[...] = gh_ref[...] + norm_back(x, inverse, gain_ref[...], gn_ref[...])
+    index = 0
+    for ref, count in ((self_ref, 4), (cross_ref, 4), (ff_ref, 3)):
+        size = ref.shape[1] // count
+        for k in range(count):
+            outs[index][...] = ref[:, k * size : (k + 1) * size].astype(F32)
+            index += 1
+
+
+def finish(emb, own_self, own_cross, own_ff, x, grad_hidden, gn, gain, vocab):
+    part, width = own_self.shape
+    shapes = []
+    for total, count in ((width, 4), (width, 4), (own_ff.shape[1], 3)):
+        shapes += [(part, total // count)] * count
+    ins = (emb, own_self, own_cross, own_ff, x, grad_hidden, gn, gain)
+    vmem = pl.BlockSpec(memory_space=pltpu.VMEM)
+    return pl.pallas_call(
+        finish_kernel,
+        in_specs=[vmem] * len(ins),
+        out_specs=[vmem] * (2 + len(shapes)),
+        out_shape=[jax.ShapeDtypeStruct((part, vocab), F32), jax.ShapeDtypeStruct(x.shape, F32)]
+        + [jax.ShapeDtypeStruct(shape, F32) for shape in shapes],
+        compiler_params=pltpu.CompilerParams(vmem_limit_bytes=VMEM_LIMIT),
+        name="finish",
+    )(*ins)
 
 
 def normalize(hidden, gain):
@@ -1242,8 +1208,10 @@
     gain_parts = jnp.stack([gain_self, gain_cross, gain_hidden, gain_exit])
     cuts = [[(i * w, (i + 1) * w) for i in range(n)] for n, w in ((4, hb), (4, hb), (3, fb))]
     vocab_half = embedding.shape[0] // ctx
-    emb_mine = lax.dynamic_slice_in_dim(embedding, core * vocab_half, vocab_half, axis=0)
-    emb_mine = jnp.concatenate([emb_mine[: vocab_half // 2], emb_mine[vocab_half // 2 :]], axis=1)
+    vblock, rblock = 512, 512
+    emb_mine = lax.dynamic_slice_in_dim(embedding.T, core * vocab_half, vocab_half, axis=1)
+    emb_mine = jnp.pad(emb_mine, ((0, 0), (0, -vocab_half % vblock)))
+    emb_t = lax.all_gather(emb_mine, "shard", axis=0, tiled=True)
 
     def take_pair(array):
         cut = array.reshape(ctx, group, depth)
@@ -1254,14 +1222,14 @@
         spare = -(depth // shards) % 128
         gain_block = jnp.pad(gain_parts.astype(F32), ((0, 4), (0, spare)))
         (
-            gains, normed1, encoder_all, normed1_pair, x_pair, g_pair, t_pair, emb_pieces, weights_self, weights_cross,
-            ff_mix,
+            gains, normed1, encoder_all, normed1_pair, x_pair, g_pair, t_pair, weights_self, weights_cross, ff_mix,
         ) = start_gather(
-            gain_block, inputs, encoder, cotangent, targets.reshape(8, group // 8), emb_mine, bundles, cuts
+            gain_block, inputs, encoder, cotangent, targets.reshape(8, group // 8), bundles, cuts
         )
         hidden0 = x_pair.astype(F32)
         cotangent_pair = g_pair.astype(F32)
         targets_all = t_pair.reshape(total)
+        ff_mix, emb_t = lax.optimization_barrier((ff_mix, emb_t))
         weights_ff = lax.all_gather(ff_mix, "shard", axis=0, tiled=True)
     else:
         gains = lax.all_gather(gain_parts, "shard", axis=1, tiled=True).astype(F32)
@@ -1273,9 +1241,6 @@
         hidden0 = couple(inputs, swap(inputs)).astype(F32)
         cotangent_pair = couple(cotangent, swap(cotangent)).astype(F32)
         targets_all = couple(targets, swap(targets))
-        emb_pieces = lax.all_gather(emb_mine, "shard", axis=0)
-        emb_pieces = emb_pieces.reshape(shards, vocab_half // 2, 2, depth // shards)
-        emb_pieces = jnp.transpose(emb_pieces, (1, 2, 0, 3)).reshape(1, vocab_half // 2, 2 * depth)
 
     gain_one, gain_two, gain_three, gain_four = [gains[i] for i in range(4)]
     inverse1_own = normalize(own_f, gain_one)[1]
@@ -1290,16 +1255,12 @@
     )
     limit = prefix[0]
     seen = jnp.maximum(positions + 1, limit)[None, :]
-    chunk = 512
-    last0 = jnp.maximum((place + 1) * rows, limit)
-    last1 = jnp.maximum(group + (place + 1) * rows, limit)
-    limits = jnp.stack([(last0 + chunk - 1) // chunk, (last1 + chunk - 1) // chunk]).astype(jnp.int32)
-    causal_blocks = ((0, rows), (rows, rows))
-    open_blocks = ((0, pair),)
+    causal_tiles = (((0, pair), (0, group), True), ((rows, pair), (group, total), True))
+    open_tiles = (((0, pair), (0, total), False),)
 
     query1 = project_q(normed1_pair, query_w)
     kv1 = matmul(normed1, weights_self[:, width : 3 * width]).astype(BF)
-    attended1, attended1_t, lse1 = attend(limits, seen, query1, kv1, True, causal_blocks, chunk)
+    attended1, attended1_t, lse1 = attend(seen, query1, kv1, causal_tiles)
 
     def add_halves(partial_sum):
         part = partial_sum.astype(BF)
@@ -1311,7 +1272,7 @@
     normed2, inverse2 = normalize(hidden1, gain_two)
     normed2 = normed2.astype(BF)
     query2 = project_q(normed2, query2_w)
-    attended2, attended2_t, lse2 = attend(limits, seen, query2, kv2, False, open_blocks, chunk)
+    attended2, attended2_t, lse2 = attend(seen, query2, kv2, open_tiles)
     hidden2 = hidden1 + add_halves(right_t(attended2, out2_w))
     normed3, inverse3 = normalize(hidden2, gain_three)
     normed3 = normed3.astype(BF)
@@ -1333,8 +1294,7 @@
     else:
         normed4_all = lax.all_gather(mine(normed4), both, axis=0, tiled=True)
     local_target = (targets_all - (place * embedding.shape[0] + core * vocab_half))[None, :].astype(jnp.int32)
-    vblock, rblock = 512, 512
-    stats, emb, expo, tops = head_stats(emb_pieces, normed4_all, local_target, vblock, rblock)
+    stats, expo, tops = head_stats(emb_t, normed4_all, local_target, vocab_half, vblock, rblock)
     if fast:
         combined = combine_stats(stats)
         logsum = combined[0].reshape(total)
@@ -1346,17 +1306,15 @@
         logsum = top + jnp.log(summed)
         loss = logsum - jnp.sum(every[:, 2], axis=0)
     exit_loss = lax.dynamic_slice_in_dim(loss, core * group, group, axis=0)
-    groups = emb_pieces.shape[0]
     emb_grad, grad_normed4 = head_back(
-        emb, expo, tops, normed4_all, local_target, logsum[None, :], groups, vocab_half, vblock, rblock
+        emb_t, expo, tops, normed4_all, local_target, logsum[None, :], vocab_half, vblock, rblock
     )
     if fast:
-        gn4, emb_own, emb_move = middle_scatter(grad_normed4, emb_grad, vocab_half // 2)
+        gn4, emb_own, emb_move = middle_scatter(grad_normed4, emb_grad.reshape(shards, depth // shards, -1))
         gn4 = gn4.astype(F32)
     else:
-        emb_grad = emb_grad[0, : vocab_half // 2].reshape(vocab_half // 2, 2, shards, depth // shards)
-        emb_grad = jnp.transpose(emb_grad, (2, 0, 1, 3)).reshape(shards * vocab_half // 2, 2 * depth // shards)
         emb_sum = lax.psum_scatter(emb_grad, "shard", scatter_dimension=0, tiled=True)
+        emb_other = swap(emb_sum)
         gn4_own = lax.psum_scatter(grad_normed4, both, scatter_dimension=0, tiled=True)
         gn4 = couple(gn4_own, swap(gn4_own)).astype(F32)
     gain4_rows = gn4 * final * inverse4
@@ -1379,7 +1337,7 @@
     if fast:
         ff_mine = lax.psum_scatter(ff_part, "shard", scatter_dimension=0, tiled=True)
     grad_query2, grad_key2, grad_value2 = attend_back(
-        limits, seen, query2, kv2, grad_attended2, attended2_t, lse2, False, open_blocks, chunk
+        seen, query2, kv2, grad_attended2, attended2_t, lse2, open_tiles
     )
     query2_grad = left_t(normed2, grad_query2).astype(BF)
     key2_grad = left_t(encoder_all, grad_key2).astype(BF)
@@ -1396,7 +1354,7 @@
     out_grad = left_t(grad_hidden1_b, attended1).astype(BF)
     grad_attended1 = matmul(grad_hidden1_b, out_w).astype(BF)
     grad_query1, grad_key1, grad_value1 = attend_back(
-        limits, seen, query1, kv1, grad_attended1, attended1_t, lse1, True, causal_blocks, chunk
+        seen, query1, kv1, grad_attended1, attended1_t, lse1, causal_tiles
     )
     query_grad = left_t(normed1_pair, grad_query1).astype(BF)
     key_grad = left_t(normed1, grad_key1).astype(BF)
@@ -1419,37 +1377,34 @@
         blocks = [
             [a.reshape(shards, depth // shards, a.shape[1]) for a in parts] for parts in (cross_parts, self_parts)
         ]
-        cut, encoder_grad = lax.optimization_barrier((cut, encoder_grad))
         gain1_part = jnp.sum(cut.astype(F32) * normed1.astype(F32), axis=0) / gain_one
         gains_part = [gain1_part] + [jnp.sum(mine(a), axis=0) for a in (gain2_rows, gain3_rows, gain4_rows)]
         gain_pad = jnp.stack(gains_part + [jnp.zeros_like(gain1_part)] * 4)
-        gn1, cross_own, self_own, ff_own, gain_sums, embedding_grad = tail_scatter(
+        gn1, cross_own, self_own, ff_own, gain_sums, emb_sums = tail_scatter(
             cut, blocks, ff_mine, gain_pad, emb_own, emb_move, [cuts[1], cuts[0], cuts[2]]
         )
-        embedding_grad = embedding_grad.astype(F32)
-        take = lambda own, index: [own[:, a:b] for a, b in cuts[index]]
-        self_grads, cross_grads, ff_grads = take(self_own, 0), take(cross_own, 1), take(ff_own, 2)
+        embedding_grad, inputs_grad, *weight_grads = finish(
+            emb_sums, self_own, cross_own, ff_own, inputs, mine(grad_hidden1), gn1, gain_one[None],
+            embedding.shape[0],
+        )
     else:
-        emb_other = swap(emb_sum)
-        emb_halves = [jnp.where(core == 0, emb_sum, emb_other), jnp.where(core == 0, emb_other, emb_sum)]
-        slim = depth // shards
-        embedding_grad = jnp.concatenate(
-            [half[:, p * slim : (p + 1) * slim] for half in emb_halves for p in range(2)], axis=0
-        ).astype(F32)
+        emb_halves = [jnp.where(core == 0, a, b)[:, :vocab_half] for a, b in ((emb_sum, emb_other), (emb_other, emb_sum))]
+        embedding_grad = jnp.concatenate(emb_halves, axis=1).astype(F32)
         gn1 = lax.psum_scatter(cut, both, scatter_dimension=0, tiled=True).astype(F32)
         ff_grads = collect_weights(ff_part, [fb, fb, fb])
         cross_grads = collect_weights(jnp.concatenate(cross_parts, axis=1), [hb] * 4)
         self_grads = collect_weights(jnp.concatenate(self_parts, axis=1), [hb] * 4)
         gain_sums = lax.psum(gain_rows(gn1), ("shard", "ctx", "tp"))
-    inputs_grad = mine(grad_hidden1) + norm_back(own_f, inverse1_own, gain_one, gn1)
+        inputs_grad = mine(grad_hidden1) + norm_back(own_f, inverse1_own, gain_one, gn1)
+        weight_grads = []
+        for grads in (self_grads, cross_grads, ff_grads):
+            weight_grads += grads
     part = depth // shards
     gain_grads = lax.dynamic_slice_in_dim(gain_sums, lax.axis_index("shard") * part, part, axis=1)
     return (
         final_own.astype(BF), exit_loss, inputs_grad, encoder_grad,
-        gain_grads[0], self_grads[0], self_grads[1], self_grads[2], self_grads[3].T,
-        gain_grads[1], cross_grads[0], cross_grads[1], cross_grads[2], cross_grads[3].T,
-        gain_grads[2], ff_grads[0], ff_grads[1], ff_grads[2].T,
-        gain_grads[3], embedding_grad,
+        gain_grads[0], *weight_grads[:3], weight_grads[3].T, gain_grads[1], *weight_grads[4:7], weight_grads[7].T,
+        gain_grads[2], *weight_grads[8:10], weight_grads[10].T, gain_grads[3], embedding_grad.T,
     )
 
 

time: 640 us -> 592 us (0.925)
  waiting for transfers between devices: 36.5 us -> 12.3 us
  Pallas kernels: 444 us -> 421 us
    pallas_call x5 -> x6, Pallas kernels: 195 us -> 168 us  [the longest x1 102 us: start_gather(): pl.pallas_call(partial(start_kernel, cuts=cuts), in_specs=[vmem] * 8, out...]
    reduce_scatter x1, waiting for transfers between devices: 20.5 us -> 0.01 us  [per_device(): lax.psum_scatter(encoder_part, both, scatter_dimension=0, tiled=True)]
    reduce_scatter x1, waiting for transfers between devices: 10.8 us -> 1.52 us  [per_device(): lax.psum_scatter(ff_part, 'shard', scatter_dimension=0, tiled=True)]
    pallas_call x1, Pallas kernels: 91.4 us -> 98.1 us  [tail_scatter(): pl.pallas_call(partial(tail_kernel, cuts=cuts, chunks=chunks), in_specs=[...]
    unnamed x149 -> x130, local copies, waits for them, and re-layouts: 19.4 us -> 15 us
  transfers between devices with their start and end apart: 8 -> 9, of which waited for: 5 -> 4; matrix products, arithmetic and copies ran while one was open for 12% -> 16% of each run, Pallas kernels for 11% -> 45%
where the time goes in v4:
time: 592 us; the launch traced here: 588 us
  Pallas kernels  421 us (71%)
  matrix products  78 us (13%)
  local copies, waits for them, and re-layouts  27.7 us (5%)
  other arithmetic  27 us (5%)
  between operations  15.8 us (3%)
  waiting for transfers between devices  12.3 us (2%)
    pallas_call x1, Pallas kernels, start_gather(): pl.pallas_call(partial(start_kernel, cuts=cuts), in_specs=[vmem] * 8, out...  102 us
    pallas_call x1, Pallas kernels, tail_scatter(): pl.pallas_call(partial(tail_kernel, cuts=cuts, chunks=chunks), in_specs=[...  98.1 us
    pallas_call x1, Pallas kernels, middle_scatter(): pl.pallas_call(partial(middle_kernel, chunks=chunks), in_specs=[vmem] * 2...  49.7 us
    pallas_call x1, Pallas kernels, head_back(): pl.pallas_call(partial(head_back_kernel, vocab=vocab, block=block, rows=r...  35.2 us
    pallas_call x2, Pallas kernels, attend_back(): pl.pallas_call(partial(attend_back_kernel, tiles=tiles), grid=(pairs,), i...  34.4 us
    pallas_call x1, Pallas kernels, gather_rows(): pl.pallas_call(rows_kernel, in_specs=[pl.BlockSpec(memory_space=pltpu.VME...  31.9 us
    pallas_call x1, Pallas kernels, head_stats(): pl.pallas_call(partial(head_stats_kernel, vocab=vocab, block=block, rows=...  30.4 us
    dot_general x9, matrix products, matmul(): return jnp.dot(left, right, preferred_element_type=F32)  27.9 us
  transfers between devices with their start and end apart: 9, of which 4 were waited for; matrix products, arithmetic and copies ran while one was open for 16% of the time, Pallas kernels for 45%

profile of v4, /device:TPU:0, one launch (start us, length us, event | category | flops | bytes accessed | tf_op | source)
XLA Modules:
  0.0 587.6 jit_solution(4259725061548867886)
XLA Ops:
  14.7 101.6 %start_gather.1 = (f32[8,768]{1,0:T(8,128)}, bf16[2048,768]{1,0:T(8,128)(2,1)}, bf16[2048,768]{1,0:T(8,128)(2,1)}, bf16[512,768]{1,0:T(8,128)(2,1)}, bf16[512,76...) custom-call(f32[8,256]{1,0:T(8,128)} %fusion.61.gains_ref, ...), custom_call_target="tpu_custom_call" | custom-call | tf_op jit(solution)/shard_map/start_gather/pallas_call | solution.py:729
  118.5 2.6 fusion.18.q_ref
  121.1 5.2 convolution_convert_fusion.1.k_ref.v_ref
  126.3 12.2 %attend.2 = (bf16[512,384]{1,0:T(8,128)(2,1)}, f32[384,512]{1,0:T(8,128)}, f32[3,8,512]{2,1,0:T(8,128)}) custom-call(s32[1,512]{1,0:T(1,128)} %fusion.65.seen_ref, bf16[512,384]{1,0:T(8,128)(2,1)} %fusion.18.q_ref, bf16[2048,768]{1,0:T(8,128)(2,1)} %convolution_convert_fusion.1.k_ref.v_ref, bf16[2048,768]{1,0:T(8,128)(2,1)} %convolution_convert_fusion.1.k_ref.v_ref), custom_call_target="tpu_custom_call" | custom-call | flops 1610612736 | bytes 4718592 | tf_op jit(solution)/shard_map/attend/pallas_call | solution.py:54
  140.5 3.9 collective-permute-start
  144.9 4.0 convolution_convert_fusion.k_ref.v_ref
  150.7 12.0 %attend.3 = (bf16[512,384]{1,0:T(8,128)(2,1)}, f32[384,512]{1,0:T(8,128)}, f32[3,8,512]{2,1,0:T(8,128)}) custom-call(s32[1,512]{1,0:T(1,128)} %fusion.65.seen_ref, bf16[512,384]{1,0:T(8,128)(2,1)} %fusion.19.q_ref, bf16[2048,768]{1,0:T(8,128)(2,1)} %convolution_convert_fusion.k_ref.v_ref, bf16[2048,768]{1,0:T(8,128)(2,1)} %convolution_convert_fusion.k_ref.v_ref), custom_call_target="tpu_custom_call" | custom-call | flops 1610612736 | bytes 4718592 | tf_op jit(solution)/shard_map/attend/pallas_call | solution.py:54
  168.1 6.4 %all-gather.5.cloned.1.call-done = bf16[768,3072]{1,0:T(8,128)(2,1)} async-done(((bf16[192,3072]{1,0:T(8,128)(2,1)}), bf16[768,3072]{1,0:T(8,128)(2,1)}) %all-gather.5.cloned.1.call-update) | async-done | bytes 4718608 | tf_op jit(solution)/shard_map/all_gather | solution.py:1233
  174.5 2.8 fusion.16
  177.8 2.6 multiply_convert_fusion.1
  189.5 31.9 %gather_rows.1.n_ref = bf16[2048,768]{1,0:T(8,128)(2,1)} custom-call(bf16[256,768]{1,0:T(8,128)(2,1)} %multiply_convert_fusion.4.n_ref), custom_call_target="tpu_custom_call" | custom-call | tf_op jit(solution)/shard_map/gather_rows/pallas_call | solution.py:766
  221.4 30.4 %head_stats.1 = (f32[48,128]{1,0:T(8,128)}, bf16[4096,2048]{1,0:T(8,128)(2,1)}, f32[8,2048]{1,0:T(8,128)}) custom-call(bf16[768,4096]{1,0:T(8,128)(2,1)} %all-gather.3.cloned.1.call-done.emb_ref, bf16[2048,768]{1,0:T(8,128)(2,1)} %gather_rows.1.n_ref, s32[1,2048]{1,0:T(1,128)} %bitcast.86), custom_call_target="tpu_custom_call" | custom-call | flops 12633243648 | bytes 25763840 | tf_op jit(solution)/shard_map/head_stats/pallas_call | solution.py:209
  251.9 8.0 %combine_stats.1 = f32[2,16,128]{2,1,0:T(8,128)} custom-call(f32[48,128]{1,0:T(8,128)} %get-tuple-element.86.stats_ref), custom_call_target="tpu_custom_call" | custom-call | tf_op jit(solution)/shard_map/combine_stats/pallas_call | solution.py:802
  261.2 35.2 %head_back.1 = (bf16[768,4096]{1,0:T(8,128)(2,1)}, bf16[2048,768]{1,0:T(8,128)(2,1)}) custom-call(bf16[768,4096]{1,0:T(8,128)(2,1)} %all-gather.3.cloned.1.call-done.emb_ref, bf16[4096,2048]{1,0:T(8,128)(2,1)} %get-tuple-element.88.expo_ref, f32[8,2048]{1,0:T(8,128)} %get-tuple-element.89.tops_ref, bf16[2048,768]{1,0:T(8,128)(2,1)} %gather_rows.1.n_ref, ...), custom_call_target="tpu_custom_call" | custom-call | flops 25266487296 | bytes 38223872 | tf_op jit(solution)/shard_map/head_back/pallas_call | solution.py:266
  296.4 49.7 %middle_scatter.1 = (bf16[512,768]{1,0:T(8,128)(2,1)}, bf16[192,4096]{1,0:T(8,128)(2,1)}, bf16[192,4096]{1,0:T(8,128)(2,1)}) custom-call(bf16[2048,768]{1,0:T(8,128)(2,1)} %get-tuple-element.90.dn_ref, bf16[4,192,4096]{2,1,0:T(8,128)(2,1)} %bitcast.71), custom_call_target="tpu_custom_call" | custom-call | tf_op jit(solution)/shard_map/middle_scatter/pallas_call | solution.py:924
  351.8 3.8 multiply_convert_fusion
  360.8 2.8 fusion.14
  363.7 4.3 fusion.71
  375.5 2.8 convolution_convert_fusion.14.do_ref
  378.3 18.0 %attend_back.2 = (bf16[512,384]{1,0:T(8,128)(2,1)}, bf16[2048,384]{1,0:T(8,128)(2,1)}, bf16[2048,384]{1,0:T(8,128)(2,1)}) custom-call(s32[1,512]{1,0:T(1,128)} %fusion.65.seen_ref, bf16[512,384]{1,0:T(8,128)(2,1)} %fusion.19.q_ref, bf16[2048,768]{1,0:T(8,128)(2,1)} %convolution_convert_fusion.k_ref.v_ref, ...), custom_call_target="tpu_custom_call" | custom-call | flops 4026531840 | bytes 10616832 | tf_op jit(solution)/shard_map/attend_back/pallas_call | solution.py:132
  396.4 3.3 fusion.72
  403.7 2.6 convolution_convert_fusion.8
  406.4 3.5 add_convert_fusion
  414.8 4.7 convolution_convert_fusion.7
  424.8 2.7 convolution_convert_fusion.13.do_ref
  427.5 16.4 %attend_back.3 = (bf16[512,384]{1,0:T(8,128)(2,1)}, bf16[2048,384]{1,0:T(8,128)(2,1)}, bf16[2048,384]{1,0:T(8,128)(2,1)}) custom-call(s32[1,512]{1,0:T(1,128)} %fusion.65.seen_ref, bf16[512,384]{1,0:T(8,128)(2,1)} %fusion.18.q_ref, bf16[2048,768]{1,0:T(8,128)(2,1)} %convolution_convert_fusion.1.k_ref.v_ref, ...), custom_call_target="tpu_custom_call" | custom-call | flops 4026531840 | bytes 10616832 | tf_op jit(solution)/shard_map/attend_back/pallas_call | solution.py:132
  451.3 2.5 multiply_reduce_fusion
  460.1 3.0 convolution_convert_fusion.9
  463.1 2.7 convolution_convert_fusion.6
  465.7 2.7 convolution_convert_fusion.5
  468.4 98.1 %tail_scatter.1 = (f32[256,768]{1,0:T(8,128)}, bf16[192,768]{1,0:T(8,128)(2,1)}, bf16[192,768]{1,0:T(8,128)(2,1)}, bf16[192,1536]{1,0:T(8,128)(2,1)}, f32[8,768]{1,0:T(8,128)}, /*index=5*/bf16[2,192,4096]{2,1,0:T(8,128)(2,1)}) custom-call(bf16[2048,768]{1,0:T(8,128)(2,1)} %bitcast.70, bf16[4,192,384]{2,1,0:T(8,128)(2,1)} %bitcast.76, ...), custom_call_target="tpu_custom_call" | custom-call | tf_op jit(solution)/shard_map/tail_scatter/pallas_call | solution.py:1062
  566.5 7.5 %finish.1 = (f32[192,8032]{1,0:T(8,128)}, f32[256,768]{1,0:T(8,128)}, f32[192,192]{1,0:T(8,128)}, f32[192,192]{1,0:T(8,128)}, f32[192,192]{1,0:T(8,128)}, /*inde...) custom-call(bf16[2,192,4096]{2,1,0:T(8,128)(2,1)} %get-tuple-element, ...), custom_call_target="tpu_custom_call" | custom-call | tf_op jit(solution)/shard_map/finish/pallas_call | solution.py:1099
  (216 shorter events, 82.1 us)
Async XLA Ops:
  7.2 109.1 %all-gather.3.cloned.1.call-start = ((), (), s32[]{:S(2)}) async-start(), calls=%async_computation.2 | async-start | bytes 7864320 | tf_op jit(solution)/shard_map/all_gather | solution.py:1214
  11.0 2.8 copy-start.38
  11.0 2.8 copy-start.39
  11.1 2.8 copy-start.40
  11.1 163.4 %all-gather.5.cloned.1.call-start = ((), (), s32[]{:S(2)}) async-start(), calls=%async_computation.3 | async-start | bytes 5898240 | tf_op jit(solution)/shard_map/all_gather | solution.py:1233
  116.3 4.8 copy-start.5
  116.3 298.4 %reduce-scatter.3.cloned.1.call-start = ((), (), s32[]{:S(2)}) async-start(), calls=%async_computation.4 | async-start | bytes 5898240 | tf_op jit(solution)/shard_map/reduce_scatter | solution.py:1338
  126.3 18.6 %copy-start.25 = (bf16[768,1536]{1,0:T(8,128)(2,1)S(1)}, bf16[768,1536]{1,0:T(8,128)(2,1)}, u32[]{:S(2)}) copy-start(bf16[768,1536]{1,0:T(8,128)(2,1)} %get-tuple-element.79) | copy-start | bytes 7077892
  138.5 5.8 copy-start.49
  138.5 6.4 %copy-start.9 = (bf16[2048,768]{1,0:T(8,128)(2,1)S(1)}, bf16[2048,768]{1,0:T(8,128)(2,1)}, u32[]{:S(2)}) copy-start(bf16[2048,768]{1,0:T(8,128)(2,1)} %get-tuple-element.80) | copy-start | bytes 9437188
  140.5 8.4 %collective-permute-start = (bf16[512,768]{1,0:T(8,128)(2,1)S(1)}, bf16[512,768]{1,0:T(8,128)(2,1)S(1)}, u32[]{:S(2)}, u32[]{:S(2)}) collective-permute-start(bf16[512,768]{1,0:T(8,128)(2,1)S(1)} %get-tuple-element.176), channel_id=1, source_target_pairs={{0,4},{4,0},{1,5},{5,1},{2,6},{6,2},{3,7},{7,3},{8,12},{12,8},{9,1... | collective-permute-start | bytes 2359304 | tf_op jit(solution)/shard_map/ppermute | solution.py:1134
  144.9 4.0 copy-start.35
  164.3 2.4 collective-permute-start.1
  174.5 2.8 copy-start.32
  174.5 3.3 copy-start.36
  182.8 2.6 collective-permute-start.2
  296.4 49.8 %copy-start.3 = (f32[512,768]{1,0:T(8,128)S(1)}, f32[512,768]{1,0:T(8,128)}, u32[]{:S(2)}) copy-start(f32[512,768]{1,0:T(8,128)} %copy-done.2) | copy-start | bytes 4718596
  349.0 2.8 copy-start.62
  351.8 3.8 copy-start.33
  360.3 218.6 %reduce-scatter.5.cloned.1.call-start = ((), (), s32[]{:S(2)}) async-start(), calls=%async_computation.5 | async-start | bytes 3538944 | tf_op jit(solution)/shard_map/reduce_scatter | solution.py:1349
  360.8 2.8 copy-start.31
  368.0 4.1 collective-permute-start.3
  372.1 2.9 copy-start.18
  375.4 24.9 %copy-start.7 = (f32[512,768]{1,0:T(8,128)}, f32[512,768]{1,0:T(8,128)S(1)}, u32[]{:S(2)}) copy-start(f32[512,768]{1,0:T(8,128)S(1)} %subtract_add_fusion.1) | copy-start | bytes 4718596
  396.3 4.0 copy-start.28
  396.3 5.5 copy-start.26
  399.7 19.8 %collective-permute-start.4 = (bf16[512,768]{1,0:T(8,128)(2,1)}, bf16[512,768]{1,0:T(8,128)(2,1)}, u32[]{:S(2)}, u32[]{:S(2)}) collective-permute-start(bf16[512,768]{1,0:T(8,128)(2,1)} %get-tuple-element.186), channel_id=1, source_target_pairs={{0,4},{4,0},{1,5},{5,1},{2,6},{6,2},{3,7},{7,3},{8,12},{12,8},{9,1... | collective-permute-start | bytes 2359304 | tf_op jit(solution)/shard_map/ppermute | solution.py:1134
  414.8 4.7 copy-start.16
  453.8 4.9 copy-start.37
  456.5 3.6 copy-start.27
  460.1 3.0 copy-start.13
  566.5 14.4 %copy-start.1 = (bf16[8032,192]{0,1:T(8,128)(2,1)S(1)}, bf16[8032,192]{0,1:T(8,128)(2,1)}, u32[]{:S(2)}) copy-start(bf16[8032,192]{0,1:T(8,128)(2,1)} %param.41) | copy-start | bytes 9252868
  (40 other events, 68.8 us)
Sparse Core Ops, SparseCore 0:
  11.2 103.3 all-gather.2
  116.5 57.9 all-gather.4
  360.4 54.3 reduce-scatter.2
  417.0 73.9 reduce-scatter.4

commit v5 on v4

--- a/solution.py
+++ b/solution.py
@@ -424,18 +424,21 @@
 
 
 class BlockLine:
-    def __init__(self, pool, me, own, take):
+    def __init__(self, pool, me, own, take, pieces=2):
         self.pool, self.me, self.own, self.take = pool, me, own, take
-        self.first = pool.take(4)
+        self.pieces, self.sub = pieces, own.shape[0] // pieces
+        self.first = pool.take(4 * pieces)
         self.where = [(me.c + 1, 1 - me.c), (3 * me.c, me.c)]
 
-    def right(self, i):
-        here = self.take.at[self.where[i][1]]
-        return self.pool.copy(self.first + i, self.me.z[1], here, here)
-
-    def left(self, i):
-        here = self.take.at[self.where[i][1]]
-        return self.pool.copy(self.first + 2 + i, self.me.z[3], here, here)
+    def make(self, lane, i, piece, peer):
+        here = self.take.at[self.where[i][1], pl.ds(piece * self.sub, self.sub)]
+        return self.pool.copy(self.first + (2 * lane + i) * self.pieces + piece, peer, here, here)
+
+    def right(self, i, piece):
+        return self.make(0, i, piece, self.me.z[1])
+
+    def left(self, i, piece):
+        return self.make(1, i, piece, self.me.z[3])
 
     def begin(self):
         t = self.me.t
@@ -444,8 +447,9 @@
             @pl.when(t == block)
             def _():
                 self.take[slot] = self.own[...]
-                pl.when(t < 3)(lambda: self.right(i).start())
-                pl.when(t > 0)(lambda: self.left(i).start())
+                for p in range(self.pieces):
+                    pl.when(t < 3)(lambda: self.right(i, p).start())
+                    pl.when(t > 0)(lambda: self.left(i, p).start())
 
     def arrive(self, distance):
         t = self.me.t
@@ -453,19 +457,22 @@
 
             @pl.when(t - block == distance)
             def _():
-                self.right(i).wait_recv()
-                pl.when(t < 3)(lambda: self.right(i).start())
+                for p in range(self.pieces):
+                    self.right(i, p).wait_recv()
+                    pl.when(t < 3)(lambda: self.right(i, p).start())
 
             @pl.when(block - t == distance)
             def _():
-                self.left(i).wait_recv()
-                pl.when(t > 0)(lambda: self.left(i).start())
+                for p in range(self.pieces):
+                    self.left(i, p).wait_recv()
+                    pl.when(t > 0)(lambda: self.left(i, p).start())
 
     def finish(self):
         t = self.me.t
         for i, (block, slot) in enumerate(self.where):
-            pl.when((t >= block) & (t < 3))(lambda: self.right(i).wait_send())
-            pl.when((t <= block) & (t > 0))(lambda: self.left(i).wait_send())
+            for p in range(self.pieces):
+                pl.when((t >= block) & (t < 3))(lambda: self.right(i, p).wait_send())
+                pl.when((t <= block) & (t > 0))(lambda: self.left(i, p).wait_send())
 
 
 class SumLine:
@@ -546,14 +553,21 @@
 
 
 class GradLine:
-    def __init__(self, pool, me, own, coming, going, shared):
+    def __init__(self, pool, me, own, coming, going, shared, pieces=2):
         self.pool, self.me, self.own, self.coming, self.going, self.shared = pool, me, own, coming, going, shared
-        self.first = pool.take(5)
+        self.pieces, self.sub = pieces, own.shape[1] // pieces
+        self.first = pool.take(4 * pieces + 1)
         self.home = me.c == me.t // 2
 
-    def copy(self, slot, source):
+    def here(self, piece):
+        return pl.ds(piece * self.sub, self.sub)
+
+    def copy(self, slot, source, piece):
         peer = self.me.z[1] if slot < 2 else self.me.z[3]
-        return self.pool.copy(self.first + slot, peer, source, self.coming.at[slot])
+        here = self.here(piece)
+        return self.pool.copy(
+            self.first + slot * self.pieces + piece, peer, source.at[here], self.coming.at[slot, here]
+        )
 
     def index(self, slot):
         return (1, 0, 0, 1)[slot]
@@ -567,7 +581,8 @@
 
     def start(self):
         for slot in (0, 2, 1, 3):
-            pl.when(self.direct(slot))(lambda: self.copy(slot, self.own.at[self.index(slot)]).start())
+            for p in range(self.pieces):
+                pl.when(self.direct(slot))(lambda: self.copy(slot, self.own.at[self.index(slot)], p).start())
 
     passing = ((0, 1), (2, 2), (1, 1), (3, 2), (0, 2), (2, 1))
 
@@ -579,21 +594,24 @@
 
             @pl.when(self.adds(slot, chip))
             def _():
-                self.copy(slot, self.going.at[slot]).wait_recv()
-                self.going[slot] = (
-                    self.own[self.index(slot)].astype(F32) + self.coming[slot].astype(F32)
-                ).astype(BF)
-                self.copy(slot, self.going.at[slot]).start()
+                for p in range(self.pieces):
+                    here = self.here(p)
+                    self.copy(slot, self.going.at[slot], p).wait_recv()
+                    self.going[slot, here] = (
+                        self.own[self.index(slot), here].astype(F32) + self.coming[slot, here].astype(F32)
+                    ).astype(BF)
+                    self.copy(slot, self.going.at[slot], p).start()
 
     def share(self):
-        return self.pool.copy(self.first + 4, self.me.core, self.shared, self.shared)
+        return self.pool.copy(self.first + 4 * self.pieces, self.me.core, self.shared, self.shared)
 
     def settle(self, total):
         t = self.me.t
 
         for slot in range(4):
             ends = (t == self.block(slot)) & (t > 0 if slot < 2 else t < 3)
-            pl.when(ends)(lambda: self.copy(slot, self.going.at[slot]).wait_recv())
+            for p in range(self.pieces):
+                pl.when(ends)(lambda: self.copy(slot, self.going.at[slot], p).wait_recv())
 
         @pl.when(self.home)
         def _():
@@ -613,9 +631,11 @@
 
     def finish(self):
         for slot in range(4):
-            pl.when(self.direct(slot))(lambda: self.copy(slot, self.own.at[self.index(slot)]).wait_send())
+            for p in range(self.pieces):
+                pl.when(self.direct(slot))(lambda: self.copy(slot, self.own.at[self.index(slot)], p).wait_send())
         for slot, chip in self.passing:
-            pl.when(self.adds(slot, chip))(lambda: self.copy(slot, self.going.at[slot]).wait_send())
+            for p in range(self.pieces):
+                pl.when(self.adds(slot, chip))(lambda: self.copy(slot, self.going.at[slot], p).wait_send())
         pl.when(self.home)(lambda: self.share().wait_send())
         pl.when(jnp.logical_not(self.home))(lambda: self.share().wait_recv())
 
@@ -895,11 +915,11 @@
     rows = summed.shape[1]
     crossing = settle_first(send, me, dn_ref, other, 4 * rows)
     plane = Planar(send, me, de_ref, first, None, move_ref, chunks)
+    plane.begin()
     crossing.wait_recv()
     settle_second(me, dn_ref, other, summed, rows)
     line = SumLine(pool, me, summed, coming, going)
     line.start()
-    plane.begin()
     for part in range(3):
         line.add(part)
     line.result(total)
@@ -956,18 +976,14 @@
     send = Sender(pool)
     rows = summed.shape[1]
     crossing = settle_first(send, me, dn_ref, other, 4 * rows)
-    for i, piece in enumerate((c0, c1, c2, c3)):
-        g0[:, :, i * piece.shape[2] : (i + 1) * piece.shape[2]] = piece[...]
-    for i, piece in enumerate((s0, s1, s2, s3)):
-        g1[:, :, i * piece.shape[2] : (i + 1) * piece.shape[2]] = piece[...]
     planes = [
         Planar(send, me, g0, first0, second0, moving0, chunks),
         Planar(send, me, g1, first1, second1, moving1, chunks),
     ]
-    planes[0].begin()
-    planes[1].begin()
-    slots[me.c * 4 + me.t] = gains_ref[...]
-    gain_copies = [send.to(peer, gains_ref, slots.at[me.c * 4 + me.t]) for peer in me.group]
+
+    def collect(target, pieces):
+        for i, piece in enumerate(pieces):
+            target[:, :, i * piece.shape[2] : (i + 1) * piece.shape[2]] = piece[...]
 
     def split(value, cut):
         return [
@@ -975,20 +991,29 @@
             for i in range(2)
         ]
 
+    collect(g0, (c0, c1, c2, c3))
+    planes[0].begin()
     ff_line = GradLine(pool, me, ab2, in2, out2, held2)
     lines = [GradLine(pool, me, ab0, in0, out0, held0), GradLine(pool, me, ab1, in1, out1, held1)]
     for i, half in enumerate(split(f_ref[...], cuts[2])):
         ab2[i] = half
+    ff_line.start()
     crossing.wait_recv()
     settle_second(me, dn_ref, other, summed, rows)
     row_line = SumLine(pool, me, summed, coming, going)
-    ff_line.start()
     row_line.start()
-    for part in range(3):
-        ff_line.add(part)
-        row_line.add(part)
+    collect(g1, (s0, s1, s2, s3))
+    planes[1].begin()
+    slots[me.c * 4 + me.t] = gains_ref[...]
+    gain_copies = [send.to(peer, gains_ref, slots.at[me.c * 4 + me.t]) for peer in me.group]
+    ff_line.add(0)
+    row_line.add(0)
     planes[0].middle()
+    ff_line.add(1)
+    row_line.add(1)
     planes[1].middle()
+    ff_line.add(2)
+    row_line.add(2)
     e_copies = [
         send.to(me.y if along_x else me.x, em_ref.at[start:stop], e_second.at[start:stop])
         for start, stop, along_x in halves(eo_ref.shape[0], 1, 16)
@@ -1056,8 +1081,8 @@
         pltpu.VMEM((8,) + gains.shape, F32),
         pltpu.VMEM(gains.shape, F32),
         pltpu.VMEM((4,) + gains.shape, F32),
-        pltpu.SemaphoreType.DMA((64,)),
-        pltpu.SemaphoreType.DMA((64,)),
+        pltpu.SemaphoreType.DMA((80,)),
+        pltpu.SemaphoreType.DMA((80,)),
     ]
     return pl.pallas_call(
         partial(tail_kernel, cuts=cuts, chunks=chunks),
@@ -1378,7 +1403,7 @@
             [a.reshape(shards, depth // shards, a.shape[1]) for a in parts] for parts in (cross_parts, self_parts)
         ]
         gain1_part = jnp.sum(cut.astype(F32) * normed1.astype(F32), axis=0) / gain_one
-        gains_part = [gain1_part] + [jnp.sum(mine(a), axis=0) for a in (gain2_rows, gain3_rows, gain4_rows)]
+        gains_part = [gain1_part] + [0.5 * jnp.sum(a, axis=0) for a in (gain2_rows, gain3_rows, gain4_rows)]
         gain_pad = jnp.stack(gains_part + [jnp.zeros_like(gain1_part)] * 4)
         gn1, cross_own, self_own, ff_own, gain_sums, emb_sums = tail_scatter(
             cut, blocks, ff_mine, gain_pad, emb_own, emb_move, [cuts[1], cuts[0], cuts[2]]

time: 592 us -> 589 us (level)
  Pallas kernels: 421 us -> 413 us
  other arithmetic: 27 us -> 33.1 us
    unnamed x130 -> x118, local copies, waits for them, and re-layouts: 15 us -> 10.9 us
  transfers between devices with their start and end apart: 9 -> 9, of which waited for: 4 -> 5; matrix products, arithmetic and copies ran while one was open for 16% -> 16% of each run, Pallas kernels for 45% -> 45%
where the time goes in v5:
time: 589 us; the launch traced here: 583 us
  Pallas kernels  413 us (70%)
  matrix products  77.7 us (13%)
  other arithmetic  33.1 us (6%)
  local copies, waits for them, and re-layouts  23.4 us (4%)
  between operations  15.7 us (3%)
  waiting for transfers between devices  14.7 us (2%)
    pallas_call x1, Pallas kernels, start_gather(): pl.pallas_call(partial(start_kernel, cuts=cuts), in_specs=[vmem] * 8, out...  102 us
    pallas_call x1, Pallas kernels, tail_scatter(): pl.pallas_call(partial(tail_kernel, cuts=cuts, chunks=chunks), in_specs=[...  93.5 us
    pallas_call x1, Pallas kernels, middle_scatter(): pl.pallas_call(partial(middle_kernel, chunks=chunks), in_specs=[vmem] * 2...  46 us
    pallas_call x1, Pallas kernels, head_back(): pl.pallas_call(partial(head_back_kernel, vocab=vocab, block=block, rows=r...  35.2 us
    pallas_call x2, Pallas kernels, attend_back(): pl.pallas_call(partial(attend_back_kernel, tiles=tiles), grid=(pairs,), i...  34.4 us
    pallas_call x1, Pallas kernels, gather_rows(): pl.pallas_call(rows_kernel, in_specs=[pl.BlockSpec(memory_space=pltpu.VME...  31.9 us
    pallas_call x1, Pallas kernels, head_stats(): pl.pallas_call(partial(head_stats_kernel, vocab=vocab, block=block, rows=...  30.4 us
    dot_general x9, matrix products, matmul(): return jnp.dot(left, right, preferred_element_type=F32)  27.9 us
  transfers between devices with their start and end apart: 9, of which 5 were waited for; matrix products, arithmetic and copies ran while one was open for 16% of the time, Pallas kernels for 45%

profile of v5, /device:TPU:0, one launch (start us, length us, event | category | flops | bytes accessed | tf_op | source)
XLA Modules:
  0.0 582.8 jit_solution(4717377505007045138)
XLA Ops:
  14.7 101.6 %start_gather.1 = (f32[8,768]{1,0:T(8,128)}, bf16[2048,768]{1,0:T(8,128)(2,1)}, bf16[2048,768]{1,0:T(8,128)(2,1)}, bf16[512,768]{1,0:T(8,128)(2,1)}, bf16[512,76...) custom-call(f32[8,256]{1,0:T(8,128)} %fusion.62.gains_ref, ...), custom_call_target="tpu_custom_call" | custom-call | tf_op jit(solution)/shard_map/start_gather/pallas_call | solution.py:749
  121.1 5.2 convolution_convert_fusion.1.k_ref.v_ref
  126.3 12.2 %attend.2 = (bf16[512,384]{1,0:T(8,128)(2,1)}, f32[384,512]{1,0:T(8,128)}, f32[3,8,512]{2,1,0:T(8,128)}) custom-call(s32[1,512]{1,0:T(1,128)} %fusion.66.seen_ref, bf16[512,384]{1,0:T(8,128)(2,1)} %fusion.25.q_ref, bf16[2048,768]{1,0:T(8,128)(2,1)} %convolution_convert_fusion.1.k_ref.v_ref, bf16[2048,768]{1,0:T(8,128)(2,1)} %convolution_convert_fusion.1.k_ref.v_ref), custom_call_target="tpu_custom_call" | custom-call | flops 1610612736 | bytes 4718592 | tf_op jit(solution)/shard_map/attend/pallas_call | solution.py:54
  140.5 3.8 collective-permute-start
  144.9 4.0 convolution_convert_fusion.k_ref.v_ref
  151.3 12.0 %attend.3 = (bf16[512,384]{1,0:T(8,128)(2,1)}, f32[384,512]{1,0:T(8,128)}, f32[3,8,512]{2,1,0:T(8,128)}) custom-call(s32[1,512]{1,0:T(1,128)} %fusion.66.seen_ref, bf16[512,384]{1,0:T(8,128)(2,1)} %fusion.26.q_ref, bf16[2048,768]{1,0:T(8,128)(2,1)} %convolution_convert_fusion.k_ref.v_ref, bf16[2048,768]{1,0:T(8,128)(2,1)} %convolution_convert_fusion.k_ref.v_ref), custom_call_target="tpu_custom_call" | custom-call | flops 1610612736 | bytes 4718592 | tf_op jit(solution)/shard_map/attend/pallas_call | solution.py:54
  168.7 5.7 all-gather.5.cloned.1.call-done
  174.5 2.8 fusion.23
  185.5 3.1 multiply_reduce_fusion.5
  190.7 31.9 %gather_rows.1.n_ref = bf16[2048,768]{1,0:T(8,128)(2,1)} custom-call(bf16[256,768]{1,0:T(8,128)(2,1)} %multiply_convert_fusion.4.n_ref), custom_call_target="tpu_custom_call" | custom-call | tf_op jit(solution)/shard_map/gather_rows/pallas_call | solution.py:786
  222.6 30.4 %head_stats.1 = (f32[48,128]{1,0:T(8,128)}, bf16[4096,2048]{1,0:T(8,128)(2,1)}, f32[8,2048]{1,0:T(8,128)}) custom-call(bf16[768,4096]{1,0:T(8,128)(2,1)} %all-gather.3.cloned.1.call-done.emb_ref, bf16[2048,768]{1,0:T(8,128)(2,1)} %gather_rows.1.n_ref, s32[1,2048]{1,0:T(1,128)} %bitcast.86), custom_call_target="tpu_custom_call" | custom-call | flops 12633243648 | bytes 25763840 | tf_op jit(solution)/shard_map/head_stats/pallas_call | solution.py:209
  253.0 8.0 %combine_stats.1 = f32[2,16,128]{2,1,0:T(8,128)} custom-call(f32[48,128]{1,0:T(8,128)} %get-tuple-element.86.stats_ref), custom_call_target="tpu_custom_call" | custom-call | tf_op jit(solution)/shard_map/combine_stats/pallas_call | solution.py:822
  262.4 35.2 %head_back.1 = (bf16[768,4096]{1,0:T(8,128)(2,1)}, bf16[2048,768]{1,0:T(8,128)(2,1)}) custom-call(bf16[768,4096]{1,0:T(8,128)(2,1)} %all-gather.3.cloned.1.call-done.emb_ref, bf16[4096,2048]{1,0:T(8,128)(2,1)} %get-tuple-element.88.expo_ref, f32[8,2048]{1,0:T(8,128)} %get-tuple-element.89.tops_ref, bf16[2048,768]{1,0:T(8,128)(2,1)} %gather_rows.1.n_ref, ...), custom_call_target="tpu_custom_call" | custom-call | flops 25266487296 | bytes 38223872 | tf_op jit(solution)/shard_map/head_back/pallas_call | solution.py:266
  297.6 46.0 %middle_scatter.1 = (bf16[512,768]{1,0:T(8,128)(2,1)}, bf16[192,4096]{1,0:T(8,128)(2,1)}, bf16[192,4096]{1,0:T(8,128)(2,1)}) custom-call(bf16[2048,768]{1,0:T(8,128)(2,1)} %get-tuple-element.90.dn_ref, bf16[4,192,4096]{2,1,0:T(8,128)(2,1)} %bitcast.71), custom_call_target="tpu_custom_call" | custom-call | tf_op jit(solution)/shard_map/middle_scatter/pallas_call | solution.py:944
  350.8 3.8 multiply_convert_fusion
  359.8 2.8 fusion.21
  362.6 4.3 fusion.72
  374.1 2.8 convolution_convert_fusion.14.do_ref
  377.0 18.0 %attend_back.2 = (bf16[512,384]{1,0:T(8,128)(2,1)}, bf16[2048,384]{1,0:T(8,128)(2,1)}, bf16[2048,384]{1,0:T(8,128)(2,1)}) custom-call(s32[1,512]{1,0:T(1,128)} %fusion.66.seen_ref, bf16[512,384]{1,0:T(8,128)(2,1)} %fusion.26.q_ref, bf16[2048,768]{1,0:T(8,128)(2,1)} %convolution_convert_fusion.k_ref.v_ref, ...), custom_call_target="tpu_custom_call" | custom-call | flops 4026531840 | bytes 10616832 | tf_op jit(solution)/shard_map/attend_back/pallas_call | solution.py:132
  395.0 2.8 fusion.73
  401.4 2.7 convolution_convert_fusion.8
  404.0 3.5 add_convert_fusion
  409.6 4.5 reduce-scatter.3.cloned.1.call-done.f_ref
  414.1 5.0 convolution_convert_fusion.7
  421.5 3.1 subtract_add_fusion
  424.6 2.7 convolution_convert_fusion.13.do_ref
  427.3 16.4 %attend_back.3 = (bf16[512,384]{1,0:T(8,128)(2,1)}, bf16[2048,384]{1,0:T(8,128)(2,1)}, bf16[2048,384]{1,0:T(8,128)(2,1)}) custom-call(s32[1,512]{1,0:T(1,128)} %fusion.66.seen_ref, bf16[512,384]{1,0:T(8,128)(2,1)} %fusion.25.q_ref, bf16[2048,768]{1,0:T(8,128)(2,1)} %convolution_convert_fusion.1.k_ref.v_ref, ...), custom_call_target="tpu_custom_call" | custom-call | flops 4026531840 | bytes 10616832 | tf_op jit(solution)/shard_map/attend_back/pallas_call | solution.py:132
  459.8 3.0 convolution_convert_fusion.9
  462.8 2.7 convolution_convert_fusion.6
  465.5 2.6 convolution_convert_fusion.5
  468.1 93.5 %tail_scatter.1 = (f32[256,768]{1,0:T(8,128)}, bf16[192,768]{1,0:T(8,128)(2,1)}, bf16[192,768]{1,0:T(8,128)(2,1)}, bf16[192,1536]{1,0:T(8,128)(2,1)}, f32[8,768]{1,0:T(8,128)}, /*index=5*/bf16[2,192,4096]{2,1,0:T(8,128)(2,1)}) custom-call(bf16[2048,768]{1,0:T(8,128)(2,1)} %bitcast.70, bf16[4,192,384]{2,1,0:T(8,128)(2,1)} %bitcast.76, ...), custom_call_target="tpu_custom_call" | custom-call | tf_op jit(solution)/shard_map/tail_scatter/pallas_call | solution.py:1087
  561.7 7.5 %finish.1 = (f32[192,8032]{1,0:T(8,128)}, f32[256,768]{1,0:T(8,128)}, f32[192,192]{1,0:T(8,128)}, f32[192,192]{1,0:T(8,128)}, f32[192,192]{1,0:T(8,128)}, /*inde...) custom-call(bf16[2,192,4096]{2,1,0:T(8,128)(2,1)} %get-tuple-element, ...), custom_call_target="tpu_custom_call" | custom-call | tf_op jit(solution)/shard_map/finish/pallas_call | solution.py:1124
  (201 shorter events, 83.5 us)
Async XLA Ops:
  7.2 109.1 %all-gather.3.cloned.1.call-start = ((), (), s32[]{:S(2)}) async-start(), calls=%async_computation.2 | async-start | bytes 7864320 | tf_op jit(solution)/shard_map/all_gather | solution.py:1239
  11.0 2.8 copy-start.32
  11.0 2.8 copy-start.33
  11.1 2.8 copy-start.34
  11.1 163.4 %all-gather.5.cloned.1.call-start = ((), (), s32[]{:S(2)}) async-start(), calls=%async_computation.3 | async-start | bytes 5898240 | tf_op jit(solution)/shard_map/all_gather | solution.py:1258
  116.3 4.8 copy-start.2
  116.3 297.8 %reduce-scatter.3.cloned.1.call-start = ((), (), s32[]{:S(2)}) async-start(), calls=%async_computation.4 | async-start | bytes 5898240 | tf_op jit(solution)/shard_map/reduce_scatter | solution.py:1363
  126.3 18.6 %copy-start.18 = (bf16[768,1536]{1,0:T(8,128)(2,1)S(1)}, bf16[768,1536]{1,0:T(8,128)(2,1)}, u32[]{:S(2)}) copy-start(bf16[768,1536]{1,0:T(8,128)(2,1)} %get-tuple-element.79) | copy-start | bytes 7077892
  138.5 5.8 copy-start.43
  138.5 6.4 %copy-start.7 = (bf16[2048,768]{1,0:T(8,128)(2,1)S(1)}, bf16[2048,768]{1,0:T(8,128)(2,1)}, u32[]{:S(2)}) copy-start(bf16[2048,768]{1,0:T(8,128)(2,1)} %get-tuple-element.80) | copy-start | bytes 9437188
  140.5 8.4 %collective-permute-start = (bf16[512,768]{1,0:T(8,128)(2,1)S(1)}, bf16[512,768]{1,0:T(8,128)(2,1)S(1)}, u32[]{:S(2)}, u32[]{:S(2)}) collective-permute-start(bf16[512,768]{1,0:T(8,128)(2,1)S(1)} %get-tuple-element.178), channel_id=1, source_target_pairs={{0,4},{4,0},{1,5},{5,1},{2,6},{6,2},{3,7},{7,3},{8,12},{12,8},{9,1... | collective-permute-start | bytes 2359304 | tf_op jit(solution)/shard_map/ppermute | solution.py:1159
  144.9 4.0 copy-start.29
  164.9 2.4 collective-permute-start.1
  174.5 2.8 copy-start.26
  174.5 3.3 copy-start.30
  182.9 2.6 collective-permute-start.2
  348.0 2.8 copy-start.56
  350.8 3.8 copy-start.27
  359.3 214.8 %reduce-scatter.5.cloned.1.call-start = ((), (), s32[]{:S(2)}) async-start(), calls=%async_computation.5 | async-start | bytes 3538944 | tf_op jit(solution)/shard_map/reduce_scatter | solution.py:1374
  359.8 2.8 copy-start.25
  366.9 2.6 collective-permute-start.3
  369.6 2.9 copy-start.13
  374.1 24.0 %copy-start.4 = (f32[512,768]{1,0:T(8,128)}, f32[512,768]{1,0:T(8,128)S(1)}, u32[]{:S(2)}) copy-start(f32[512,768]{1,0:T(8,128)S(1)} %subtract_add_fusion.1) | copy-start | bytes 4718596
  394.9 3.1 copy-start.22
  395.0 4.5 copy-start.19
  397.8 21.4 %collective-permute-start.4 = (bf16[512,768]{1,0:T(8,128)(2,1)}, bf16[512,768]{1,0:T(8,128)(2,1)}, u32[]{:S(2)}, u32[]{:S(2)}) collective-permute-start(bf16[512,768]{1,0:T(8,128)(2,1)} %get-tuple-element.188), channel_id=1, source_target_pairs={{0,4},{4,0},{1,5},{5,1},{2,6},{6,2},{3,7},{7,3},{8,12},{12,8},{9,1... | collective-permute-start | bytes 2359304 | tf_op jit(solution)/shard_map/ppermute | solution.py:1159
  404.0 4.1 copy-start.23
  421.5 3.1 copy-start.17
  453.5 4.9 copy-start.31
  456.3 3.6 copy-start.21
  459.8 3.0 copy-start.10
  561.7 14.4 %copy-start.1 = (bf16[8032,192]{0,1:T(8,128)(2,1)S(1)}, bf16[8032,192]{0,1:T(8,128)(2,1)}, u32[]{:S(2)}) copy-start(bf16[8032,192]{0,1:T(8,128)(2,1)} %param.41) | copy-start | bytes 9252868
  (34 other events, 62.7 us)
Sparse Core Ops, SparseCore 0:
  11.2 103.3 all-gather.2
  116.5 57.9 all-gather.4
  359.4 54.6 reduce-scatter.2
  416.3 73.7 reduce-scatter.4

commit v6 on v5

--- a/solution.py
+++ b/solution.py
@@ -8,6 +8,7 @@
 from jax.sharding import PartitionSpec as P
 
 HEAD_DIM = 64
+LN2 = 0.6931471805599453
 EPS = 1e-06
 MASKED = -1e30
 BF = jnp.bfloat16
@@ -183,23 +184,24 @@
 
     for first in range(0, total, rows):
         columns = slice(first, first + rows)
-        logits = jnp.dot(emb, nt_ref[:, columns], preferred_element_type=F32) * scale
+        logits = jnp.dot(emb, nt_ref[:, columns], preferred_element_type=F32) * (scale / LN2)
         logits = jnp.where(valid, logits, MASKED)
         top = run_ref[0:1, columns]
         new_top = jnp.maximum(top, jnp.max(logits, axis=0, keepdims=True))
-        expo = jnp.exp(logits - new_top)
+        expo = jnp.exp2(logits - new_top)
         expo_ref[:, columns] = expo.astype(BF)
         run_ref[0:1, columns] = new_top
-        run_ref[1:2, columns] = run_ref[1:2, columns] * jnp.exp(top - new_top) + jnp.sum(expo, axis=0, keepdims=True)
+        run_ref[1:2, columns] = run_ref[1:2, columns] * jnp.exp2(top - new_top) + jnp.sum(expo, axis=0, keepdims=True)
         run_ref[2:3, columns] += jnp.sum(jnp.where(ids == target_ref[:, columns], logits, 0.0), axis=0, keepdims=True)
-    tops_ref[pl.ds(step, 1), :] = run_ref[0:1, :]
+    tops_ref[pl.ds(step, 1), :] = run_ref[0:1, :] * LN2
 
     @pl.when(step == pl.num_programs(0) - 1)
     def _():
         lines = total // 128
         for k in range(3):
             for i in range(lines):
-                stats_ref[k * lines + i : k * lines + i + 1, :] = run_ref[k : k + 1, i * 128 : (i + 1) * 128]
+                part = run_ref[k : k + 1, i * 128 : (i + 1) * 128]
+                stats_ref[k * lines + i : k * lines + i + 1, :] = part if k == 1 else part * LN2
 
 
 def head_stats(emb_t, normed, target, vocab, block, rows):

time: 589 us -> 589 us (level)
  no operation moved by 1% of the time
where the time goes in v6:
time: 589 us; the launch traced here: 583 us
  Pallas kernels  413 us (70%)
  matrix products  77.7 us (13%)
  other arithmetic  33.1 us (6%)
  local copies, waits for them, and re-layouts  23.4 us (4%)
  between operations  15.7 us (3%)
  waiting for transfers between devices  14.7 us (2%)
    pallas_call x1, Pallas kernels, start_gather(): pl.pallas_call(partial(start_kernel, cuts=cuts), in_specs=[vmem] * 8, out...  102 us
    pallas_call x1, Pallas kernels, tail_scatter(): pl.pallas_call(partial(tail_kernel, cuts=cuts, chunks=chunks), in_specs=[...  93.5 us
    pallas_call x1, Pallas kernels, middle_scatter(): pl.pallas_call(partial(middle_kernel, chunks=chunks), in_specs=[vmem] * 2...  46 us
    pallas_call x1, Pallas kernels, head_back(): pl.pallas_call(partial(head_back_kernel, vocab=vocab, block=block, rows=r...  35.2 us
    pallas_call x2, Pallas kernels, attend_back(): pl.pallas_call(partial(attend_back_kernel, tiles=tiles), grid=(pairs,), i...  34.4 us
    pallas_call x1, Pallas kernels, gather_rows(): pl.pallas_call(rows_kernel, in_specs=[pl.BlockSpec(memory_space=pltpu.VME...  31.9 us
    pallas_call x1, Pallas kernels, head_stats(): pl.pallas_call(partial(head_stats_kernel, vocab=vocab, block=block, rows=...  30.4 us
    dot_general x9, matrix products, matmul(): return jnp.dot(left, right, preferred_element_type=F32)  27.9 us
  transfers between devices with their start and end apart: 9, of which 5 were waited for; matrix products, arithmetic and copies ran while one was open for 16% of the time, Pallas kernels for 45%

profile of v6, /device:TPU:0, one launch (start us, length us, event | category | flops | bytes accessed | tf_op | source)
XLA Modules:
  0.0 582.8 jit_solution(10141558451069294280)
XLA Ops:
  14.7 101.6 %start_gather.1 = (f32[8,768]{1,0:T(8,128)}, bf16[2048,768]{1,0:T(8,128)(2,1)}, bf16[2048,768]{1,0:T(8,128)(2,1)}, bf16[512,768]{1,0:T(8,128)(2,1)}, bf16[512,76...) custom-call(f32[8,256]{1,0:T(8,128)} %fusion.62.gains_ref, ...), custom_call_target="tpu_custom_call" | custom-call | tf_op jit(solution)/shard_map/start_gather/pallas_call | solution.py:751
  121.1 5.2 convolution_convert_fusion.1.k_ref.v_ref
  126.3 12.2 %attend.2 = (bf16[512,384]{1,0:T(8,128)(2,1)}, f32[384,512]{1,0:T(8,128)}, f32[3,8,512]{2,1,0:T(8,128)}) custom-call(s32[1,512]{1,0:T(1,128)} %fusion.66.seen_ref, bf16[512,384]{1,0:T(8,128)(2,1)} %fusion.25.q_ref, bf16[2048,768]{1,0:T(8,128)(2,1)} %convolution_convert_fusion.1.k_ref.v_ref, bf16[2048,768]{1,0:T(8,128)(2,1)} %convolution_convert_fusion.1.k_ref.v_ref), custom_call_target="tpu_custom_call" | custom-call | flops 1610612736 | bytes 4718592 | tf_op jit(solution)/shard_map/attend/pallas_call | solution.py:55
  140.5 3.8 collective-permute-start
  144.9 4.0 convolution_convert_fusion.k_ref.v_ref
  151.3 12.0 %attend.3 = (bf16[512,384]{1,0:T(8,128)(2,1)}, f32[384,512]{1,0:T(8,128)}, f32[3,8,512]{2,1,0:T(8,128)}) custom-call(s32[1,512]{1,0:T(1,128)} %fusion.66.seen_ref, bf16[512,384]{1,0:T(8,128)(2,1)} %fusion.26.q_ref, bf16[2048,768]{1,0:T(8,128)(2,1)} %convolution_convert_fusion.k_ref.v_ref, bf16[2048,768]{1,0:T(8,128)(2,1)} %convolution_convert_fusion.k_ref.v_ref), custom_call_target="tpu_custom_call" | custom-call | flops 1610612736 | bytes 4718592 | tf_op jit(solution)/shard_map/attend/pallas_call | solution.py:55
  168.7 5.7 all-gather.5.cloned.1.call-done
  174.5 2.8 fusion.23
  185.5 3.1 multiply_reduce_fusion.5
  190.7 31.9 %gather_rows.1.n_ref = bf16[2048,768]{1,0:T(8,128)(2,1)} custom-call(bf16[256,768]{1,0:T(8,128)(2,1)} %multiply_convert_fusion.4.n_ref), custom_call_target="tpu_custom_call" | custom-call | tf_op jit(solution)/shard_map/gather_rows/pallas_call | solution.py:788
  222.6 30.4 %head_stats.1 = (f32[48,128]{1,0:T(8,128)}, bf16[4096,2048]{1,0:T(8,128)(2,1)}, f32[8,2048]{1,0:T(8,128)}) custom-call(bf16[768,4096]{1,0:T(8,128)(2,1)} %all-gather.3.cloned.1.call-done.emb_ref, bf16[2048,768]{1,0:T(8,128)(2,1)} %gather_rows.1.n_ref, s32[1,2048]{1,0:T(1,128)} %bitcast.86), custom_call_target="tpu_custom_call" | custom-call | flops 12633243648 | bytes 25763840 | tf_op jit(solution)/shard_map/head_stats/pallas_call | solution.py:211
  253.0 8.0 %combine_stats.1 = f32[2,16,128]{2,1,0:T(8,128)} custom-call(f32[48,128]{1,0:T(8,128)} %get-tuple-element.86.stats_ref), custom_call_target="tpu_custom_call" | custom-call | tf_op jit(solution)/shard_map/combine_stats/pallas_call | solution.py:824
  262.3 35.2 %head_back.1 = (bf16[768,4096]{1,0:T(8,128)(2,1)}, bf16[2048,768]{1,0:T(8,128)(2,1)}) custom-call(bf16[768,4096]{1,0:T(8,128)(2,1)} %all-gather.3.cloned.1.call-done.emb_ref, bf16[4096,2048]{1,0:T(8,128)(2,1)} %get-tuple-element.88.expo_ref, f32[8,2048]{1,0:T(8,128)} %get-tuple-element.89.tops_ref, bf16[2048,768]{1,0:T(8,128)(2,1)} %gather_rows.1.n_ref, ...), custom_call_target="tpu_custom_call" | custom-call | flops 25266487296 | bytes 38223872 | tf_op jit(solution)/shard_map/head_back/pallas_call | solution.py:268
  297.5 46.0 %middle_scatter.1 = (bf16[512,768]{1,0:T(8,128)(2,1)}, bf16[192,4096]{1,0:T(8,128)(2,1)}, bf16[192,4096]{1,0:T(8,128)(2,1)}) custom-call(bf16[2048,768]{1,0:T(8,128)(2,1)} %get-tuple-element.90.dn_ref, bf16[4,192,4096]{2,1,0:T(8,128)(2,1)} %bitcast.71), custom_call_target="tpu_custom_call" | custom-call | tf_op jit(solution)/shard_map/middle_scatter/pallas_call | solution.py:946
  350.7 3.8 multiply_convert_fusion
  359.8 2.8 fusion.21
  362.6 4.3 fusion.72
  374.1 2.8 convolution_convert_fusion.14.do_ref
  376.9 18.0 %attend_back.2 = (bf16[512,384]{1,0:T(8,128)(2,1)}, bf16[2048,384]{1,0:T(8,128)(2,1)}, bf16[2048,384]{1,0:T(8,128)(2,1)}) custom-call(s32[1,512]{1,0:T(1,128)} %fusion.66.seen_ref, bf16[512,384]{1,0:T(8,128)(2,1)} %fusion.26.q_ref, bf16[2048,768]{1,0:T(8,128)(2,1)} %convolution_convert_fusion.k_ref.v_ref, ...), custom_call_target="tpu_custom_call" | custom-call | flops 4026531840 | bytes 10616832 | tf_op jit(solution)/shard_map/attend_back/pallas_call | solution.py:133
  394.9 2.8 fusion.73
  401.3 2.6 convolution_convert_fusion.8
  404.0 3.5 add_convert_fusion
  409.6 4.5 reduce-scatter.3.cloned.1.call-done.f_ref
  414.1 5.0 convolution_convert_fusion.7
  421.5 3.1 subtract_add_fusion
  424.6 2.7 convolution_convert_fusion.13.do_ref
  427.3 16.4 %attend_back.3 = (bf16[512,384]{1,0:T(8,128)(2,1)}, bf16[2048,384]{1,0:T(8,128)(2,1)}, bf16[2048,384]{1,0:T(8,128)(2,1)}) custom-call(s32[1,512]{1,0:T(1,128)} %fusion.66.seen_ref, bf16[512,384]{1,0:T(8,128)(2,1)} %fusion.25.q_ref, bf16[2048,768]{1,0:T(8,128)(2,1)} %convolution_convert_fusion.1.k_ref.v_ref, ...), custom_call_target="tpu_custom_call" | custom-call | flops 4026531840 | bytes 10616832 | tf_op jit(solution)/shard_map/attend_back/pallas_call | solution.py:133
  459.8 3.0 convolution_convert_fusion.9
  462.8 2.7 convolution_convert_fusion.6
  465.4 2.6 convolution_convert_fusion.5
  468.1 93.5 %tail_scatter.1 = (f32[256,768]{1,0:T(8,128)}, bf16[192,768]{1,0:T(8,128)(2,1)}, bf16[192,768]{1,0:T(8,128)(2,1)}, bf16[192,1536]{1,0:T(8,128)(2,1)}, f32[8,768]{1,0:T(8,128)}, /*index=5*/bf16[2,192,4096]{2,1,0:T(8,128)(2,1)}) custom-call(bf16[2048,768]{1,0:T(8,128)(2,1)} %bitcast.70, bf16[4,192,384]{2,1,0:T(8,128)(2,1)} %bitcast.76, ...), custom_call_target="tpu_custom_call" | custom-call | tf_op jit(solution)/shard_map/tail_scatter/pallas_call | solution.py:1089
  561.6 7.5 %finish.1 = (f32[192,8032]{1,0:T(8,128)}, f32[256,768]{1,0:T(8,128)}, f32[192,192]{1,0:T(8,128)}, f32[192,192]{1,0:T(8,128)}, f32[192,192]{1,0:T(8,128)}, /*inde...) custom-call(bf16[2,192,4096]{2,1,0:T(8,128)(2,1)} %get-tuple-element, ...), custom_call_target="tpu_custom_call" | custom-call | tf_op jit(solution)/shard_map/finish/pallas_call | solution.py:1126
  (201 shorter events, 83.5 us)
Async XLA Ops:
  7.2 109.1 %all-gather.3.cloned.1.call-start = ((), (), s32[]{:S(2)}) async-start(), calls=%async_computation.2 | async-start | bytes 7864320 | tf_op jit(solution)/shard_map/all_gather | solution.py:1241
  11.0 2.8 copy-start.32
  11.0 2.8 copy-start.33
  11.1 2.8 copy-start.34
  11.1 163.4 %all-gather.5.cloned.1.call-start = ((), (), s32[]{:S(2)}) async-start(), calls=%async_computation.3 | async-start | bytes 5898240 | tf_op jit(solution)/shard_map/all_gather | solution.py:1260
  116.3 4.8 copy-start.2
  116.3 297.7 %reduce-scatter.3.cloned.1.call-start = ((), (), s32[]{:S(2)}) async-start(), calls=%async_computation.4 | async-start | bytes 5898240 | tf_op jit(solution)/shard_map/reduce_scatter | solution.py:1365
  126.3 18.6 %copy-start.18 = (bf16[768,1536]{1,0:T(8,128)(2,1)S(1)}, bf16[768,1536]{1,0:T(8,128)(2,1)}, u32[]{:S(2)}) copy-start(bf16[768,1536]{1,0:T(8,128)(2,1)} %get-tuple-element.79) | copy-start | bytes 7077892
  138.5 5.8 copy-start.43
  138.5 6.4 %copy-start.7 = (bf16[2048,768]{1,0:T(8,128)(2,1)S(1)}, bf16[2048,768]{1,0:T(8,128)(2,1)}, u32[]{:S(2)}) copy-start(bf16[2048,768]{1,0:T(8,128)(2,1)} %get-tuple-element.80) | copy-start | bytes 9437188
  140.5 8.4 %collective-permute-start = (bf16[512,768]{1,0:T(8,128)(2,1)S(1)}, bf16[512,768]{1,0:T(8,128)(2,1)S(1)}, u32[]{:S(2)}, u32[]{:S(2)}) collective-permute-start(bf16[512,768]{1,0:T(8,128)(2,1)S(1)} %get-tuple-element.178), channel_id=1, source_target_pairs={{0,4},{4,0},{1,5},{5,1},{2,6},{6,2},{3,7},{7,3},{8,12},{12,8},{9,1... | collective-permute-start | bytes 2359304 | tf_op jit(solution)/shard_map/ppermute | solution.py:1161
  144.9 4.0 copy-start.29
  164.9 2.4 collective-permute-start.1
  174.5 2.8 copy-start.26
  174.5 3.3 copy-start.30
  182.9 2.6 collective-permute-start.2
  348.0 2.8 copy-start.56
  350.7 3.8 copy-start.27
  359.2 214.9 %reduce-scatter.5.cloned.1.call-start = ((), (), s32[]{:S(2)}) async-start(), calls=%async_computation.5 | async-start | bytes 3538944 | tf_op jit(solution)/shard_map/reduce_scatter | solution.py:1376
  359.8 2.8 copy-start.25
  366.9 2.6 collective-permute-start.3
  369.5 2.9 copy-start.13
  374.1 24.0 %copy-start.4 = (f32[512,768]{1,0:T(8,128)}, f32[512,768]{1,0:T(8,128)S(1)}, u32[]{:S(2)}) copy-start(f32[512,768]{1,0:T(8,128)S(1)} %subtract_add_fusion.1) | copy-start | bytes 4718596
  394.9 3.1 copy-start.22
  394.9 4.5 copy-start.19
  397.7 21.4 %collective-permute-start.4 = (bf16[512,768]{1,0:T(8,128)(2,1)}, bf16[512,768]{1,0:T(8,128)(2,1)}, u32[]{:S(2)}, u32[]{:S(2)}) collective-permute-start(bf16[512,768]{1,0:T(8,128)(2,1)} %get-tuple-element.188), channel_id=1, source_target_pairs={{0,4},{4,0},{1,5},{5,1},{2,6},{6,2},{3,7},{7,3},{8,12},{12,8},{9,1... | collective-permute-start | bytes 2359304 | tf_op jit(solution)/shard_map/ppermute | solution.py:1161
  404.0 4.1 copy-start.23
  421.5 3.1 copy-start.17
  453.5 4.9 copy-start.31
  456.2 3.6 copy-start.21
  459.8 3.0 copy-start.10
  561.6 14.4 %copy-start.1 = (bf16[8032,192]{0,1:T(8,128)(2,1)S(1)}, bf16[8032,192]{0,1:T(8,128)(2,1)}, u32[]{:S(2)}) copy-start(bf16[8032,192]{0,1:T(8,128)(2,1)} %param.41) | copy-start | bytes 9252868
  (34 other events, 62.7 us)
Sparse Core Ops, SparseCore 0:
  11.2 103.3 all-gather.2
  116.5 57.9 all-gather.4
  359.4 54.6 reduce-scatter.2
  416.2 73.7 reduce-scatter.4
